TPU v7x, 512 devices: a whole 4x4x16 slice. The times are simulated.
512 devices in a mesh: blk: 16 (over z), pen: 32 (over x, y, core).
Axes of the slice: x: 4, y: 4, z: 16, core: 2. Of those that a mesh axis runs over, the one named last changes fastest.
Arguments:
- state: bfloat16 [16, 2, 32, 512, 512], P('blk', None, None, 'pen'), may hold values from -6 to 6
- inverse_x: bfloat16 [16, 2, 512, 512], P('blk')
- inverse_y: bfloat16 [16, 2, 512, 512], P('blk')
- rates: float32 [16, 3], P('blk'), may hold values from 0.05 to 0.4
- partner: int32 [16, 2], P('blk'), may hold values from 0 to 15
- face_side: int32 [16, 2], P('blk'), may hold values from 0 to 1
- orient: int32 [16, 2], P('blk'), may hold values from 0 to 1
- offset: int32 [16, 2], P('blk'), may hold values from 0 to 31
Outputs:
- relaxed: bfloat16 [16, 2, 32, 512, 512], P('blk', None, None, 'pen')
All inputs are finite; a program needn't handle non-finite values.
Results may differ from a plain program's by a relative error of at most 0.0058.
Values may be sent and summed in bfloat16 or wider, within the bound.
No kernel may reach another device: no remote copies, remote signals or barrier semaphores. Data moves between devices by JAX's collectives and lax.ppermute only.
A program may use at most 64 MiB of HBM per device.

v0:
```python
import jax
import jax.numpy as jnp
from jax import lax
from jax.sharding import PartitionSpec as P

STEPS = 2


def plane_ghosts(layers, partner_row, side_row, orient_row, offset_row, tile_rows):
    blocks = lax.all_gather(layers[None], "blk", axis=0, tiled=True)
    lines = layers.shape[-1]
    rows_y = jnp.arange(lines, dtype=jnp.int32)
    result = []
    for which in range(2):
        piece = lax.dynamic_index_in_dim(blocks, partner_row[which], 0, keepdims=False)
        segment = lax.dynamic_index_in_dim(piece, side_row[which], 0, keepdims=False)
        mirrored = jnp.where(orient_row[which] == 1, lines - 1 - rows_y, rows_y)
        take_at = (mirrored + offset_row[which] * tile_rows) % lines
        result.append(jnp.take(segment, take_at, axis=-1))
    return result


def local(state, inverse_x, inverse_y, rates, partner, face_side, orient, offset):
    magnet = state[0]
    inv_x = inverse_x[0]
    inv_y = inverse_y[0]
    rate_row = rates[0]
    first_col = inv_x[:, :, 0].astype(jnp.float32)
    last_col = inv_x[:, :, -1].astype(jnp.float32)
    tile_rows = magnet.shape[2]
    planes = lax.all_to_all(magnet, "pen", split_axis=1, concat_axis=2, tiled=True)
    for repeat in range(STEPS):
        layers = jnp.stack([planes[..., 0], planes[..., -1]], axis=0)
        ghosts = plane_ghosts(layers, partner[0], face_side[0], orient[0], offset[0], tile_rows)
        interior = jnp.einsum("fax,fzyx->fzya", inv_x, planes, preferred_element_type=jnp.float32)
        edges = first_col[:, None, None, :] * ghosts[0].astype(jnp.float32)[..., None]
        edges = edges + last_col[:, None, None, :] * ghosts[1].astype(jnp.float32)[..., None]
        swept_x = (interior + edges).astype(jnp.bfloat16)
        swept_y = jnp.einsum("fcy,fzyx->fzcx", inv_y, swept_x, preferred_element_type=jnp.float32)
        proton = swept_y[0]
        carbon = swept_y[1]
        new_proton = proton - (rate_row[0] * proton + rate_row[2] * carbon)
        new_carbon = carbon - (rate_row[1] * carbon + rate_row[2] * proton)
        planes = jnp.stack([new_proton, new_carbon]).astype(jnp.bfloat16)
    magnet = lax.all_to_all(planes, "pen", split_axis=2, concat_axis=1, tiled=True)
    return magnet[None]


def solution(mesh):
    return jax.shard_map(
        local,
        mesh=mesh,
        in_specs=(
            P("blk", None, None, "pen", None),
            P("blk", None, None, None),
            P("blk", None, None, None),
            P("blk", None),
            P("blk", None),
            P("blk", None),
            P("blk", None),
            P("blk", None),
        ),
        out_specs=P("blk", None, None, "pen", None),
        check_vma=False,
    )
```

profile of v0, /device:TPU:1, one launch (start us, length us, event | category | flops | bytes accessed | tf_op | source)
XLA Modules:
  0.0 137.5 jit_solution(13616519110712983959)
XLA Ops:
  0.1 2.4 %copy.81 = bf16[1,2,32,16,512]{4,3,1,2,0:T(8,128)(2,1)} copy(bf16[1,2,32,16,512]{4,3,2,1,0:T(8,128)(2,1)} %param.10) | data formatting | bytes 2097152 | tf_op args[0]
  2.5 10.5 %all-to-all-start = ((bf16[2,32,16,512]{3,2,0,1:T(8,128)(2,1)}), bf16[2,32,16,512]{3,2,0,1:T(8,128)(2,1)S(1)}, u32[]{:S(2)}, u32[]{:S(2)}) async-start(bf16[2,32,16,512]{3,2,0,1:T(8,128)(2,1)} %bitcast.95), calls=%async_computation | async-start | bytes 2097152 | tf_op jit(solution)/shard_map/all_to_all | solution.py:31
  13.0 0.6 fusion.19
  16.1 0.6 fusion.18
  21.5 0.6 fusion.16
  23.4 0.7 fusion.17
  25.5 0.7 fusion.15
  26.2 0.3 convert_reduce_fusion.1
  26.5 3.5 %all-to-all-done = bf16[2,32,16,512]{3,2,0,1:T(8,128)(2,1)S(1)} async-done(((bf16[2,32,16,512]{3,2,0,1:T(8,128)(2,1)}), bf16[2,32,16,512]{3,2,0,1:T(8,128)(2,1)S(1)}, u32[]{:S(2)}, u32[]{:S(2)}) %all-to-all-start) | async-done | bytes 1048608 | tf_op jit(solution)/shard_map/all_to_all | solution.py:31
  30.0 0.3 slice_reduce_fusion.1
  30.4 26.5 %all-gather = bf16[32,2,1,512]{3,1,2,0:T(2,128)(2,1)S(1)} all-gather(bf16[2,2,1,512]{3,1,2,0:T(2,128)(2,1)S(1)} %pad_maximum_fusion.3), channel_id=2, replica_groups=mesh['blk'=16,'pen'=32] {'blk'}, dimensions={0}, use_global_device_ids=true | all-gather | bytes 69632 | tf_op jit(solution)/shard_map/all_gather | solution.py:10
  56.9 0.2 copy.74
  57.1 1.3 gather_fusion
  58.5 0.1 bitcast_convert_fusion.3
  58.6 0.1 copy.57
  58.7 0.2 copy.75
  58.9 1.3 gather_fusion.1
  60.3 0.1 bitcast_convert_fusion.2
  60.5 4.0 %convolution_bitcast_fusion.1 = f32[2,1,512,512]{2,3,0,1:T(8,128)} fusion(bf16[1,2,512,512]{3,2,1,0:T(8,128)(2,1)S(1)} %copy-done, bf16[2,512,512]{2,1,0:T(8,128)(2,1)S(1)} %bitcast.97, f32[2,512]{1,0:T(2,128)S(1)} %copy.59, f32[2,512]{1,0:T(2,128)S(1)} %get-tuple-element.7, f32[2,512]{1,0:T(2,128)S(1)} %copy.57, f32[2,512]{1,0:T(2,128)S(1)} %get-tuple-element.6, ...), kind=kOutput, calls=%fused_computation.7 | convolution fusion | flops 1076363264 | bytes 5259264 | tf_op jit(solution)/shard_map/fcy,fzyx->fzcx/dot_general | solution.py:39
  64.5 3.8 %subtract_convert_fusion.3 = (bf16[1,1,512,512]{2,3,0,1:T(8,128)(2,1)S(1)}, bf16[1,1,512,512]{2,3,0,1:T(8,128)(2,1)S(1)}) fusion(f32[2,1,512,512]{2,3,0,1:T(8,128)} %convolution_bitcast_fusion.1, f32[]{:T(128)} %bitcast.27, f32[]{:T(128)} %bitcast.26, f32[]{:T(128)} %bitcast.30), kind=kLoop, calls=%fused_computation.18 | loop fusion | flops 2621440 | bytes 3145740 | tf_op jit(solution)/shard_map/convert.13
  68.3 19.7 %all-gather.1 = bf16[32,2,1,512]{3,1,2,0:T(2,128)(2,1)S(1)} all-gather(bf16[2,2,1,512]{3,1,2,0:T(2,128)(2,1)S(1)} %pad_maximum_fusion.4), channel_id=3, replica_groups=mesh['blk'=16,'pen'=32] {'blk'}, dimensions={0}, use_global_device_ids=true | all-gather | bytes 69632 | tf_op jit(solution)/shard_map/all_gather | solution.py:10
  88.1 0.2 copy.76
  88.3 1.3 gather_fusion.2
  89.6 0.7 bitcast_convert_fusion.1
  90.5 0.2 copy.77
  90.7 1.3 gather_fusion.3
  92.0 0.7 bitcast_convert_fusion
  92.9 3.9 %convolution_bitcast_fusion = f32[2,1,512,512]{2,3,0,1:T(8,128)} fusion(bf16[1,2,512,512]{3,2,1,0:T(8,128)(2,1)S(1)} %copy-done, bf16[1,512,512]{1,2,0:T(8,128)(2,1)S(1)} %bitcast.99, bf16[1,512,512]{1,2,0:T(8,128)(2,1)S(1)} %bitcast.98, f32[2,512]{1,0:T(2,128)S(1)} %copy.65, f32[2,512]{1,0:T(2,128)S(1)} %copy.63, f32[2,512]{1,0:T(2,128)} %copy-done.4, ...), kind=kOutput, calls=%fused_computation.6 | convolution fusion | flops 1076887552 | bytes 5259264 | tf_op jit(solution)/shard_map/fcy,fzyx->fzcx/dot_general | solution.py:39
  96.8 3.8 %subtract_convert_fusion.1 = (bf16[1,1,512,512]{2,3,0,1:T(8,128)(2,1)S(1)}, bf16[1,1,512,512]{2,3,0,1:T(8,128)(2,1)S(1)}) fusion(f32[2,1,512,512]{2,3,0,1:T(8,128)} %convolution_bitcast_fusion, f32[]{:T(128)} %bitcast.27, f32[]{:T(128)} %bitcast.26, f32[]{:T(128)} %bitcast.30), kind=kLoop, calls=%fused_computation.16 | loop fusion | flops 2621440 | bytes 3145740 | tf_op jit(solution)/shard_map/convert.6
  100.7 1.0 copy.67
  101.7 34.6 %all_to_all.21 = bf16[2,1,512,512]{3,0,1,2:T(2,128)(2,1)S(1)} all-to-all(bf16[2,1,512,512]{3,0,1,2:T(2,128)(2,1)S(1)} %copy.67), channel_id=1, replica_groups=mesh['blk'=16,'pen'=32] {'pen'}, dimensions={2} | all-to-all | bytes 2097152 | tf_op jit(solution)/shard_map/all_to_all | solution.py:45
  136.3 1.1 copy.68
  (39 shorter events, 0.7 us)
Async XLA Ops:
  0.0 60.5 %copy-start = (bf16[1,2,512,512]{3,2,1,0:T(8,128)(2,1)S(1)}, bf16[1,2,512,512]{3,2,1,0:T(8,128)(2,1)}, u32[]{:S(2)}) copy-start(bf16[1,2,512,512]{3,2,1,0:T(8,128)(2,1)} %param.12) | copy-start | bytes 3145732
  0.0 12.9 %copy-start.7 = (s32[1,2]{1,0:T(1,128)S(1)}, s32[1,2]{1,0:T(1,128)}, u32[]{:S(2)}) copy-start(s32[1,2]{1,0:T(1,128)} %param.14) | copy-start | bytes 28
  0.0 16.1 %copy-start.8 = (s32[1,2]{1,0:T(1,128)S(1)}, s32[1,2]{1,0:T(1,128)}, u32[]{:S(2)}) copy-start(s32[1,2]{1,0:T(1,128)} %param.15) | copy-start | bytes 28
  0.0 21.5 %copy-start.9 = (s32[1,2]{1,0:T(1,128)S(1)}, s32[1,2]{1,0:T(1,128)}, u32[]{:S(2)}) copy-start(s32[1,2]{1,0:T(1,128)} %param.16) | copy-start | bytes 28
  0.0 23.3 %copy-start.10 = (s32[1,2]{1,0:T(1,128)S(1)}, s32[1,2]{1,0:T(1,128)}, u32[]{:S(2)}) copy-start(s32[1,2]{1,0:T(1,128)} %param.17) | copy-start | bytes 28
  0.0 25.5 %copy-start.3 = (f32[1,3]{1,0:T(1,128)S(1)}, f32[1,3]{1,0:T(1,128)}, u32[]{:S(2)}) copy-start(f32[1,3]{1,0:T(1,128)} %param.13) | copy-start | bytes 40
  0.0 26.1 %copy-start.1 = (bf16[1,2,512,512]{3,2,1,0:T(8,128)(2,1)S(1)}, bf16[1,2,512,512]{3,2,1,0:T(8,128)(2,1)}, u32[]{:S(2)}) copy-start(bf16[1,2,512,512]{3,2,1,0:T(8,128)(2,1)} %param.11) | copy-start | bytes 3145732
  2.5 27.5 %all-to-all-start = ((bf16[2,32,16,512]{3,2,0,1:T(8,128)(2,1)}), bf16[2,32,16,512]{3,2,0,1:T(8,128)(2,1)S(1)}, u32[]{:S(2)}, u32[]{:S(2)}) async-start(bf16[2,32,16,512]{3,2,0,1:T(8,128)(2,1)} %bitcast.95), calls=%async_computation | async-start | bytes 2097152 | tf_op jit(solution)/shard_map/all_to_all | solution.py:31
  25.4 33.5 %copy-start.6 = (pred[512]{0:T(512)(128)(4,1)}, pred[512]{0:T(512)(128)(4,1)S(1)}, u32[]{:S(2)}) copy-start(pred[512]{0:T(512)(128)(4,1)S(1)} %compare_and_fusion.1) | copy-start | bytes 1540
  25.4 34.8 %copy-start.5 = (pred[512]{0:T(512)(128)(4,1)}, pred[512]{0:T(512)(128)(4,1)S(1)}, u32[]{:S(2)}) copy-start(pred[512]{0:T(512)(128)(4,1)S(1)} %compare_and_fusion) | copy-start | bytes 1540
  26.5 34.0 %copy-start.4 = (f32[2,512]{1,0:T(2,128)}, f32[2,512]{1,0:T(2,128)S(1)}, u32[]{:S(2)}) copy-start(f32[2,512]{1,0:T(2,128)S(1)} %get-tuple-element.7) | copy-start | bytes 12292
  68.3 24.6 %copy-start.2 = (bf16[1,2,512,512]{3,2,1,0:T(8,128)(2,1)S(1)}, bf16[1,2,512,512]{3,2,1,0:T(8,128)(2,1)}, u32[]{:S(2)}) copy-start(bf16[1,2,512,512]{3,2,1,0:T(8,128)(2,1)} %param.11) | copy-start | bytes 3145732
where the time goes:
time: 138 us; the launch traced here: 137 us
  blocking collectives  80.9 us (59%)
  local copies, waits for them, and re-layouts  14.7 us (11%)
  starting transfers between devices  10.5 us (8%)
  between operations  10.2 us (7%)
  other arithmetic  9.87 us (7%)
  matrix products  7.85 us (6%)
  waiting for transfers between devices  3.45 us (2%)
    all_gather x2, blocking collectives, plane_ghosts(): blocks = lax.all_gather(layers[None], 'blk', axis=0, tiled=True)  46.3 us
    all_to_all x1, blocking collectives, local(): lax.all_to_all(planes, 'pen', split_axis=2, concat_axis=1, tiled=True)  34.6 us
    all_to_all x1, starting transfers between devices, local(): lax.all_to_all(magnet, 'pen', split_axis=1, concat_axis=2, tiled=True)  10.5 us
    dot_general x2, matrix products, local(): jnp.einsum('fcy,fzyx->fzcx', inv_y, swept_x, preferred_element_type=jnp.f...  7.85 us
    another operation x2, other arithmetic  7.59 us
    gather x4, local copies, waits for them, and re-layouts, plane_ghosts(): result.append(jnp.take(segment, take_at, axis=-1))  5.36 us
    all_to_all x1, waiting for transfers between devices, local(): lax.all_to_all(magnet, 'pen', split_axis=1, concat_axis=2, tiled=True)  3.45 us
    unnamed x28, local copies, waits for them, and re-layouts  3.23 us
  transfers between devices with their start and end apart: 1, of which 1 were waited for; matrix products, arithmetic and copies ran while one was open for 3% of the time, Pallas kernels for 0%

commit v1 on v0

--- a/solution.py
+++ b/solution.py
@@ -7,7 +7,8 @@
 
 
 def plane_ghosts(layers, partner_row, side_row, orient_row, offset_row, tile_rows):
-    blocks = lax.all_gather(layers[None], "blk", axis=0, tiled=True)
+    copies = jnp.broadcast_to(layers[None], (lax.axis_size("blk"),) + layers.shape)
+    blocks = lax.all_to_all(copies, "blk", split_axis=0, concat_axis=0, tiled=True)
     lines = layers.shape[-1]
     rows_y = jnp.arange(lines, dtype=jnp.int32)
     result = []

time: 138 us -> 120 us (0.87)
  blocking collectives: 80.9 us -> 37.9 us
  starting transfers between devices: 10.5 us -> 23.4 us
  waiting for transfers between devices: 3.45 us -> 14 us
    all_gather x2 -> x0, blocking collectives: 46.3 us -> none  [plane_ghosts(): blocks = lax.all_gather(layers[None], 'blk', axis=0, tiled=True)]
    all_to_all x0 -> x1, blocking collectives: none -> 15.5 us  [plane_ghosts(): lax.all_to_all(copies, 'blk', split_axis=0, concat_axis=0, tiled=True)]
    all_to_all x0 -> x1, starting transfers between devices: none -> 13 us  [plane_ghosts(): lax.all_to_all(copies, 'blk', split_axis=0, concat_axis=0, tiled=True)]
    all_to_all x1, blocking collectives: 34.6 us -> 22.5 us  [local(): lax.all_to_all(planes, 'pen', split_axis=2, concat_axis=1, tiled=True)]
    all_to_all x0 -> x1, waiting for transfers between devices: none -> 10.2 us  [plane_ghosts(): lax.all_to_all(copies, 'blk', split_axis=0, concat_axis=0, tiled=True)]
    unnamed x28 -> x22, local copies, waits for them, and re-layouts: 3.23 us -> 2.42 us
    another operation x4 -> x2, other arithmetic: 7.61 us -> 7.49 us
  transfers between devices with their start and end apart: 1 -> 2, of which waited for: 1 -> 2; matrix products, arithmetic and copies ran while one was open for 3% -> 4% of each run, Pallas kernels for 0% -> 0%
where the time goes in v1:
time: 120 us
  blocking collectives  37.9 us (32%)
  starting transfers between devices  23.4 us (20%)
  local copies, waits for them, and re-layouts  15.3 us (13%)
  waiting for transfers between devices  14 us (12%)
  other arithmetic  10.9 us (9%)
  between operations  10.2 us (8%)
  matrix products  7.86 us (7%)
    all_to_all x1, blocking collectives, local(): lax.all_to_all(planes, 'pen', split_axis=2, concat_axis=1, tiled=True)  22.5 us
    all_to_all x1, blocking collectives, plane_ghosts(): lax.all_to_all(copies, 'blk', split_axis=0, concat_axis=0, tiled=True)  15.5 us
    all_to_all x1, starting transfers between devices, plane_ghosts(): lax.all_to_all(copies, 'blk', split_axis=0, concat_axis=0, tiled=True)  13 us
    all_to_all x1, starting transfers between devices, local(): lax.all_to_all(magnet, 'pen', split_axis=1, concat_axis=2, tiled=True)  10.5 us
    all_to_all x1, waiting for transfers between devices, plane_ghosts(): lax.all_to_all(copies, 'blk', split_axis=0, concat_axis=0, tiled=True)  10.2 us
    dot_general x2, matrix products, local(): jnp.einsum('fcy,fzyx->fzcx', inv_y, swept_x, preferred_element_type=jnp.f...  7.86 us
    another operation x2, other arithmetic  7.49 us
    gather x4, local copies, waits for them, and re-layouts, plane_ghosts(): result.append(jnp.take(segment, take_at, axis=-1))  5.36 us
  transfers between devices with their start and end apart: 2, of which 2 were waited for; matrix products, arithmetic and copies ran while one was open for 4% of the time, Pallas kernels for 0%

profile of v1, /device:TPU:1, one launch (start us, length us, event | category | flops | bytes accessed | tf_op | source)
XLA Modules:
  0.0 119.7 jit_solution(8040975433714026391)
XLA Ops:
  0.0 2.4 %copy.70 = bf16[1,2,32,16,512]{4,3,1,2,0:T(8,128)(2,1)} copy(bf16[1,2,32,16,512]{4,3,2,1,0:T(8,128)(2,1)} %param.10) | data formatting | bytes 2097152 | tf_op args[0]
  2.4 10.5 %all-to-all-start = ((bf16[2,32,16,512]{3,2,0,1:T(8,128)(2,1)}), bf16[2,32,16,512]{3,2,0,1:T(8,128)(2,1)S(1)}, u32[]{:S(2)}, u32[]{:S(2)}) async-start(bf16[2,32,16,512]{3,2,0,1:T(8,128)(2,1)} %bitcast.97), calls=%async_computation | async-start | bytes 2097152 | tf_op jit(solution)/shard_map/all_to_all | solution.py:32
  12.9 0.6 fusion.19
  16.0 0.7 fusion.18
  21.7 0.6 fusion.16
  23.4 0.7 fusion.17
  25.4 0.7 fusion.15
  26.1 3.8 %all-to-all-done = bf16[2,32,16,512]{3,2,0,1:T(8,128)(2,1)S(1)} async-done(((bf16[2,32,16,512]{3,2,0,1:T(8,128)(2,1)}), bf16[2,32,16,512]{3,2,0,1:T(8,128)(2,1)S(1)}, u32[]{:S(2)}, u32[]{:S(2)}) %all-to-all-start) | async-done | bytes 1048608 | tf_op jit(solution)/shard_map/all_to_all | solution.py:32
  30.0 0.3 slice_reduce_fusion.1
  30.3 0.7 broadcast_in_dim.20
  31.0 13.0 %all-to-all-start.1 = ((bf16[16,2,2,1,512]{4,2,3,1,0:T(2,128)(2,1)}), bf16[16,2,2,1,512]{4,2,3,1,0:T(2,128)(2,1)S(1)}, u32[]{:S(2)}, u32[]{:S(2)}) async-start(bf16[16,2,2,1,512]{4,2,3,1,0:T(2,128)(2,1)} %broadcast_in_dim.20), calls=%async_computation.1 | async-start | bytes 131072 | tf_op jit(solution)/shard_map/all_to_all | solution.py:11
  44.0 1.3 %convert_reduce_fusion.1 = (f32[2,512]{1,0:T(2,128)S(1)}, f32[2,512]{1,0:T(2,128)S(1)}) fusion(bf16[2,512,512]{2,1,0:T(8,128)(2,1)} %bitcast.102), kind=kLoop, calls=%fused_computation.20 | loop fusion | flops 2048 | bytes 12288 | tf_op jit(solution)/shard_map/convert_element_type | solution.py:29
  45.3 10.2 %all-to-all-done.1 = bf16[16,2,2,1,512]{4,2,3,1,0:T(2,128)(2,1)S(1)} async-done(((bf16[16,2,2,1,512]{4,2,3,1,0:T(2,128)(2,1)}), bf16[16,2,2,1,512]{4,2,3,1,0:T(2,128)(2,1)S(1)}, u32[]{:S(2)}, u32[]{:S(2)}) %all-to-all-start.1) | async-done | bytes 65568 | tf_op jit(solution)/shard_map/all_to_all | solution.py:11
  55.6 0.2 copy.49
  55.8 1.3 %gather_fusion = bf16[512,2]{1,0:T(8,128)(2,1)S(1)} fusion(bf16[2,512]{0,1:T(8,128)(2,1)S(1)} %bitcast.105, s32[1024]{0:T(1024)S(1)} %pad_clamp_fusion.1), kind=kCustom, calls=%fused_computation.clone | custom fusion | bytes 6144 | tf_op jit(solution)/shard_map/jit(_take)/gather | solution.py:20
  57.4 0.2 copy.51
  57.6 1.3 %gather_fusion.1 = bf16[512,2]{1,0:T(8,128)(2,1)S(1)} fusion(bf16[2,512]{0,1:T(8,128)(2,1)S(1)} %bitcast.106, s32[1024]{0:T(1024)S(1)} %pad_clamp_fusion), kind=kCustom, calls=%fused_computation.1.clone | custom fusion | bytes 6144 | tf_op jit(solution)/shard_map/jit(_take)/gather | solution.py:20
  58.9 0.1 bitcast_convert_fusion.2
  59.2 4.0 %convolution_bitcast_fusion.1 = f32[2,1,512,512]{2,3,0,1:T(8,128)} fusion(bf16[1,2,512,512]{3,2,1,0:T(8,128)(2,1)S(1)} %copy-done, bf16[2,512,512]{2,1,0:T(8,128)(2,1)S(1)} %bitcast.99, f32[2,512]{1,0:T(2,128)S(1)} %copy.52, f32[2,512]{1,0:T(2,128)S(1)} %get-tuple-element.7, f32[2,512]{1,0:T(2,128)S(1)} %copy.50, f32[2,512]{1,0:T(2,128)S(1)} %get-tuple-element.6, ...), kind=kOutput, calls=%fused_computation.7 | convolution fusion | flops 1076363264 | bytes 5259264 | tf_op jit(solution)/shard_map/fcy,fzyx->fzcx/dot_general | solution.py:40
  63.1 3.7 %subtract_convert_fusion.3 = (bf16[1,1,512,512]{2,3,0,1:T(8,128)(2,1)S(1)}, bf16[1,1,512,512]{2,3,0,1:T(8,128)(2,1)S(1)}) fusion(f32[2,1,512,512]{2,3,0,1:T(8,128)} %convolution_bitcast_fusion.1, f32[]{:T(128)} %bitcast.27, f32[]{:T(128)} %bitcast.26, f32[]{:T(128)} %bitcast.30), kind=kLoop, calls=%fused_computation.18 | loop fusion | flops 2621440 | bytes 3145740 | tf_op jit(solution)/shard_map/convert.13
  67.0 15.5 %all_to_all.31 = bf16[16,2,2,1,512]{4,2,3,1,0:T(2,128)(2,1)S(1)} all-to-all(bf16[16,2,2,1,512]{4,2,3,1,0:T(2,128)(2,1)S(1)} %broadcast_in_dim.22), channel_id=1, replica_groups=mesh['blk'=16,'pen'=32] {'blk'}, dimensions={0} | all-to-all | bytes 131072 | tf_op jit(solution)/shard_map/all_to_all | solution.py:11
  82.5 0.2 copy.55
  82.7 1.3 %gather_fusion.2 = bf16[512,2]{1,0:T(8,128)(2,1)S(1)} fusion(bf16[2,512]{0,1:T(8,128)(2,1)S(1)} %bitcast.103, s32[1024]{0:T(1024)S(1)} %pad_clamp_fusion.1), kind=kCustom, calls=%fused_computation.2.clone | custom fusion | bytes 6144 | tf_op jit(solution)/shard_map/jit(_take)/gather | solution.py:20
  84.0 0.8 bitcast_convert_fusion.1
  84.9 0.2 copy.57
  85.1 1.3 %gather_fusion.3 = bf16[512,2]{1,0:T(8,128)(2,1)S(1)} fusion(bf16[2,512]{0,1:T(8,128)(2,1)S(1)} %bitcast.104, s32[1024]{0:T(1024)S(1)} %pad_clamp_fusion), kind=kCustom, calls=%fused_computation.3.clone | custom fusion | bytes 6144 | tf_op jit(solution)/shard_map/jit(_take)/gather | solution.py:20
  86.5 0.7 bitcast_convert_fusion
  87.3 3.9 %convolution_bitcast_fusion = f32[2,1,512,512]{2,3,0,1:T(8,128)} fusion(bf16[1,2,512,512]{3,2,1,0:T(8,128)(2,1)S(1)} %copy-done, bf16[1,512,512]{1,2,0:T(8,128)(2,1)S(1)} %bitcast.101, bf16[1,512,512]{1,2,0:T(8,128)(2,1)S(1)} %bitcast.100, f32[2,512]{1,0:T(2,128)S(1)} %copy.58, f32[2,512]{1,0:T(2,128)S(1)} %copy.56, f32[2,512]{1,0:T(2,128)} %copy-done.3, ...), kind=kOutput, calls=%fused_computation.6 | convolution fusion | flops 1076887552 | bytes 5259264 | tf_op jit(solution)/shard_map/fcy,fzyx->fzcx/dot_general | solution.py:40
  91.2 3.7 %subtract_convert_fusion.1 = (bf16[1,1,512,512]{2,3,0,1:T(8,128)(2,1)S(1)}, bf16[1,1,512,512]{2,3,0,1:T(8,128)(2,1)S(1)}) fusion(f32[2,1,512,512]{2,3,0,1:T(8,128)} %convolution_bitcast_fusion, f32[]{:T(128)} %bitcast.27, f32[]{:T(128)} %bitcast.26, f32[]{:T(128)} %bitcast.30), kind=kLoop, calls=%fused_computation.16 | loop fusion | flops 2621440 | bytes 3145740 | tf_op jit(solution)/shard_map/convert.6
  95.1 1.0 copy.60
  96.1 22.5 %all_to_all.32 = bf16[2,1,512,512]{3,0,1,2:T(2,128)(2,1)S(1)} all-to-all(bf16[2,1,512,512]{3,0,1,2:T(2,128)(2,1)S(1)} %copy.60), channel_id=1, replica_groups=mesh['blk'=16,'pen'=32] {'pen'}, dimensions={2} | all-to-all | bytes 2097152 | tf_op jit(solution)/shard_map/all_to_all | solution.py:46
  118.5 1.1 copy.61
  (40 shorter events, 1.0 us)
Async XLA Ops:
  0.0 59.2 %copy-start = (bf16[1,2,512,512]{3,2,1,0:T(8,128)(2,1)S(1)}, bf16[1,2,512,512]{3,2,1,0:T(8,128)(2,1)}, u32[]{:S(2)}) copy-start(bf16[1,2,512,512]{3,2,1,0:T(8,128)(2,1)} %param.12) | copy-start | bytes 3145732
  0.0 12.9 %copy-start.6 = (s32[1,2]{1,0:T(1,128)S(1)}, s32[1,2]{1,0:T(1,128)}, u32[]{:S(2)}) copy-start(s32[1,2]{1,0:T(1,128)} %param.14) | copy-start | bytes 28
  0.0 16.0 %copy-start.7 = (s32[1,2]{1,0:T(1,128)S(1)}, s32[1,2]{1,0:T(1,128)}, u32[]{:S(2)}) copy-start(s32[1,2]{1,0:T(1,128)} %param.15) | copy-start | bytes 28
  0.0 21.6 %copy-start.8 = (s32[1,2]{1,0:T(1,128)S(1)}, s32[1,2]{1,0:T(1,128)}, u32[]{:S(2)}) copy-start(s32[1,2]{1,0:T(1,128)} %param.16) | copy-start | bytes 28
  0.0 23.4 %copy-start.9 = (s32[1,2]{1,0:T(1,128)S(1)}, s32[1,2]{1,0:T(1,128)}, u32[]{:S(2)}) copy-start(s32[1,2]{1,0:T(1,128)} %param.17) | copy-start | bytes 28
  0.0 25.4 %copy-start.2 = (f32[1,3]{1,0:T(1,128)S(1)}, f32[1,3]{1,0:T(1,128)}, u32[]{:S(2)}) copy-start(f32[1,3]{1,0:T(1,128)} %param.13) | copy-start | bytes 40
  2.4 27.5 %all-to-all-start = ((bf16[2,32,16,512]{3,2,0,1:T(8,128)(2,1)}), bf16[2,32,16,512]{3,2,0,1:T(8,128)(2,1)S(1)}, u32[]{:S(2)}, u32[]{:S(2)}) async-start(bf16[2,32,16,512]{3,2,0,1:T(8,128)(2,1)} %bitcast.97), calls=%async_computation | async-start | bytes 2097152 | tf_op jit(solution)/shard_map/all_to_all | solution.py:32
  25.3 32.0 %copy-start.4 = (pred[512]{0:T(512)(128)(4,1)}, pred[512]{0:T(512)(128)(4,1)S(1)}, u32[]{:S(2)}) copy-start(pred[512]{0:T(512)(128)(4,1)S(1)} %compare_and_fusion.1) | copy-start | bytes 1540
  31.0 24.6 %all-to-all-start.1 = ((bf16[16,2,2,1,512]{4,2,3,1,0:T(2,128)(2,1)}), bf16[16,2,2,1,512]{4,2,3,1,0:T(2,128)(2,1)S(1)}, u32[]{:S(2)}, u32[]{:S(2)}) async-start(bf16[16,2,2,1,512]{4,2,3,1,0:T(2,128)(2,1)} %broadcast_in_dim.20), calls=%async_computation.1 | async-start | bytes 131072 | tf_op jit(solution)/shard_map/all_to_all | solution.py:11
  44.0 19.2 %copy-start.5 = (pred[512]{0:T(512)(128)(4,1)}, pred[512]{0:T(512)(128)(4,1)S(1)}, u32[]{:S(2)}) copy-start(pred[512]{0:T(512)(128)(4,1)S(1)} %compare_and_fusion) | copy-start | bytes 1540
  45.3 17.8 %copy-start.3 = (f32[2,512]{1,0:T(2,128)}, f32[2,512]{1,0:T(2,128)S(1)}, u32[]{:S(2)}) copy-start(f32[2,512]{1,0:T(2,128)S(1)} %get-tuple-element.7) | copy-start | bytes 12292
  66.9 20.4 %copy-start.1 = (bf16[1,2,512,512]{3,2,1,0:T(8,128)(2,1)S(1)}, bf16[1,2,512,512]{3,2,1,0:T(8,128)(2,1)}, u32[]{:S(2)}) copy-start(bf16[1,2,512,512]{3,2,1,0:T(8,128)(2,1)} %param.11) | copy-start | bytes 3145732

commit v2 on v0

v2 whole, which is shorter than its diff:
```python
import functools

import jax
import jax.numpy as jnp
from jax import lax
from jax.experimental import pallas as pl
from jax.experimental.pallas import tpu as pltpu
from jax.sharding import PartitionSpec as P

STEPS = 2
SLOT_ROWS = 8
F32 = jnp.float32
BF16 = jnp.bfloat16
VMEM = pl.BlockSpec(memory_space=pltpu.VMEM)
SMEM = pl.BlockSpec(memory_space=pltpu.SMEM)
NT = (((1,), (1,)), ((), ()))
TN = (((0,), (0,)), ((), ()))


def params():
    return pltpu.CompilerParams(vmem_limit_bytes=32 * 1024 * 1024)


def rows_of(shape):
    return lax.broadcasted_iota(jnp.int32, shape, 0)


def transpose_kernel(source, target):
    for field in range(2):
        target[:, field] = source[field]


def untranspose_kernel(source, target):
    for field in range(2):
        target[field] = source[:, field]


def to_planes(state):
    fields, planes, lines, cells = state.shape
    chunk = planes // 4
    return pl.pallas_call(
        transpose_kernel,
        out_shape=jax.ShapeDtypeStruct((planes, fields, lines, cells), BF16),
        grid=(4,),
        in_specs=[pl.BlockSpec((fields, chunk, lines, cells), lambda i: (0, i, 0, 0))],
        out_specs=pl.BlockSpec((chunk, fields, lines, cells), lambda i: (i, 0, 0, 0)),
        name="to_planes",
    )(state)


def from_planes(moved):
    planes, fields, lines, cells = moved.shape
    chunk = planes // 4
    return pl.pallas_call(
        untranspose_kernel,
        out_shape=jax.ShapeDtypeStruct((fields, planes, lines, cells), BF16),
        grid=(4,),
        in_specs=[pl.BlockSpec((chunk, fields, lines, cells), lambda i: (i, 0, 0, 0))],
        out_specs=pl.BlockSpec((fields, chunk, lines, cells), lambda i: (0, i, 0, 0)),
        name="from_planes",
    )(moved)


def field_plane(planes, field):
    cells = planes.shape[-1]
    return planes[:, field].reshape(-1, cells)


def ends_kernel(inv_x, ends):
    cells = inv_x.shape[-1]
    lane = lax.broadcasted_iota(jnp.int32, (16, cells), 1)
    row = rows_of((16, cells))
    pick = ((row == 0) & (lane == 0)) | ((row == 1) & (lane == cells - 1))
    pick = jnp.where(pick, 1.0, 0.0).astype(BF16)
    for field in range(2):
        ends[field] = lax.dot_general(pick, inv_x[field], NT, preferred_element_type=F32).astype(BF16)


def layers_kernel(planes, sent):
    cells = planes.shape[-1]
    total = None
    lane = lax.broadcasted_iota(jnp.int32, (SLOT_ROWS, 128), 1)
    row = rows_of((SLOT_ROWS, 128))
    for field in range(2):
        for end in range(2):
            pick = (row == field * 2 + end) & (lane == end * 127)
            pick = jnp.where(pick, 1.0, 0.0).astype(BF16)
            start = end * (cells - 128)
            edge = planes[:, field, :, start:start + 128].reshape(-1, 128)
            part = lax.dot_general(pick, edge, NT, preferred_element_type=F32)
            total = part if total is None else total + part
    total = total.astype(BF16)
    for slot in range(sent.shape[0]):
        sent[slot] = total


def interior_kernel(planes, inv_x, interior, corners):
    cells = inv_x.shape[-1]
    row = rows_of((16, cells))
    for field in range(2):
        plane = field_plane(planes, field)
        weights = inv_x[field]
        interior[field] = lax.dot_general(plane, weights, NT, preferred_element_type=F32)
        first = weights[0:16].astype(F32)[0:1]
        last = weights[cells - 16:cells].astype(F32)[15:16]
        two = jnp.where(row == 0, first, jnp.where(row == 1, last, 0.0)).astype(BF16)
        corners[field] = lax.dot_general(two, plane, NT, preferred_element_type=F32)[0:8]


def turned(layer, orient, shift):
    cells = layer.shape[-1]
    layer = pltpu.roll(layer, lax.rem(cells - shift, cells), 1)
    back = 127 - lax.broadcasted_iota(jnp.int32, (layer.shape[0], 128), 1)
    pieces = [
        jnp.take_along_axis(layer[:, at:at + 128], back, axis=1)
        for at in range(cells - 128, -1, -128)
    ]
    return jnp.where(orient == 1, jnp.concatenate(pieces, axis=1), layer)


def ghost_rows(tables, blocks, tile_rows):
    result = []
    for which in range(2):
        layer = blocks[tables[0, which]].astype(F32)
        moved = pltpu.roll(layer, SLOT_ROWS - 1, 0)
        layer = jnp.where(tables[1, which] == 1, moved, layer)
        result.append(turned(layer, tables[2, which], tables[3, which] * tile_rows))
    return result


def packed_ghosts(sides, field):
    cells = sides[0].shape[-1]
    row = rows_of((16, cells))
    at = field * 2
    low = sides[0][at:at + 1]
    high = sides[1][at:at + 1]
    return jnp.where(row == 0, low, jnp.where(row == 1, high, 0.0)).astype(BF16)


def mix(rates, proton, carbon):
    new_proton = proton - (rates[0, 0] * proton + rates[0, 2] * carbon)
    new_carbon = carbon - (rates[0, 1] * carbon + rates[0, 2] * proton)
    return new_proton, new_carbon


def next_layers_kernel(tile_rows, tables, rates, blocks, corners, ends, inv_y, sent, ghosts):
    cells = ends.shape[-1]
    sides = ghost_rows(tables, blocks, tile_rows)
    row = rows_of((16, cells))
    swept = []
    for field in range(2):
        at = field * 2
        edge = ends[field].astype(F32)
        ghosts[field] = packed_ghosts(sides, field)
        found = []
        for end in range(2):
            lane = end * (cells - 1)
            value = corners[field][end:end + 1]
            for which in range(2):
                value = value + edge[which:which + 1, lane:lane + 1] * sides[which][at:at + 1]
            found.append(value)
        two = jnp.where(row == 0, found[0], jnp.where(row == 1, found[1], 0.0)).astype(BF16)
        swept.append(lax.dot_general(two, inv_y[field], NT, preferred_element_type=F32)[0:8])
    new_proton, new_carbon = mix(rates, swept[0], swept[1])
    row8 = rows_of(new_proton.shape)
    total = jnp.where(row8 < 2, new_proton, pltpu.roll(new_carbon, 2, 0)).astype(BF16)
    for slot in range(sent.shape[0]):
        sent[slot] = total


def second_sweep(rates, interior, ghosts, ends, inv_y, emit):
    lines = inv_y.shape[-2]
    swept = []
    for field in range(2):
        outer = lax.dot_general(ghosts[field], ends[field], TN, preferred_element_type=F32)
        swept.append((interior[field] + outer).astype(BF16))
    chunk = lines // 2
    for start in range(0, lines, chunk):
        moved = [
            jnp.dot(inv_y[field, start:start + chunk], swept[field], preferred_element_type=F32)
            for field in range(2)
        ]
        new = mix(rates, moved[0], moved[1])
        for field in range(2):
            emit(field, start, chunk, new[field].astype(BF16))


def middle_kernel(rates, interior, ghosts, ends, inv_y, inv_x, following):
    def emit(field, start, chunk, values):
        following[field, start:start + chunk] = lax.dot_general(
            values, inv_x[field], NT, preferred_element_type=F32
        )

    second_sweep(rates, interior, ghosts, ends, inv_y, emit)


def last_kernel(tile_rows, tables, rates, blocks, interior, ends, inv_y, planes):
    sides = ghost_rows(tables, blocks, tile_rows)
    ghosts = [packed_ghosts(sides, field) for field in range(2)]
    cells = ends.shape[-1]

    def emit(field, start, chunk, values):
        first = start // tile_rows
        planes[first:first + chunk // tile_rows, field] = values.reshape(-1, tile_rows, cells)

    second_sweep(rates, interior, ghosts, ends, inv_y, emit)


def cost(flops, nbytes):
    return pl.CostEstimate(flops=flops, bytes_accessed=nbytes, transcendentals=0)


def local(state, inverse_x, inverse_y, rates, partner, face_side, orient, offset):
    magnet = state[0]
    inv_x = inverse_x[0]
    inv_y = inverse_y[0]
    fields, depth, tile_rows, cells = magnet.shape
    lines = inv_y.shape[-1]
    count = lax.axis_size("blk")
    tables = jnp.concatenate([partner, face_side, orient, offset], axis=0)
    slots = jax.ShapeDtypeStruct((count, SLOT_ROWS, lines), BF16)
    packed = jax.ShapeDtypeStruct((fields, 16, lines), BF16)
    swept = jax.ShapeDtypeStruct((fields, lines, cells), F32)
    sweep_flops = 2 * fields * lines * cells * cells
    array_bytes = 2 * fields * lines * cells

    moved = lax.all_to_all(to_planes(magnet), "pen", split_axis=0, concat_axis=0, tiled=True)
    ends = pl.pallas_call(
        ends_kernel,
        out_shape=jax.ShapeDtypeStruct((fields, 16, cells), BF16),
        in_specs=[VMEM],
        out_specs=VMEM,
        compiler_params=params(),
        cost_estimate=cost(sweep_flops // 16, array_bytes),
        name="ends",
    )(inv_x)
    sent = pl.pallas_call(
        layers_kernel,
        out_shape=slots,
        in_specs=[VMEM],
        out_specs=VMEM,
        compiler_params=params(),
        cost_estimate=cost(sweep_flops // 16, array_bytes),
        name="layers",
    )(moved)
    blocks = lax.all_to_all(sent, "blk", split_axis=0, concat_axis=0, tiled=True)
    interior, corners = pl.pallas_call(
        interior_kernel,
        out_shape=(swept, jax.ShapeDtypeStruct((fields, 8, lines), F32)),
        in_specs=[VMEM, VMEM],
        out_specs=(VMEM, VMEM),
        compiler_params=params(),
        cost_estimate=cost(sweep_flops, 4 * array_bytes),
        name="interior",
    )(moved, inv_x)
    sent, ghosts = pl.pallas_call(
        functools.partial(next_layers_kernel, tile_rows),
        out_shape=(slots, packed),
        in_specs=[SMEM, SMEM, VMEM, VMEM, VMEM, VMEM],
        out_specs=(VMEM, VMEM),
        compiler_params=params(),
        cost_estimate=cost(sweep_flops // 16, array_bytes),
        name="next_layers",
    )(tables, rates, blocks, corners, ends, inv_y)
    blocks = lax.all_to_all(sent, "blk", split_axis=0, concat_axis=0, tiled=True)
    interior = pl.pallas_call(
        middle_kernel,
        out_shape=swept,
        in_specs=[SMEM, VMEM, VMEM, VMEM, VMEM, VMEM],
        out_specs=VMEM,
        compiler_params=params(),
        cost_estimate=cost(2 * sweep_flops, 6 * array_bytes),
        name="middle",
    )(rates, interior, ghosts, ends, inv_y, inv_x)
    planes = pl.pallas_call(
        functools.partial(last_kernel, tile_rows),
        out_shape=jax.ShapeDtypeStruct((lines // tile_rows, fields, tile_rows, cells), BF16),
        in_specs=[SMEM, SMEM, VMEM, VMEM, VMEM, VMEM],
        out_specs=VMEM,
        compiler_params=params(),
        cost_estimate=cost(sweep_flops, 4 * array_bytes),
        name="last",
    )(tables, rates, blocks, interior, ends, inv_y)
    back = lax.all_to_all(planes, "pen", split_axis=0, concat_axis=0, tiled=True)
    return from_planes(back)[None]


def solution(mesh):
    return jax.shard_map(
        local,
        mesh=mesh,
        in_specs=(
            P("blk", None, None, "pen", None),
            P("blk", None, None, None),
            P("blk", None, None, None),
            P("blk", None),
            P("blk", None),
            P("blk", None),
            P("blk", None),
            P("blk", None),
        ),
        out_specs=P("blk", None, None, "pen", None),
        check_vma=False,
    )
```

time: 138 us -> 109 us (0.79)
  blocking collectives: 80.9 us -> 51.6 us
  Pallas kernels: 0 us -> 15 us
  waiting for transfers between devices: 3.45 us -> 16.1 us
  between operations: 10.2 us -> 0.12 us
  other arithmetic: 9.87 us -> 0.01 us
  starting transfers between devices: 10.5 us -> 19.4 us
  local copies, waits for them, and re-layouts: 14.7 us -> 5.86 us
  matrix products: 7.85 us -> 0 us
    all_gather x2 -> x0, blocking collectives: 46.3 us -> none  [plane_ghosts(): blocks = lax.all_gather(layers[None], 'blk', axis=0, tiled=True)]
    all_to_all x1 -> x2, blocking collectives: 34.6 us -> 51.6 us  [the longest x1 27.6 us: local(): lax.all_to_all(to_planes(magnet), 'pen', split_axis=0, concat_axis=0, til...]
    pallas_call x0 -> x8, Pallas kernels: none -> 15 us  [the longest x1 3.36 us: to_planes(): pl.pallas_call(transpose_kernel, out_shape=jax.ShapeDtypeStruct((planes,...]
    all_to_all x1 -> x2, waiting for transfers between devices: 3.45 us -> 16.1 us  [local(): lax.all_to_all(sent, 'blk', split_axis=0, concat_axis=0, tiled=True)]
    all_to_all x1 -> x2, starting transfers between devices: 10.5 us -> 19.4 us  [local(): lax.all_to_all(sent, 'blk', split_axis=0, concat_axis=0, tiled=True)]
    dot_general x2 -> x0, matrix products: 7.85 us -> none  [local(): jnp.einsum('fcy,fzyx->fzcx', inv_y, swept_x, preferred_element_type=jnp.f...]
    another operation x5 -> x0, other arithmetic: 7.71 us -> none
    gather x4 -> x0, local copies, waits for them, and re-layouts: 5.36 us -> none  [plane_ghosts(): result.append(jnp.take(segment, take_at, axis=-1))]
  transfers between devices with their start and end apart: 1 -> 2, of which waited for: 1 -> 2; matrix products, arithmetic and copies ran while one was open for 3% -> 0% of each run, Pallas kernels for 0% -> 3%
where the time goes in v2:
time: 109 us; the launch traced here: 108 us
  blocking collectives  51.6 us (47%)
  starting transfers between devices  19.4 us (18%)
  waiting for transfers between devices  16.1 us (15%)
  Pallas kernels  15 us (14%)
  local copies, waits for them, and re-layouts  5.86 us (5%)
    all_to_all x1, blocking collectives, local(): lax.all_to_all(to_planes(magnet), 'pen', split_axis=0, concat_axis=0, til...  27.6 us
    all_to_all x1, blocking collectives, local(): lax.all_to_all(planes, 'pen', split_axis=0, concat_axis=0, tiled=True)  24 us
    all_to_all x2, starting transfers between devices, local(): lax.all_to_all(sent, 'blk', split_axis=0, concat_axis=0, tiled=True)  19.4 us
    all_to_all x2, waiting for transfers between devices, local(): lax.all_to_all(sent, 'blk', split_axis=0, concat_axis=0, tiled=True)  16.1 us
    unnamed x22, local copies, waits for them, and re-layouts  5.86 us
    pallas_call x1, Pallas kernels, to_planes(): pl.pallas_call(transpose_kernel, out_shape=jax.ShapeDtypeStruct((planes,...  3.36 us
    pallas_call x1, Pallas kernels, from_planes(): pl.pallas_call(untranspose_kernel, out_shape=jax.ShapeDtypeStruct((fields...  3.36 us
    pallas_call x1, Pallas kernels, local(): pl.pallas_call(middle_kernel, out_shape=swept, in_specs=[SMEM, VMEM, VMEM...  2.41 us
  transfers between devices with their start and end apart: 2, of which 2 were waited for; matrix products, arithmetic and copies ran while one was open for 0% of the time, Pallas kernels for 3%

profile of v2, /device:TPU:1, one launch (start us, length us, event | category | flops | bytes accessed | tf_op | source)
XLA Modules:
  0.0 108.1 jit_solution(5210072938564286129)
XLA Ops:
  0.0 3.4 %to_planes.1 = bf16[32,2,16,512]{3,2,1,0:T(8,128)(2,1)} custom-call(bf16[2,32,16,512]{3,2,1,0:T(8,128)(2,1)} %bitcast.10), custom_call_target="tpu_custom_call" | custom-call | tf_op jit(solution)/shard_map/to_planes/pallas_call | solution.py:41
  3.4 0.0 copy-start
  3.4 0.0 copy-start.7
  3.4 0.0 copy-start.8
  3.4 0.0 copy-start.9
  3.4 0.0 copy-start.10
  3.4 27.6 %all_to_all.20.planes = bf16[32,2,16,512]{3,2,1,0:T(8,128)(2,1)S(1)} all-to-all(bf16[32,2,16,512]{3,2,1,0:T(8,128)(2,1)} %to_planes.1), channel_id=1, replica_groups=mesh['blk'=16,'pen'=32] {'pen'}, dimensions={0} | all-to-all | bytes 2097152 | tf_op jit(solution)/shard_map/all_to_all | solution.py:227
  31.0 0.9 layers.1
  31.9 13.0 %all-to-all-start.1 = ((bf16[16,8,512]{2,1,0:T(8,128)(2,1)}), bf16[16,8,512]{2,1,0:T(8,128)(2,1)S(1)}, u32[]{:S(2)}, u32[]{:S(2)}) async-start(bf16[16,8,512]{2,1,0:T(8,128)(2,1)} %layers.1), calls=%async_computation.1 | async-start | bytes 262144 | tf_op jit(solution)/shard_map/all_to_all | solution.py:246
  44.9 0.0 copy-done
  44.9 0.4 ends.1
  45.3 0.0 copy-done.7
  45.3 0.0 copy-done.8
  45.3 0.0 copy-done.9
  45.3 0.0 copy-done.10
  45.3 1.0 interior.1
  46.3 1.3 %copy-done.4 = f32[2,512,512]{2,1,0:T(8,128)} copy-done((f32[2,512,512]{2,1,0:T(8,128)}, f32[2,512,512]{2,1,0:T(8,128)S(1)}, u32[]{:S(2)}) %copy-start.4) | copy-done | bytes 2097176
  47.6 9.4 %all-to-all-done.1.blocks = bf16[16,8,512]{2,1,0:T(8,128)(2,1)S(1)} async-done(((bf16[16,8,512]{2,1,0:T(8,128)(2,1)}), bf16[16,8,512]{2,1,0:T(8,128)(2,1)S(1)}, u32[]{:S(2)}, u32[]{:S(2)}) %all-to-all-start.1) | async-done | bytes 131104 | tf_op jit(solution)/shard_map/all_to_all | solution.py:246
  57.0 0.0 copy-done.1
  57.0 0.0 copy-done.6
  57.0 1.7 %next_layers.1 = (bf16[16,8,512]{2,1,0:T(8,128)(2,1)}, bf16[2,16,512]{2,1,0:T(8,128)(2,1)S(1)}) custom-call(s32[4,2]{1,0:T(4,128)S(1)} %pad_add_fusion.tables, f32[1,3]{1,0:T(1,128)S(1)} %copy-done.6, bf16[16,8,512]{2,1,0:T(8,128)(2,1)S(1)} %all-to-all-done.1.blocks, f32[2,8,512]{2,1,0:T(8,128)S(1)} %get-tuple-element.9.corners, ...), custom_call_target="tpu_custom_call" | custom-call | flops 33554432 | bytes 1048576 | tf_op jit(solution)/shard_map/next_layers/pallas_call | solution.py:256
  58.8 6.4 %all-to-all-start.2 = ((bf16[16,8,512]{2,1,0:T(8,128)(2,1)}), bf16[16,8,512]{2,1,0:T(8,128)(2,1)S(1)}, u32[]{:S(2)}, u32[]{:S(2)}) async-start(bf16[16,8,512]{2,1,0:T(8,128)(2,1)} %get-tuple-element.10), calls=%async_computation.2 | async-start | bytes 262144 | tf_op jit(solution)/shard_map/all_to_all | solution.py:265
  65.2 0.0 copy-start.5
  65.2 1.6 %copy-done.5 = f32[2,512,512]{2,1,0:T(8,128)S(1)} copy-done((f32[2,512,512]{2,1,0:T(8,128)S(1)}, f32[2,512,512]{2,1,0:T(8,128)}, u32[]{:S(2)}) %copy-start.5) | copy-done | bytes 2097176
  66.8 2.4 %middle.1.interior = f32[2,512,512]{2,1,0:T(8,128)S(1)} custom-call(f32[1,3]{1,0:T(1,128)S(1)} %copy-done.6, f32[2,512,512]{2,1,0:T(8,128)S(1)} %copy-done.5, bf16[2,16,512]{2,1,0:T(8,128)(2,1)S(1)} %get-tuple-element.12.ghosts, bf16[2,16,512]{2,1,0:T(8,128)(2,1)S(1)} %ends.1, bf16[2,512,512]{2,1,0:T(8,128)(2,1)S(1)} %bitcast.8, bf16[2,512,512]{2,1,0:T(8,128)(2,1)S(1)} %bitcast.6), custom_call_target="tpu_custom_call" | custom-call | flops 1073741824 | bytes 6291456 | tf_op jit(solution)/shard_map/middle/pallas_call | solution.py:266
  69.2 0.0 copy-start.2
  69.2 1.3 %copy-done.2 = f32[2,512,512]{2,1,0:T(8,128)} copy-done((f32[2,512,512]{2,1,0:T(8,128)}, f32[2,512,512]{2,1,0:T(8,128)S(1)}, u32[]{:S(2)}) %copy-start.2) | copy-done | bytes 2097176
  70.5 6.7 %all-to-all-done.2.blocks = bf16[16,8,512]{2,1,0:T(8,128)(2,1)S(1)} async-done(((bf16[16,8,512]{2,1,0:T(8,128)(2,1)}), bf16[16,8,512]{2,1,0:T(8,128)(2,1)S(1)}, u32[]{:S(2)}, u32[]{:S(2)}) %all-to-all-start.2) | async-done | bytes 131104 | tf_op jit(solution)/shard_map/all_to_all | solution.py:265
  77.2 1.6 %copy-done.3 = f32[2,512,512]{2,1,0:T(8,128)S(1)} copy-done((f32[2,512,512]{2,1,0:T(8,128)S(1)}, f32[2,512,512]{2,1,0:T(8,128)}, u32[]{:S(2)}) %copy-start.3) | copy-done | bytes 2097176
  78.8 1.9 %last.1 = bf16[32,2,16,512]{3,2,1,0:T(8,128)(2,1)S(1)} custom-call(s32[4,2]{1,0:T(4,128)S(1)} %pad_add_fusion.tables, f32[1,3]{1,0:T(1,128)S(1)} %copy-done.6, bf16[16,8,512]{2,1,0:T(8,128)(2,1)S(1)} %all-to-all-done.2.blocks, f32[2,512,512]{2,1,0:T(8,128)S(1)} %copy-done.3, bf16[2,16,512]{2,1,0:T(8,128)(2,1)S(1)} %ends.1, bf16[2,512,512]{2,1,0:T(8,128)(2,1)S(1)} %bitcast.9), custom_call_target="tpu_custom_call" | custom-call | flops 536870912 | bytes 4194304 | tf_op jit(solution)/shard_map/last/pallas_call | solution.py:275
  80.7 24.0 %all_to_all.21.source = bf16[32,2,16,512]{3,2,1,0:T(8,128)(2,1)} all-to-all(bf16[32,2,16,512]{3,2,1,0:T(8,128)(2,1)S(1)} %last.1), channel_id=1, replica_groups=mesh['blk'=16,'pen'=32] {'pen'}, dimensions={0} | all-to-all | bytes 2097152 | tf_op jit(solution)/shard_map/all_to_all | solution.py:284
  104.7 3.4 %from_planes.1 = bf16[2,32,16,512]{3,2,1,0:T(8,128)(2,1)} custom-call(bf16[32,2,16,512]{3,2,1,0:T(8,128)(2,1)} %all_to_all.21.source), custom_call_target="tpu_custom_call" | custom-call | tf_op jit(solution)/shard_map/from_planes/pallas_call | solution.py:54
  (5 shorter events, 0.0 us)
Async XLA Ops:
  3.4 41.5 %copy-start = (bf16[1,2,512,512]{3,2,1,0:T(8,128)(2,1)S(1)}, bf16[1,2,512,512]{3,2,1,0:T(8,128)(2,1)}, u32[]{:S(2)}) copy-start(bf16[1,2,512,512]{3,2,1,0:T(8,128)(2,1)} %param.9) | copy-start | bytes 3145732
  3.4 41.9 %copy-start.7 = (s32[1,2]{1,0:T(1,128)S(1)}, s32[1,2]{1,0:T(1,128)}, u32[]{:S(2)}) copy-start(s32[1,2]{1,0:T(1,128)} %param.15) | copy-start | bytes 28
  3.4 41.9 %copy-start.8 = (s32[1,2]{1,0:T(1,128)S(1)}, s32[1,2]{1,0:T(1,128)}, u32[]{:S(2)}) copy-start(s32[1,2]{1,0:T(1,128)} %param.14) | copy-start | bytes 28
  3.4 41.9 %copy-start.9 = (s32[1,2]{1,0:T(1,128)S(1)}, s32[1,2]{1,0:T(1,128)}, u32[]{:S(2)}) copy-start(s32[1,2]{1,0:T(1,128)} %param.13) | copy-start | bytes 28
  3.4 41.9 %copy-start.10 = (s32[1,2]{1,0:T(1,128)S(1)}, s32[1,2]{1,0:T(1,128)}, u32[]{:S(2)}) copy-start(s32[1,2]{1,0:T(1,128)} %param.12) | copy-start | bytes 28
  31.0 26.0 %copy-start.1 = (bf16[1,2,512,512]{3,2,1,0:T(8,128)(2,1)S(1)}, bf16[1,2,512,512]{3,2,1,0:T(8,128)(2,1)}, u32[]{:S(2)}) copy-start(bf16[1,2,512,512]{3,2,1,0:T(8,128)(2,1)} %param.10) | copy-start | bytes 3145732
  31.0 26.0 %copy-start.6 = (f32[1,3]{1,0:T(1,128)S(1)}, f32[1,3]{1,0:T(1,128)}, u32[]{:S(2)}) copy-start(f32[1,3]{1,0:T(1,128)} %rates.5) | copy-start | bytes 40
  31.9 25.1 %all-to-all-start.1 = ((bf16[16,8,512]{2,1,0:T(8,128)(2,1)}), bf16[16,8,512]{2,1,0:T(8,128)(2,1)S(1)}, u32[]{:S(2)}, u32[]{:S(2)}) async-start(bf16[16,8,512]{2,1,0:T(8,128)(2,1)} %layers.1), calls=%async_computation.1 | async-start | bytes 262144 | tf_op jit(solution)/shard_map/all_to_all | solution.py:246
  46.3 1.3 %copy-start.4 = (f32[2,512,512]{2,1,0:T(8,128)}, f32[2,512,512]{2,1,0:T(8,128)S(1)}, u32[]{:S(2)}) copy-start(f32[2,512,512]{2,1,0:T(8,128)S(1)} %get-tuple-element.11.interior) | copy-start | bytes 6291460
  58.8 18.5 %all-to-all-start.2 = ((bf16[16,8,512]{2,1,0:T(8,128)(2,1)}), bf16[16,8,512]{2,1,0:T(8,128)(2,1)S(1)}, u32[]{:S(2)}, u32[]{:S(2)}) async-start(bf16[16,8,512]{2,1,0:T(8,128)(2,1)} %get-tuple-element.10), calls=%async_computation.2 | async-start | bytes 262144 | tf_op jit(solution)/shard_map/all_to_all | solution.py:265
  65.2 1.6 %copy-start.5 = (f32[2,512,512]{2,1,0:T(8,128)S(1)}, f32[2,512,512]{2,1,0:T(8,128)}, u32[]{:S(2)}) copy-start(f32[2,512,512]{2,1,0:T(8,128)} %copy-done.4) | copy-start | bytes 6291460
  69.2 1.3 %copy-start.2 = (f32[2,512,512]{2,1,0:T(8,128)}, f32[2,512,512]{2,1,0:T(8,128)S(1)}, u32[]{:S(2)}) copy-start(f32[2,512,512]{2,1,0:T(8,128)S(1)} %middle.1.interior) | copy-start | bytes 6291460
  77.2 1.6 %copy-start.3 = (f32[2,512,512]{2,1,0:T(8,128)S(1)}, f32[2,512,512]{2,1,0:T(8,128)}, u32[]{:S(2)}) copy-start(f32[2,512,512]{2,1,0:T(8,128)} %copy-done.2) | copy-start | bytes 6291460

commit v3 on v2

--- a/solution.py
+++ b/solution.py
@@ -15,6 +15,10 @@
 SMEM = pl.BlockSpec(memory_space=pltpu.SMEM)
 NT = (((1,), (1,)), ((), ()))
 TN = (((0,), (0,)), ((), ()))
+
+
+def turned_group(size, first):
+    return [[(first + member) % size for member in range(size)]]
 
 
 def params():
@@ -61,9 +65,10 @@
     )(moved)
 
 
-def field_plane(planes, field):
-    cells = planes.shape[-1]
-    return planes[:, field].reshape(-1, cells)
+def in_order(tiles, first):
+    count = tiles.shape[0]
+    ordered = jnp.concatenate([tiles[count - first:], tiles[:count - first]], axis=0)
+    return ordered.reshape(-1, tiles.shape[-1])
 
 
 def ends_kernel(inv_x, ends):
@@ -76,7 +81,7 @@
         ends[field] = lax.dot_general(pick, inv_x[field], NT, preferred_element_type=F32).astype(BF16)
 
 
-def layers_kernel(planes, sent):
+def layers_kernel(first, planes, sent):
     cells = planes.shape[-1]
     total = None
     lane = lax.broadcasted_iota(jnp.int32, (SLOT_ROWS, 128), 1)
@@ -86,7 +91,7 @@
             pick = (row == field * 2 + end) & (lane == end * 127)
             pick = jnp.where(pick, 1.0, 0.0).astype(BF16)
             start = end * (cells - 128)
-            edge = planes[:, field, :, start:start + 128].reshape(-1, 128)
+            edge = in_order(planes[:, field, :, start:start + 128], first)
             part = lax.dot_general(pick, edge, NT, preferred_element_type=F32)
             total = part if total is None else total + part
     total = total.astype(BF16)
@@ -94,11 +99,11 @@
         sent[slot] = total
 
 
-def interior_kernel(planes, inv_x, interior, corners):
+def interior_kernel(tile0, planes, inv_x, interior, corners):
     cells = inv_x.shape[-1]
     row = rows_of((16, cells))
     for field in range(2):
-        plane = field_plane(planes, field)
+        plane = in_order(planes[:, field], tile0)
         weights = inv_x[field]
         interior[field] = lax.dot_general(plane, weights, NT, preferred_element_type=F32)
         first = weights[0:16].astype(F32)[0:1]
@@ -120,8 +125,10 @@
 
 def ghost_rows(tables, blocks, tile_rows):
     result = []
+    count = blocks.shape[0]
     for which in range(2):
-        layer = blocks[tables[0, which]].astype(F32)
+        place = lax.rem(tables[0, which] + (count - count // 2), count)
+        layer = blocks[place].astype(F32)
         moved = pltpu.roll(layer, SLOT_ROWS - 1, 0)
         layer = jnp.where(tables[1, which] == 1, moved, layer)
         result.append(turned(layer, tables[2, which], tables[3, which] * tile_rows))
@@ -194,14 +201,16 @@
     second_sweep(rates, interior, ghosts, ends, inv_y, emit)
 
 
-def last_kernel(tile_rows, tables, rates, blocks, interior, ends, inv_y, planes):
+def last_kernel(tile_rows, tile0, tables, rates, blocks, interior, ends, inv_y, planes):
     sides = ghost_rows(tables, blocks, tile_rows)
     ghosts = [packed_ghosts(sides, field) for field in range(2)]
     cells = ends.shape[-1]
 
     def emit(field, start, chunk, values):
-        first = start // tile_rows
-        planes[first:first + chunk // tile_rows, field] = values.reshape(-1, tile_rows, cells)
+        count = planes.shape[0]
+        for row in range(0, chunk, tile_rows):
+            place = ((start + row) // tile_rows + count - tile0) % count
+            planes[place, field] = values[row:row + tile_rows]
 
     second_sweep(rates, interior, ghosts, ends, inv_y, emit)
 
@@ -217,6 +226,10 @@
     fields, depth, tile_rows, cells = magnet.shape
     lines = inv_y.shape[-1]
     count = lax.axis_size("blk")
+    width = lax.axis_size("pen")
+    tile0 = (width * 5) // 8
+    across = turned_group(count, count // 2)
+    within = turned_group(width, tile0)
     tables = jnp.concatenate([partner, face_side, orient, offset], axis=0)
     slots = jax.ShapeDtypeStruct((count, SLOT_ROWS, lines), BF16)
     packed = jax.ShapeDtypeStruct((fields, 16, lines), BF16)
@@ -224,7 +237,7 @@
     sweep_flops = 2 * fields * lines * cells * cells
     array_bytes = 2 * fields * lines * cells
 
-    moved = lax.all_to_all(to_planes(magnet), "pen", split_axis=0, concat_axis=0, tiled=True)
+    moved = lax.all_to_all(to_planes(magnet), "pen", split_axis=0, concat_axis=0, tiled=True, axis_index_groups=within)
     ends = pl.pallas_call(
         ends_kernel,
         out_shape=jax.ShapeDtypeStruct((fields, 16, cells), BF16),
@@ -235,7 +248,7 @@
         name="ends",
     )(inv_x)
     sent = pl.pallas_call(
-        layers_kernel,
+        functools.partial(layers_kernel, tile0),
         out_shape=slots,
         in_specs=[VMEM],
         out_specs=VMEM,
@@ -243,9 +256,9 @@
         cost_estimate=cost(sweep_flops // 16, array_bytes),
         name="layers",
     )(moved)
-    blocks = lax.all_to_all(sent, "blk", split_axis=0, concat_axis=0, tiled=True)
+    blocks = lax.all_to_all(sent, "blk", split_axis=0, concat_axis=0, tiled=True, axis_index_groups=across)
     interior, corners = pl.pallas_call(
-        interior_kernel,
+        functools.partial(interior_kernel, tile0),
         out_shape=(swept, jax.ShapeDtypeStruct((fields, 8, lines), F32)),
         in_specs=[VMEM, VMEM],
         out_specs=(VMEM, VMEM),
@@ -262,7 +275,7 @@
         cost_estimate=cost(sweep_flops // 16, array_bytes),
         name="next_layers",
     )(tables, rates, blocks, corners, ends, inv_y)
-    blocks = lax.all_to_all(sent, "blk", split_axis=0, concat_axis=0, tiled=True)
+    blocks = lax.all_to_all(sent, "blk", split_axis=0, concat_axis=0, tiled=True, axis_index_groups=across)
     interior = pl.pallas_call(
         middle_kernel,
         out_shape=swept,
@@ -273,7 +286,7 @@
         name="middle",
     )(rates, interior, ghosts, ends, inv_y, inv_x)
     planes = pl.pallas_call(
-        functools.partial(last_kernel, tile_rows),
+        functools.partial(last_kernel, tile_rows, tile0),
         out_shape=jax.ShapeDtypeStruct((lines // tile_rows, fields, tile_rows, cells), BF16),
         in_specs=[SMEM, SMEM, VMEM, VMEM, VMEM, VMEM],
         out_specs=VMEM,
@@ -281,7 +294,7 @@
         cost_estimate=cost(sweep_flops, 4 * array_bytes),
         name="last",
     )(tables, rates, blocks, interior, ends, inv_y)
-    back = lax.all_to_all(planes, "pen", split_axis=0, concat_axis=0, tiled=True)
+    back = lax.all_to_all(planes, "pen", split_axis=0, concat_axis=0, tiled=True, axis_index_groups=within)
     return from_planes(back)[None]
 
 

time: 109 us -> 102 us (0.936)
  waiting for transfers between devices: 16.1 us -> 3.51 us
  starting transfers between devices: 19.4 us -> 26.4 us
  blocking collectives: 51.6 us -> 50.2 us
    all_to_all x2, waiting for transfers between devices: 16.1 us -> 3.51 us  [local(): lax.all_to_all(sent, 'blk', split_axis=0, concat_axis=0, tiled=True, axis...]
    all_to_all x2, starting transfers between devices: 19.4 us -> 26.4 us  [local(): lax.all_to_all(sent, 'blk', split_axis=0, concat_axis=0, tiled=True, axis...]
    all_to_all x1, blocking collectives: 27.6 us -> 26.5 us  [local(): lax.all_to_all(to_planes(magnet), 'pen', split_axis=0, concat_axis=0, til...]
  transfers between devices with their start and end apart: 2 -> 2, of which waited for: 2 -> 2; matrix products, arithmetic and copies ran while one was open for 0% -> 0% of each run, Pallas kernels for 3% -> 4%
where the time goes in v3:
time: 102 us; the launch traced here: 101 us
  blocking collectives  50.2 us (49%)
  starting transfers between devices  26.4 us (26%)
  Pallas kernels  15 us (15%)
  local copies, waits for them, and re-layouts  5.87 us (6%)
  waiting for transfers between devices  3.51 us (3%)
    all_to_all x1, blocking collectives, local(): lax.all_to_all(to_planes(magnet), 'pen', split_axis=0, concat_axis=0, til...  26.5 us
    all_to_all x2, starting transfers between devices, local(): lax.all_to_all(sent, 'blk', split_axis=0, concat_axis=0, tiled=True, axis...  26.4 us
    all_to_all x1, blocking collectives, local(): lax.all_to_all(planes, 'pen', split_axis=0, concat_axis=0, tiled=True, ax...  23.7 us
    unnamed x22, local copies, waits for them, and re-layouts  5.87 us
    all_to_all x2, waiting for transfers between devices, local(): lax.all_to_all(sent, 'blk', split_axis=0, concat_axis=0, tiled=True, axis...  3.51 us
    pallas_call x1, Pallas kernels, to_planes(): pl.pallas_call(transpose_kernel, out_shape=jax.ShapeDtypeStruct((planes,...  3.36 us
    pallas_call x1, Pallas kernels, from_planes(): pl.pallas_call(untranspose_kernel, out_shape=jax.ShapeDtypeStruct((fields...  3.36 us
    pallas_call x1, Pallas kernels, local(): pl.pallas_call(middle_kernel, out_shape=swept, in_specs=[SMEM, VMEM, VMEM...  2.41 us
  transfers between devices with their start and end apart: 2, of which 2 were waited for; matrix products, arithmetic and copies ran while one was open for 0% of the time, Pallas kernels for 4%

profile of v3, /device:TPU:1, one launch (start us, length us, event | category | flops | bytes accessed | tf_op | source)
XLA Modules:
  0.0 101.1 jit_solution(17531602064008360017)
XLA Ops:
  0.0 3.4 %to_planes.1 = bf16[32,2,16,512]{3,2,1,0:T(8,128)(2,1)} custom-call(bf16[2,32,16,512]{3,2,1,0:T(8,128)(2,1)} %bitcast.10), custom_call_target="tpu_custom_call" | custom-call | tf_op jit(solution)/shard_map/to_planes/pallas_call | solution.py:45
  3.4 0.0 copy-start
  3.4 0.0 copy-start.7
  3.4 0.0 copy-start.8
  3.4 0.0 copy-start.9
  3.4 0.0 copy-start.10
  3.4 26.5 %all_to_all.20.planes = bf16[32,2,16,512]{3,2,1,0:T(8,128)(2,1)S(1)} all-to-all(bf16[32,2,16,512]{3,2,1,0:T(8,128)(2,1)} %to_planes.1), channel_id=1, replica_groups={{20,21,22,23,24,25,26,27,28,29,30,31,0,1,2,3,4,5,6,7,8,9,10,11,12,13,14..., dimensions={0} | all-to-all | bytes 2097152 | tf_op jit(solution)/shard_map/all_to_all | solution.py:240
  29.8 0.0 copy-start.1
  29.8 0.9 layers.1
  30.8 14.8 %all-to-all-start.1 = ((bf16[16,8,512]{2,1,0:T(8,128)(2,1)}), bf16[16,8,512]{2,1,0:T(8,128)(2,1)S(1)}, u32[]{:S(2)}, u32[]{:S(2)}) async-start(bf16[16,8,512]{2,1,0:T(8,128)(2,1)} %layers.1), calls=%async_computation.1 | async-start | bytes 262144 | tf_op jit(solution)/shard_map/all_to_all | solution.py:259
  45.6 0.0 copy-done
  45.6 0.4 ends.1
  45.9 0.0 copy-done.7
  45.9 0.0 copy-done.8
  46.0 0.0 copy-done.9
  46.0 0.0 copy-done.10
  46.0 1.0 interior.1
  47.0 1.3 %copy-done.4 = f32[2,512,512]{2,1,0:T(8,128)} copy-done((f32[2,512,512]{2,1,0:T(8,128)}, f32[2,512,512]{2,1,0:T(8,128)S(1)}, u32[]{:S(2)}) %copy-start.4) | copy-done | bytes 2097176
  48.3 3.3 %all-to-all-done.1.blocks = bf16[16,8,512]{2,1,0:T(8,128)(2,1)S(1)} async-done(((bf16[16,8,512]{2,1,0:T(8,128)(2,1)}), bf16[16,8,512]{2,1,0:T(8,128)(2,1)S(1)}, u32[]{:S(2)}, u32[]{:S(2)}) %all-to-all-start.1) | async-done | bytes 131104 | tf_op jit(solution)/shard_map/all_to_all | solution.py:259
  51.6 0.0 copy-done.1
  51.6 0.0 copy-done.6
  51.6 1.7 %next_layers.1 = (bf16[16,8,512]{2,1,0:T(8,128)(2,1)}, bf16[2,16,512]{2,1,0:T(8,128)(2,1)S(1)}) custom-call(s32[4,2]{1,0:T(4,128)S(1)} %pad_add_fusion.tables, f32[1,3]{1,0:T(1,128)S(1)} %copy-done.6, bf16[16,8,512]{2,1,0:T(8,128)(2,1)S(1)} %all-to-all-done.1.blocks, f32[2,8,512]{2,1,0:T(8,128)S(1)} %get-tuple-element.9.corners, ...), custom_call_target="tpu_custom_call" | custom-call | flops 33554432 | bytes 1048576 | tf_op jit(solution)/shard_map/next_layers/pallas_call | solution.py:269
  53.3 11.6 %all-to-all-start.2 = ((bf16[16,8,512]{2,1,0:T(8,128)(2,1)}), bf16[16,8,512]{2,1,0:T(8,128)(2,1)S(1)}, u32[]{:S(2)}, u32[]{:S(2)}) async-start(bf16[16,8,512]{2,1,0:T(8,128)(2,1)} %get-tuple-element.10), calls=%async_computation.2 | async-start | bytes 262144 | tf_op jit(solution)/shard_map/all_to_all | solution.py:278
  64.9 1.6 %copy-done.5 = f32[2,512,512]{2,1,0:T(8,128)S(1)} copy-done((f32[2,512,512]{2,1,0:T(8,128)S(1)}, f32[2,512,512]{2,1,0:T(8,128)}, u32[]{:S(2)}) %copy-start.5) | copy-done | bytes 2097176
  66.5 2.4 %middle.1.interior = f32[2,512,512]{2,1,0:T(8,128)S(1)} custom-call(f32[1,3]{1,0:T(1,128)S(1)} %copy-done.6, f32[2,512,512]{2,1,0:T(8,128)S(1)} %copy-done.5, bf16[2,16,512]{2,1,0:T(8,128)(2,1)S(1)} %get-tuple-element.12.ghosts, bf16[2,16,512]{2,1,0:T(8,128)(2,1)S(1)} %ends.1, bf16[2,512,512]{2,1,0:T(8,128)(2,1)S(1)} %bitcast.8, bf16[2,512,512]{2,1,0:T(8,128)(2,1)S(1)} %bitcast.6), custom_call_target="tpu_custom_call" | custom-call | flops 1073741824 | bytes 6291456 | tf_op jit(solution)/shard_map/middle/pallas_call | solution.py:279
  68.9 0.0 copy-start.2
  68.9 1.3 %copy-done.2 = f32[2,512,512]{2,1,0:T(8,128)} copy-done((f32[2,512,512]{2,1,0:T(8,128)}, f32[2,512,512]{2,1,0:T(8,128)S(1)}, u32[]{:S(2)}) %copy-start.2) | copy-done | bytes 2097176
  70.3 0.2 all-to-all-done.2.blocks
  70.5 1.6 %copy-done.3 = f32[2,512,512]{2,1,0:T(8,128)S(1)} copy-done((f32[2,512,512]{2,1,0:T(8,128)S(1)}, f32[2,512,512]{2,1,0:T(8,128)}, u32[]{:S(2)}) %copy-start.3) | copy-done | bytes 2097176
  72.1 1.9 %last.1 = bf16[32,2,16,512]{3,2,1,0:T(8,128)(2,1)S(1)} custom-call(s32[4,2]{1,0:T(4,128)S(1)} %pad_add_fusion.tables, f32[1,3]{1,0:T(1,128)S(1)} %copy-done.6, bf16[16,8,512]{2,1,0:T(8,128)(2,1)S(1)} %all-to-all-done.2.blocks, f32[2,512,512]{2,1,0:T(8,128)S(1)} %copy-done.3, bf16[2,16,512]{2,1,0:T(8,128)(2,1)S(1)} %ends.1, bf16[2,512,512]{2,1,0:T(8,128)(2,1)S(1)} %bitcast.9), custom_call_target="tpu_custom_call" | custom-call | flops 536870912 | bytes 4194304 | tf_op jit(solution)/shard_map/last/pallas_call | solution.py:288
  74.0 23.7 %all_to_all.21.source = bf16[32,2,16,512]{3,2,1,0:T(8,128)(2,1)} all-to-all(bf16[32,2,16,512]{3,2,1,0:T(8,128)(2,1)S(1)} %last.1), channel_id=1, replica_groups={{20,21,22,23,24,25,26,27,28,29,30,31,0,1,2,3,4,5,6,7,8,9,10,11,12,13,14..., dimensions={0} | all-to-all | bytes 2097152 | tf_op jit(solution)/shard_map/all_to_all | solution.py:297
  97.7 3.4 %from_planes.1 = bf16[2,32,16,512]{3,2,1,0:T(8,128)(2,1)} custom-call(bf16[32,2,16,512]{3,2,1,0:T(8,128)(2,1)} %all_to_all.21.source), custom_call_target="tpu_custom_call" | custom-call | tf_op jit(solution)/shard_map/from_planes/pallas_call | solution.py:58
  (5 shorter events, 0.0 us)
Async XLA Ops:
  3.4 42.2 %copy-start = (bf16[1,2,512,512]{3,2,1,0:T(8,128)(2,1)S(1)}, bf16[1,2,512,512]{3,2,1,0:T(8,128)(2,1)}, u32[]{:S(2)}) copy-start(bf16[1,2,512,512]{3,2,1,0:T(8,128)(2,1)} %param.9) | copy-start | bytes 3145732
  3.4 42.6 %copy-start.7 = (s32[1,2]{1,0:T(1,128)S(1)}, s32[1,2]{1,0:T(1,128)}, u32[]{:S(2)}) copy-start(s32[1,2]{1,0:T(1,128)} %param.15) | copy-start | bytes 28
  3.4 42.6 %copy-start.8 = (s32[1,2]{1,0:T(1,128)S(1)}, s32[1,2]{1,0:T(1,128)}, u32[]{:S(2)}) copy-start(s32[1,2]{1,0:T(1,128)} %param.14) | copy-start | bytes 28
  3.4 42.6 %copy-start.9 = (s32[1,2]{1,0:T(1,128)S(1)}, s32[1,2]{1,0:T(1,128)}, u32[]{:S(2)}) copy-start(s32[1,2]{1,0:T(1,128)} %param.13) | copy-start | bytes 28
  3.4 42.6 %copy-start.10 = (s32[1,2]{1,0:T(1,128)S(1)}, s32[1,2]{1,0:T(1,128)}, u32[]{:S(2)}) copy-start(s32[1,2]{1,0:T(1,128)} %param.12) | copy-start | bytes 28
  29.8 21.7 %copy-start.1 = (bf16[1,2,512,512]{3,2,1,0:T(8,128)(2,1)S(1)}, bf16[1,2,512,512]{3,2,1,0:T(8,128)(2,1)}, u32[]{:S(2)}) copy-start(bf16[1,2,512,512]{3,2,1,0:T(8,128)(2,1)} %param.10) | copy-start | bytes 3145732
  29.8 21.7 %copy-start.6 = (f32[1,3]{1,0:T(1,128)S(1)}, f32[1,3]{1,0:T(1,128)}, u32[]{:S(2)}) copy-start(f32[1,3]{1,0:T(1,128)} %rates.5) | copy-start | bytes 40
  30.8 20.8 %all-to-all-start.1 = ((bf16[16,8,512]{2,1,0:T(8,128)(2,1)}), bf16[16,8,512]{2,1,0:T(8,128)(2,1)S(1)}, u32[]{:S(2)}, u32[]{:S(2)}) async-start(bf16[16,8,512]{2,1,0:T(8,128)(2,1)} %layers.1), calls=%async_computation.1 | async-start | bytes 262144 | tf_op jit(solution)/shard_map/all_to_all | solution.py:259
  47.0 1.3 %copy-start.4 = (f32[2,512,512]{2,1,0:T(8,128)}, f32[2,512,512]{2,1,0:T(8,128)S(1)}, u32[]{:S(2)}) copy-start(f32[2,512,512]{2,1,0:T(8,128)S(1)} %get-tuple-element.11.interior) | copy-start | bytes 6291460
  53.3 17.2 %all-to-all-start.2 = ((bf16[16,8,512]{2,1,0:T(8,128)(2,1)}), bf16[16,8,512]{2,1,0:T(8,128)(2,1)S(1)}, u32[]{:S(2)}, u32[]{:S(2)}) async-start(bf16[16,8,512]{2,1,0:T(8,128)(2,1)} %get-tuple-element.10), calls=%async_computation.2 | async-start | bytes 262144 | tf_op jit(solution)/shard_map/all_to_all | solution.py:278
  64.9 1.6 %copy-start.5 = (f32[2,512,512]{2,1,0:T(8,128)S(1)}, f32[2,512,512]{2,1,0:T(8,128)}, u32[]{:S(2)}) copy-start(f32[2,512,512]{2,1,0:T(8,128)} %copy-done.4) | copy-start | bytes 6291460
  68.9 1.3 %copy-start.2 = (f32[2,512,512]{2,1,0:T(8,128)}, f32[2,512,512]{2,1,0:T(8,128)S(1)}, u32[]{:S(2)}) copy-start(f32[2,512,512]{2,1,0:T(8,128)S(1)} %middle.1.interior) | copy-start | bytes 6291460
  70.5 1.6 %copy-start.3 = (f32[2,512,512]{2,1,0:T(8,128)S(1)}, f32[2,512,512]{2,1,0:T(8,128)}, u32[]{:S(2)}) copy-start(f32[2,512,512]{2,1,0:T(8,128)} %copy-done.2) | copy-start | bytes 6291460

commit v4 on v3

--- a/solution.py
+++ b/solution.py
@@ -8,10 +8,11 @@
 from jax.sharding import PartitionSpec as P
 
 STEPS = 2
-SLOT_ROWS = 8
+SLOT_ROWS = 4
 F32 = jnp.float32
 BF16 = jnp.bfloat16
 VMEM = pl.BlockSpec(memory_space=pltpu.VMEM)
+HBM = pl.BlockSpec(memory_space=pltpu.HBM)
 SMEM = pl.BlockSpec(memory_space=pltpu.SMEM)
 NT = (((1,), (1,)), ((), ()))
 TN = (((0,), (0,)), ((), ()))
@@ -22,45 +23,63 @@
 
 
 def params():
-    return pltpu.CompilerParams(vmem_limit_bytes=32 * 1024 * 1024)
+    return pltpu.CompilerParams(vmem_limit_bytes=16 * 1024 * 1024)
 
 
 def rows_of(shape):
     return lax.broadcasted_iota(jnp.int32, shape, 0)
 
 
-def transpose_kernel(source, target):
-    for field in range(2):
-        target[:, field] = source[field]
-
-
-def untranspose_kernel(source, target):
-    for field in range(2):
-        target[field] = source[:, field]
+def transfer(pairs, sems):
+    copies = [
+        pltpu.make_async_copy(source, target, sems.at[number])
+        for number, (source, target) in enumerate(pairs)
+    ]
+    for copy in copies:
+        copy.start()
+    for copy in copies:
+        copy.wait()
+
+
+def pieces_of(by_field, by_plane, parts):
+    chunk = by_plane.shape[0] // parts
+    return [
+        (by_field.at[field, pl.ds(part * chunk, chunk)], by_plane.at[pl.ds(part * chunk, chunk), field])
+        for part in range(parts)
+        for field in range(2)
+    ]
+
+
+def to_planes_kernel(source, target, sems):
+    transfer(pieces_of(source, target, 4), sems)
+
+
+def from_planes_kernel(source, target, sems):
+    transfer([(held, sent) for sent, held in pieces_of(target, source, 4)], sems)
 
 
 def to_planes(state):
     fields, planes, lines, cells = state.shape
-    chunk = planes // 4
     return pl.pallas_call(
-        transpose_kernel,
+        to_planes_kernel,
         out_shape=jax.ShapeDtypeStruct((planes, fields, lines, cells), BF16),
-        grid=(4,),
-        in_specs=[pl.BlockSpec((fields, chunk, lines, cells), lambda i: (0, i, 0, 0))],
-        out_specs=pl.BlockSpec((chunk, fields, lines, cells), lambda i: (i, 0, 0, 0)),
+        in_specs=[HBM],
+        out_specs=VMEM,
+        scratch_shapes=[pltpu.SemaphoreType.DMA((8,))],
+        compiler_params=params(),
         name="to_planes",
     )(state)
 
 
 def from_planes(moved):
     planes, fields, lines, cells = moved.shape
-    chunk = planes // 4
     return pl.pallas_call(
-        untranspose_kernel,
+        from_planes_kernel,
         out_shape=jax.ShapeDtypeStruct((fields, planes, lines, cells), BF16),
-        grid=(4,),
-        in_specs=[pl.BlockSpec((chunk, fields, lines, cells), lambda i: (i, 0, 0, 0))],
-        out_specs=pl.BlockSpec((fields, chunk, lines, cells), lambda i: (0, i, 0, 0)),
+        in_specs=[VMEM],
+        out_specs=HBM,
+        scratch_shapes=[pltpu.SemaphoreType.DMA((8,))],
+        compiler_params=params(),
         name="from_planes",
     )(moved)
 
@@ -84,8 +103,8 @@
 def layers_kernel(first, planes, sent):
     cells = planes.shape[-1]
     total = None
-    lane = lax.broadcasted_iota(jnp.int32, (SLOT_ROWS, 128), 1)
-    row = rows_of((SLOT_ROWS, 128))
+    lane = lax.broadcasted_iota(jnp.int32, (16, 128), 1)
+    row = rows_of((16, 128))
     for field in range(2):
         for end in range(2):
             pick = (row == field * 2 + end) & (lane == end * 127)
@@ -94,7 +113,7 @@
             edge = in_order(planes[:, field, :, start:start + 128], first)
             part = lax.dot_general(pick, edge, NT, preferred_element_type=F32)
             total = part if total is None else total + part
-    total = total.astype(BF16)
+    total = total[0:SLOT_ROWS].astype(BF16)
     for slot in range(sent.shape[0]):
         sent[slot] = total
 
@@ -105,7 +124,7 @@
     for field in range(2):
         plane = in_order(planes[:, field], tile0)
         weights = inv_x[field]
-        interior[field] = lax.dot_general(plane, weights, NT, preferred_element_type=F32)
+        interior[field] = lax.dot_general(plane, weights, NT, preferred_element_type=F32).astype(BF16)
         first = weights[0:16].astype(F32)[0:1]
         last = weights[cells - 16:cells].astype(F32)[15:16]
         two = jnp.where(row == 0, first, jnp.where(row == 1, last, 0.0)).astype(BF16)
@@ -123,24 +142,26 @@
     return jnp.where(orient == 1, jnp.concatenate(pieces, axis=1), layer)
 
 
-def ghost_rows(tables, blocks, tile_rows):
+def ghost_rows(tables, blocks, origin, tile_rows):
     result = []
-    count = blocks.shape[0]
+    count, _, lines = blocks.shape
+    row = rows_of((8, lines))
     for which in range(2):
-        place = lax.rem(tables[0, which] + (count - count // 2), count)
+        place = lax.rem(tables[0, which] + (count - origin), count)
         layer = blocks[place].astype(F32)
-        moved = pltpu.roll(layer, SLOT_ROWS - 1, 0)
-        layer = jnp.where(tables[1, which] == 1, moved, layer)
-        result.append(turned(layer, tables[2, which], tables[3, which] * tile_rows))
+        far = tables[1, which] == 1
+        proton = jnp.where(far, layer[1:2], layer[0:1])
+        carbon = jnp.where(far, layer[3:4], layer[2:3])
+        both = jnp.where(row == 0, proton, carbon)
+        result.append(turned(both, tables[2, which], tables[3, which] * tile_rows))
     return result
 
 
 def packed_ghosts(sides, field):
     cells = sides[0].shape[-1]
     row = rows_of((16, cells))
-    at = field * 2
-    low = sides[0][at:at + 1]
-    high = sides[1][at:at + 1]
+    low = sides[0][field:field + 1]
+    high = sides[1][field:field + 1]
     return jnp.where(row == 0, low, jnp.where(row == 1, high, 0.0)).astype(BF16)
 
 
@@ -150,13 +171,12 @@
     return new_proton, new_carbon
 
 
-def next_layers_kernel(tile_rows, tables, rates, blocks, corners, ends, inv_y, sent, ghosts):
+def next_layers_kernel(tile_rows, origin, tables, rates, blocks, corners, ends, inv_y, sent, ghosts):
     cells = ends.shape[-1]
-    sides = ghost_rows(tables, blocks, tile_rows)
+    sides = ghost_rows(tables, blocks, origin, tile_rows)
     row = rows_of((16, cells))
     swept = []
     for field in range(2):
-        at = field * 2
         edge = ends[field].astype(F32)
         ghosts[field] = packed_ghosts(sides, field)
         found = []
@@ -164,13 +184,13 @@
             lane = end * (cells - 1)
             value = corners[field][end:end + 1]
             for which in range(2):
-                value = value + edge[which:which + 1, lane:lane + 1] * sides[which][at:at + 1]
+                value = value + edge[which:which + 1, lane:lane + 1] * sides[which][field:field + 1]
             found.append(value)
         two = jnp.where(row == 0, found[0], jnp.where(row == 1, found[1], 0.0)).astype(BF16)
         swept.append(lax.dot_general(two, inv_y[field], NT, preferred_element_type=F32)[0:8])
     new_proton, new_carbon = mix(rates, swept[0], swept[1])
     row8 = rows_of(new_proton.shape)
-    total = jnp.where(row8 < 2, new_proton, pltpu.roll(new_carbon, 2, 0)).astype(BF16)
+    total = jnp.where(row8 < 2, new_proton, pltpu.roll(new_carbon, 2, 0))[0:SLOT_ROWS].astype(BF16)
     for slot in range(sent.shape[0]):
         sent[slot] = total
 
@@ -180,7 +200,7 @@
     swept = []
     for field in range(2):
         outer = lax.dot_general(ghosts[field], ends[field], TN, preferred_element_type=F32)
-        swept.append((interior[field] + outer).astype(BF16))
+        swept.append((interior[field].astype(F32) + outer).astype(BF16))
     chunk = lines // 2
     for start in range(0, lines, chunk):
         moved = [
@@ -192,17 +212,22 @@
             emit(field, start, chunk, new[field].astype(BF16))
 
 
-def middle_kernel(rates, interior, ghosts, ends, inv_y, inv_x, following):
+def middle_kernel(rates, interior, ghosts, ends, inv_y, far_x, following, inv_x, sem):
+    fetch = pltpu.make_async_copy(far_x, inv_x, sem)
+    fetch.start()
+
     def emit(field, start, chunk, values):
+        if start == 0 and field == 0:
+            fetch.wait()
         following[field, start:start + chunk] = lax.dot_general(
             values, inv_x[field], NT, preferred_element_type=F32
-        )
+        ).astype(BF16)
 
     second_sweep(rates, interior, ghosts, ends, inv_y, emit)
 
 
-def last_kernel(tile_rows, tile0, tables, rates, blocks, interior, ends, inv_y, planes):
-    sides = ghost_rows(tables, blocks, tile_rows)
+def last_kernel(tile_rows, tile0, origin, tables, rates, blocks, interior, ends, inv_y, planes):
+    sides = ghost_rows(tables, blocks, origin, tile_rows)
     ghosts = [packed_ghosts(sides, field) for field in range(2)]
     cells = ends.shape[-1]
 
@@ -228,12 +253,13 @@
     count = lax.axis_size("blk")
     width = lax.axis_size("pen")
     tile0 = (width * 5) // 8
-    across = turned_group(count, count // 2)
+    origin = (count * 5) // 8
+    across = turned_group(count, origin)
     within = turned_group(width, tile0)
     tables = jnp.concatenate([partner, face_side, orient, offset], axis=0)
     slots = jax.ShapeDtypeStruct((count, SLOT_ROWS, lines), BF16)
     packed = jax.ShapeDtypeStruct((fields, 16, lines), BF16)
-    swept = jax.ShapeDtypeStruct((fields, lines, cells), F32)
+    swept = jax.ShapeDtypeStruct((fields, lines, cells), BF16)
     sweep_flops = 2 * fields * lines * cells * cells
     array_bytes = 2 * fields * lines * cells
 
@@ -267,7 +293,7 @@
         name="interior",
     )(moved, inv_x)
     sent, ghosts = pl.pallas_call(
-        functools.partial(next_layers_kernel, tile_rows),
+        functools.partial(next_layers_kernel, tile_rows, origin),
         out_shape=(slots, packed),
         in_specs=[SMEM, SMEM, VMEM, VMEM, VMEM, VMEM],
         out_specs=(VMEM, VMEM),
@@ -279,14 +305,15 @@
     interior = pl.pallas_call(
         middle_kernel,
         out_shape=swept,
-        in_specs=[SMEM, VMEM, VMEM, VMEM, VMEM, VMEM],
-        out_specs=VMEM,
+        in_specs=[SMEM, VMEM, VMEM, VMEM, VMEM, HBM],
+        out_specs=VMEM,
+        scratch_shapes=[pltpu.VMEM(inv_x.shape, BF16), pltpu.SemaphoreType.DMA],
         compiler_params=params(),
         cost_estimate=cost(2 * sweep_flops, 6 * array_bytes),
         name="middle",
     )(rates, interior, ghosts, ends, inv_y, inv_x)
     planes = pl.pallas_call(
-        functools.partial(last_kernel, tile_rows, tile0),
+        functools.partial(last_kernel, tile_rows, tile0, origin),
         out_shape=jax.ShapeDtypeStruct((lines // tile_rows, fields, tile_rows, cells), BF16),
         in_specs=[SMEM, SMEM, VMEM, VMEM, VMEM, VMEM],
         out_specs=VMEM,

time: 102 us -> 89.9 us (0.88)
  Pallas kernels: 15 us -> 9.59 us
  starting transfers between devices: 26.4 us -> 22.8 us
  local copies, waits for them, and re-layouts: 5.87 us -> 4.38 us
    pallas_call x4, Pallas kernels: 10.3 us -> 4.82 us  [the longest x1 1.86 us: local(): pl.pallas_call(functools.partial(last_kernel, tile_rows, tile0, origin),...]
    all_to_all x2, starting transfers between devices: 26.4 us -> 22.8 us  [local(): lax.all_to_all(sent, 'blk', split_axis=0, concat_axis=0, tiled=True, axis...]
    unnamed x22 -> x20, local copies, waits for them, and re-layouts: 5.87 us -> 4.38 us
where the time goes in v4:
time: 89.9 us; the launch traced here: 89.5 us
  blocking collectives  49.3 us (55%)
  starting transfers between devices  22.8 us (25%)
  Pallas kernels  9.59 us (11%)
  local copies, waits for them, and re-layouts  4.38 us (5%)
  waiting for transfers between devices  3.33 us (4%)
    all_to_all x1, blocking collectives, local(): lax.all_to_all(to_planes(magnet), 'pen', split_axis=0, concat_axis=0, til...  26.1 us
    all_to_all x1, blocking collectives, local(): lax.all_to_all(planes, 'pen', split_axis=0, concat_axis=0, tiled=True, ax...  23.2 us
    all_to_all x2, starting transfers between devices, local(): lax.all_to_all(sent, 'blk', split_axis=0, concat_axis=0, tiled=True, axis...  22.8 us
    unnamed x20, local copies, waits for them, and re-layouts  4.38 us
    all_to_all x2, waiting for transfers between devices, local(): lax.all_to_all(sent, 'blk', split_axis=0, concat_axis=0, tiled=True, axis...  3.33 us
    pallas_call x1, Pallas kernels, local(): pl.pallas_call(middle_kernel, out_shape=swept, in_specs=[SMEM, VMEM, VMEM...  2.56 us
    pallas_call x1, Pallas kernels, local(): pl.pallas_call(functools.partial(last_kernel, tile_rows, tile0, origin),...  1.86 us
  transfers between devices with their start and end apart: 2, of which 2 were waited for; matrix products, arithmetic and copies ran while one was open for 0% of the time, Pallas kernels for 4%

profile of v4, /device:TPU:1, one launch (start us, length us, event | category | flops | bytes accessed | tf_op | source)
XLA Modules:
  0.0 89.5 jit_solution(239709783585388062)
XLA Ops:
  0.0 0.0 copy-start.4
  0.0 1.2 %copy-done.4 = bf16[1,2,32,16,512]{4,3,2,1,0:T(8,128)(2,1)S(1)} copy-done((bf16[1,2,32,16,512]{4,3,2,1,0:T(8,128)(2,1)S(1)}, bf16[1,2,32,16,512]{4,3,2,1,0:T(8,128)(2,1)}, u32[]{:S(2)}) %copy-start.4) | copy-done | bytes 1048600
  1.2 0.3 to_planes.1
  1.5 26.1 %all_to_all.20.planes = bf16[32,2,16,512]{3,2,1,0:T(8,128)(2,1)S(1)} all-to-all(bf16[32,2,16,512]{3,2,1,0:T(8,128)(2,1)S(1)} %to_planes.1), channel_id=1, replica_groups={{20,21,22,23,24,25,26,27,28,29,30,31,0,1,2,3,4,5,6,7,8,9,10,11,12,13,14..., dimensions={0} | all-to-all | bytes 2097152 | tf_op jit(solution)/shard_map/all_to_all | solution.py:266
  27.6 0.0 copy-start.1
  27.6 0.9 layers.1
  28.5 12.8 %all-to-all-start.1 = ((bf16[16,4,512]{2,1,0:T(4,128)(2,1)}), bf16[16,4,512]{2,1,0:T(4,128)(2,1)S(1)}, u32[]{:S(2)}, u32[]{:S(2)}) async-start(bf16[16,4,512]{2,1,0:T(4,128)(2,1)} %layers.1), calls=%async_computation.1 | async-start | bytes 131072 | tf_op jit(solution)/shard_map/all_to_all | solution.py:285
  41.2 0.0 copy-done.1
  41.2 0.0 copy-start.6
  41.3 0.0 copy-start.7
  41.3 0.0 copy-start.8
  41.3 0.0 copy-start.9
  41.3 0.4 ends.1
  41.7 0.2 copy-done.6
  41.9 0.0 copy-done.7
  41.9 0.0 copy-done.8
  41.9 0.0 copy-done.9
  42.0 0.0 copy-start
  42.0 1.0 %interior.1 = (bf16[2,512,512]{2,1,0:T(8,128)(2,1)S(1)}, f32[2,8,512]{2,1,0:T(8,128)S(1)}) custom-call(bf16[32,2,16,512]{3,2,1,0:T(8,128)(2,1)S(1)} %all_to_all.20.planes, bf16[2,512,512]{2,1,0:T(8,128)(2,1)S(1)} %bitcast.8), custom_call_target="tpu_custom_call" | custom-call | flops 536870912 | bytes 4194304 | tf_op jit(solution)/shard_map/interior/pallas_call | solution.py:286
  42.9 0.0 copy-start.2
  42.9 1.0 %copy-done.2 = bf16[2,512,512]{2,1,0:T(8,128)(2,1)} copy-done((bf16[2,512,512]{2,1,0:T(8,128)(2,1)}, bf16[2,512,512]{2,1,0:T(8,128)(2,1)S(1)}, u32[]{:S(2)}) %copy-start.2) | copy-done | bytes 1048600
  43.9 2.2 %all-to-all-done.1.blocks = bf16[16,4,512]{2,1,0:T(4,128)(2,1)S(1)} async-done(((bf16[16,4,512]{2,1,0:T(4,128)(2,1)}), bf16[16,4,512]{2,1,0:T(4,128)(2,1)S(1)}, u32[]{:S(2)}, u32[]{:S(2)}) %all-to-all-start.1) | async-done | bytes 65568 | tf_op jit(solution)/shard_map/all_to_all | solution.py:285
  46.1 0.0 copy-done
  46.1 0.7 copy-done.5
  46.8 1.7 %next_layers.1 = (bf16[16,4,512]{2,1,0:T(4,128)(2,1)}, bf16[2,16,512]{2,1,0:T(8,128)(2,1)S(1)}) custom-call(s32[4,2]{1,0:T(4,128)S(1)} %pad_add_fusion.tables, f32[1,3]{1,0:T(1,128)S(1)} %copy-done.5, bf16[16,4,512]{2,1,0:T(4,128)(2,1)S(1)} %all-to-all-done.1.blocks, f32[2,8,512]{2,1,0:T(8,128)S(1)} %get-tuple-element.9.corners, ...), custom_call_target="tpu_custom_call" | custom-call | flops 33554432 | bytes 1048576 | tf_op jit(solution)/shard_map/next_layers/pallas_call | solution.py:295
  48.5 10.1 %all-to-all-start.2 = ((bf16[16,4,512]{2,1,0:T(4,128)(2,1)}), bf16[16,4,512]{2,1,0:T(4,128)(2,1)S(1)}, u32[]{:S(2)}, u32[]{:S(2)}) async-start(bf16[16,4,512]{2,1,0:T(4,128)(2,1)} %get-tuple-element.10), calls=%async_computation.2 | async-start | bytes 131072 | tf_op jit(solution)/shard_map/all_to_all | solution.py:304
  58.6 1.2 %copy-done.3 = bf16[2,512,512]{2,1,0:T(8,128)(2,1)S(1)} copy-done((bf16[2,512,512]{2,1,0:T(8,128)(2,1)S(1)}, bf16[2,512,512]{2,1,0:T(8,128)(2,1)}, u32[]{:S(2)}) %copy-start.3) | copy-done | bytes 1048600
  59.8 2.6 %middle.1.interior = bf16[2,512,512]{2,1,0:T(8,128)(2,1)S(1)} custom-call(f32[1,3]{1,0:T(1,128)S(1)} %copy-done.5, bf16[2,512,512]{2,1,0:T(8,128)(2,1)S(1)} %copy-done.3, bf16[2,16,512]{2,1,0:T(8,128)(2,1)S(1)} %get-tuple-element.12.ghosts, bf16[2,16,512]{2,1,0:T(8,128)(2,1)S(1)} %ends.1, bf16[2,512,512]{2,1,0:T(8,128)(2,1)S(1)} %bitcast.5, ...), custom_call_target="tpu_custom_call" | custom-call | flops 1073741824 | bytes 6291456 | tf_op jit(solution)/shard_map/middle/pallas_call | solution.py:305
  62.4 1.1 %all-to-all-done.2.blocks = bf16[16,4,512]{2,1,0:T(4,128)(2,1)S(1)} async-done(((bf16[16,4,512]{2,1,0:T(4,128)(2,1)}), bf16[16,4,512]{2,1,0:T(4,128)(2,1)S(1)}, u32[]{:S(2)}, u32[]{:S(2)}) %all-to-all-start.2) | async-done | bytes 65568 | tf_op jit(solution)/shard_map/all_to_all | solution.py:304
  63.5 1.9 %last.1 = bf16[32,2,16,512]{3,2,1,0:T(8,128)(2,1)S(1)} custom-call(s32[4,2]{1,0:T(4,128)S(1)} %pad_add_fusion.tables, f32[1,3]{1,0:T(1,128)S(1)} %copy-done.5, bf16[16,4,512]{2,1,0:T(4,128)(2,1)S(1)} %all-to-all-done.2.blocks, bf16[2,512,512]{2,1,0:T(8,128)(2,1)S(1)} %middle.1.interior, bf16[2,16,512]{2,1,0:T(8,128)(2,1)S(1)} %ends.1, ...), custom_call_target="tpu_custom_call" | custom-call | flops 536870912 | bytes 4194304 | tf_op jit(solution)/shard_map/last/pallas_call | solution.py:315
  65.3 23.2 %all_to_all.21.source = bf16[32,2,16,512]{3,2,1,0:T(8,128)(2,1)S(1)} all-to-all(bf16[32,2,16,512]{3,2,1,0:T(8,128)(2,1)S(1)} %last.1), channel_id=1, replica_groups={{20,21,22,23,24,25,26,27,28,29,30,31,0,1,2,3,4,5,6,7,8,9,10,11,12,13,14..., dimensions={0} | all-to-all | bytes 2097152 | tf_op jit(solution)/shard_map/all_to_all | solution.py:324
  88.5 1.0 %from_planes.1 = bf16[2,32,16,512]{3,2,1,0:T(8,128)(2,1)} custom-call(bf16[32,2,16,512]{3,2,1,0:T(8,128)(2,1)S(1)} %all_to_all.21.source), custom_call_target="tpu_custom_call" | custom-call | tf_op jit(solution)/shard_map/from_planes/pallas_call | solution.py:76
  (3 shorter events, 0.0 us)
Async XLA Ops:
  0.0 1.2 %copy-start.4 = (bf16[1,2,32,16,512]{4,3,2,1,0:T(8,128)(2,1)S(1)}, bf16[1,2,32,16,512]{4,3,2,1,0:T(8,128)(2,1)}, u32[]{:S(2)}) copy-start(bf16[1,2,32,16,512]{4,3,2,1,0:T(8,128)(2,1)} %param.8) | copy-start | bytes 3145732
  27.6 13.6 %copy-start.1 = (bf16[1,2,512,512]{3,2,1,0:T(8,128)(2,1)S(1)}, bf16[1,2,512,512]{3,2,1,0:T(8,128)(2,1)}, u32[]{:S(2)}) copy-start(bf16[1,2,512,512]{3,2,1,0:T(8,128)(2,1)} %param.9) | copy-start | bytes 3145732
  28.5 17.6 %all-to-all-start.1 = ((bf16[16,4,512]{2,1,0:T(4,128)(2,1)}), bf16[16,4,512]{2,1,0:T(4,128)(2,1)S(1)}, u32[]{:S(2)}, u32[]{:S(2)}) async-start(bf16[16,4,512]{2,1,0:T(4,128)(2,1)} %layers.1), calls=%async_computation.1 | async-start | bytes 131072 | tf_op jit(solution)/shard_map/all_to_all | solution.py:285
  41.2 0.7 copy-start.6
  41.3 0.7 copy-start.7
  41.3 0.7 copy-start.8
  41.3 0.7 copy-start.9
  42.0 4.2 %copy-start = (bf16[1,2,512,512]{3,2,1,0:T(8,128)(2,1)S(1)}, bf16[1,2,512,512]{3,2,1,0:T(8,128)(2,1)}, u32[]{:S(2)}) copy-start(bf16[1,2,512,512]{3,2,1,0:T(8,128)(2,1)} %param.10) | copy-start | bytes 3145732
  42.9 1.0 %copy-start.2 = (bf16[2,512,512]{2,1,0:T(8,128)(2,1)}, bf16[2,512,512]{2,1,0:T(8,128)(2,1)S(1)}, u32[]{:S(2)}) copy-start(bf16[2,512,512]{2,1,0:T(8,128)(2,1)S(1)} %get-tuple-element.11.interior) | copy-start | bytes 3145732
  46.1 0.7 copy-start.5
  48.5 15.0 %all-to-all-start.2 = ((bf16[16,4,512]{2,1,0:T(4,128)(2,1)}), bf16[16,4,512]{2,1,0:T(4,128)(2,1)S(1)}, u32[]{:S(2)}, u32[]{:S(2)}) async-start(bf16[16,4,512]{2,1,0:T(4,128)(2,1)} %get-tuple-element.10), calls=%async_computation.2 | async-start | bytes 131072 | tf_op jit(solution)/shard_map/all_to_all | solution.py:304
  58.6 1.2 %copy-start.3 = (bf16[2,512,512]{2,1,0:T(8,128)(2,1)S(1)}, bf16[2,512,512]{2,1,0:T(8,128)(2,1)}, u32[]{:S(2)}) copy-start(bf16[2,512,512]{2,1,0:T(8,128)(2,1)} %copy-done.2) | copy-start | bytes 3145732

commit v5 on v4

--- a/solution.py
+++ b/solution.py
@@ -90,7 +90,16 @@
     return ordered.reshape(-1, tiles.shape[-1])
 
 
-def ends_kernel(inv_x, ends):
+def table_rows(lines, tile_rows):
+    bits = (lines // tile_rows).bit_length() - 1
+    names = ["proton", "carbon", "cross"]
+    for which in range(2):
+        names += [("place", which), ("far", which), ("turn", which)]
+        names += [("bit", which, bit) for bit in range(bits)]
+    return names
+
+
+def prepare_kernel(tile_rows, origin, count, tables, rates, inv_x, ends, consts):
     cells = inv_x.shape[-1]
     lane = lax.broadcasted_iota(jnp.int32, (16, cells), 1)
     row = rows_of((16, cells))
@@ -98,6 +107,19 @@
     pick = jnp.where(pick, 1.0, 0.0).astype(BF16)
     for field in range(2):
         ends[field] = lax.dot_general(pick, inv_x[field], NT, preferred_element_type=F32).astype(BF16)
+    values = [rates[0, number] for number in range(3)]
+    for which in range(2):
+        place = lax.rem(tables[0, which] + (count - origin), count)
+        numbers = [place, tables[1, which], tables[2, which]]
+        bits = len(table_rows(cells, tile_rows)) // 2 - 4
+        numbers += [(tables[3, which] >> bit) & 1 for bit in range(bits)]
+        values += [number.astype(F32) for number in numbers]
+    shape = consts.shape
+    at = rows_of(shape)
+    filled = jnp.zeros(shape, F32)
+    for number, value in enumerate(values):
+        filled = jnp.where(at == number, value, filled)
+    consts[...] = filled
 
 
 def layers_kernel(first, planes, sent):
@@ -118,42 +140,51 @@
         sent[slot] = total
 
 
-def interior_kernel(tile0, planes, inv_x, interior, corners):
+def corners_kernel(tile0, planes, inv_x, corners):
     cells = inv_x.shape[-1]
     row = rows_of((16, cells))
     for field in range(2):
         plane = in_order(planes[:, field], tile0)
-        weights = inv_x[field]
-        interior[field] = lax.dot_general(plane, weights, NT, preferred_element_type=F32).astype(BF16)
-        first = weights[0:16].astype(F32)[0:1]
-        last = weights[cells - 16:cells].astype(F32)[15:16]
+        first = inv_x[field, 0:16].astype(F32)[0:1]
+        last = inv_x[field, cells - 16:cells].astype(F32)[15:16]
         two = jnp.where(row == 0, first, jnp.where(row == 1, last, 0.0)).astype(BF16)
         corners[field] = lax.dot_general(two, plane, NT, preferred_element_type=F32)[0:8]
 
 
-def turned(layer, orient, shift):
+def constant(consts, names, name, lines):
+    at = names.index(name)
+    return jnp.concatenate([consts[at:at + 1]] * (lines // consts.shape[1]), axis=1)
+
+
+def mirrored(layer):
     cells = layer.shape[-1]
-    layer = pltpu.roll(layer, lax.rem(cells - shift, cells), 1)
     back = 127 - lax.broadcasted_iota(jnp.int32, (layer.shape[0], 128), 1)
     pieces = [
         jnp.take_along_axis(layer[:, at:at + 128], back, axis=1)
         for at in range(cells - 128, -1, -128)
     ]
-    return jnp.where(orient == 1, jnp.concatenate(pieces, axis=1), layer)
-
-
-def ghost_rows(tables, blocks, origin, tile_rows):
+    return jnp.concatenate(pieces, axis=1)
+
+
+def ghost_rows(consts, blocks, tile_rows):
     result = []
     count, _, lines = blocks.shape
+    names = table_rows(lines, tile_rows)
     row = rows_of((8, lines))
     for which in range(2):
-        place = lax.rem(tables[0, which] + (count - origin), count)
-        layer = blocks[place].astype(F32)
-        far = tables[1, which] == 1
+        get = lambda *name: constant(consts, names, name, lines)
+        place = get("place", which)
+        layer = blocks[0].astype(F32)
+        for slot in range(1, count):
+            layer = jnp.where(place == slot, blocks[slot].astype(F32), layer)
+        far = get("far", which) == 1
         proton = jnp.where(far, layer[1:2], layer[0:1])
         carbon = jnp.where(far, layer[3:4], layer[2:3])
         both = jnp.where(row == 0, proton, carbon)
-        result.append(turned(both, tables[2, which], tables[3, which] * tile_rows))
+        for bit in range(len(names) // 2 - 4):
+            moved = pltpu.roll(both, lines - (tile_rows << bit), 1)
+            both = jnp.where(get("bit", which, bit) == 1, moved, both)
+        result.append(jnp.where(get("turn", which) == 1, mirrored(both), both))
     return result
 
 
@@ -165,15 +196,18 @@
     return jnp.where(row == 0, low, jnp.where(row == 1, high, 0.0)).astype(BF16)
 
 
-def mix(rates, proton, carbon):
-    new_proton = proton - (rates[0, 0] * proton + rates[0, 2] * carbon)
-    new_carbon = carbon - (rates[0, 1] * carbon + rates[0, 2] * proton)
+def mix(consts, tile_rows, proton, carbon):
+    lines = proton.shape[-1]
+    names = table_rows(lines, tile_rows)
+    first, second, cross = (constant(consts, names, name, lines) for name in names[:3])
+    new_proton = proton - (first * proton + cross * carbon)
+    new_carbon = carbon - (second * carbon + cross * proton)
     return new_proton, new_carbon
 
 
-def next_layers_kernel(tile_rows, origin, tables, rates, blocks, corners, ends, inv_y, sent, ghosts):
+def next_layers_kernel(tile_rows, consts, blocks, corners, ends, inv_y, sent, ghosts):
     cells = ends.shape[-1]
-    sides = ghost_rows(tables, blocks, origin, tile_rows)
+    sides = ghost_rows(consts, blocks, tile_rows)
     row = rows_of((16, cells))
     swept = []
     for field in range(2):
@@ -188,48 +222,50 @@
             found.append(value)
         two = jnp.where(row == 0, found[0], jnp.where(row == 1, found[1], 0.0)).astype(BF16)
         swept.append(lax.dot_general(two, inv_y[field], NT, preferred_element_type=F32)[0:8])
-    new_proton, new_carbon = mix(rates, swept[0], swept[1])
+    new_proton, new_carbon = mix(consts, tile_rows, swept[0], swept[1])
     row8 = rows_of(new_proton.shape)
     total = jnp.where(row8 < 2, new_proton, pltpu.roll(new_carbon, 2, 0))[0:SLOT_ROWS].astype(BF16)
     for slot in range(sent.shape[0]):
         sent[slot] = total
 
 
-def second_sweep(rates, interior, ghosts, ends, inv_y, emit):
+def second_sweep(consts, tile_rows, interior, ghosts, ends, inv_y, emit):
     lines = inv_y.shape[-2]
     swept = []
     for field in range(2):
         outer = lax.dot_general(ghosts[field], ends[field], TN, preferred_element_type=F32)
-        swept.append((interior[field].astype(F32) + outer).astype(BF16))
+        swept.append((interior(field) + outer).astype(BF16))
     chunk = lines // 2
     for start in range(0, lines, chunk):
         moved = [
             jnp.dot(inv_y[field, start:start + chunk], swept[field], preferred_element_type=F32)
             for field in range(2)
         ]
-        new = mix(rates, moved[0], moved[1])
+        new = mix(consts, tile_rows, moved[0], moved[1])
         for field in range(2):
             emit(field, start, chunk, new[field].astype(BF16))
 
 
-def middle_kernel(rates, interior, ghosts, ends, inv_y, far_x, following, inv_x, sem):
-    fetch = pltpu.make_async_copy(far_x, inv_x, sem)
-    fetch.start()
+def middle_kernel(tile_rows, tile0, consts, planes, ghosts, ends, inv_y, inv_x, following):
+    def interior(field):
+        plane = in_order(planes[:, field], tile0)
+        return lax.dot_general(plane, inv_x[field], NT, preferred_element_type=F32)
 
     def emit(field, start, chunk, values):
-        if start == 0 and field == 0:
-            fetch.wait()
-        following[field, start:start + chunk] = lax.dot_general(
-            values, inv_x[field], NT, preferred_element_type=F32
-        ).astype(BF16)
-
-    second_sweep(rates, interior, ghosts, ends, inv_y, emit)
-
-
-def last_kernel(tile_rows, tile0, origin, tables, rates, blocks, interior, ends, inv_y, planes):
-    sides = ghost_rows(tables, blocks, origin, tile_rows)
+        rows = lax.dot_general(values, inv_x[field], NT, preferred_element_type=F32)
+        rows = rows.astype(BF16).reshape(-1, tile_rows, rows.shape[-1])
+        first = start // tile_rows
+        following[first:first + rows.shape[0], field] = rows
+
+    second_sweep(consts, tile_rows, interior, ghosts, ends, inv_y, emit)
+
+
+def last_kernel(tile_rows, tile0, consts, blocks, interior, ends, inv_y, planes):
+    sides = ghost_rows(consts, blocks, tile_rows)
     ghosts = [packed_ghosts(sides, field) for field in range(2)]
-    cells = ends.shape[-1]
+
+    def whole(field):
+        return interior[:, field].reshape(-1, interior.shape[-1]).astype(F32)
 
     def emit(field, start, chunk, values):
         count = planes.shape[0]
@@ -237,7 +273,9 @@
             place = ((start + row) // tile_rows + count - tile0) % count
             planes[place, field] = values[row:row + tile_rows]
 
-    second_sweep(rates, interior, ghosts, ends, inv_y, emit)
+    second_sweep(
+        consts, tile_rows, whole, ghosts, ends, inv_y, emit
+    )
 
 
 def cost(flops, nbytes):
@@ -259,20 +297,19 @@
     tables = jnp.concatenate([partner, face_side, orient, offset], axis=0)
     slots = jax.ShapeDtypeStruct((count, SLOT_ROWS, lines), BF16)
     packed = jax.ShapeDtypeStruct((fields, 16, lines), BF16)
-    swept = jax.ShapeDtypeStruct((fields, lines, cells), BF16)
     sweep_flops = 2 * fields * lines * cells * cells
     array_bytes = 2 * fields * lines * cells
 
     moved = lax.all_to_all(to_planes(magnet), "pen", split_axis=0, concat_axis=0, tiled=True, axis_index_groups=within)
-    ends = pl.pallas_call(
-        ends_kernel,
-        out_shape=jax.ShapeDtypeStruct((fields, 16, cells), BF16),
-        in_specs=[VMEM],
-        out_specs=VMEM,
+    ends, consts = pl.pallas_call(
+        functools.partial(prepare_kernel, tile_rows, origin, count),
+        out_shape=(packed, jax.ShapeDtypeStruct((24, 128), F32)),
+        in_specs=[SMEM, SMEM, VMEM],
+        out_specs=(VMEM, VMEM),
         compiler_params=params(),
         cost_estimate=cost(sweep_flops // 16, array_bytes),
-        name="ends",
-    )(inv_x)
+        name="prepare",
+    )(tables, rates, inv_x)
     sent = pl.pallas_call(
         functools.partial(layers_kernel, tile0),
         out_shape=slots,
@@ -283,44 +320,44 @@
         name="layers",
     )(moved)
     blocks = lax.all_to_all(sent, "blk", split_axis=0, concat_axis=0, tiled=True, axis_index_groups=across)
-    interior, corners = pl.pallas_call(
-        functools.partial(interior_kernel, tile0),
-        out_shape=(swept, jax.ShapeDtypeStruct((fields, 8, lines), F32)),
+    corners = pl.pallas_call(
+        functools.partial(corners_kernel, tile0),
+        out_shape=jax.ShapeDtypeStruct((fields, 8, lines), F32),
         in_specs=[VMEM, VMEM],
-        out_specs=(VMEM, VMEM),
-        compiler_params=params(),
-        cost_estimate=cost(sweep_flops, 4 * array_bytes),
-        name="interior",
+        out_specs=VMEM,
+        compiler_params=params(),
+        cost_estimate=cost(sweep_flops // 16, 2 * array_bytes),
+        name="corners",
     )(moved, inv_x)
     sent, ghosts = pl.pallas_call(
-        functools.partial(next_layers_kernel, tile_rows, origin),
+        functools.partial(next_layers_kernel, tile_rows),
         out_shape=(slots, packed),
-        in_specs=[SMEM, SMEM, VMEM, VMEM, VMEM, VMEM],
+        in_specs=[VMEM] * 5,
         out_specs=(VMEM, VMEM),
         compiler_params=params(),
         cost_estimate=cost(sweep_flops // 16, array_bytes),
         name="next_layers",
-    )(tables, rates, blocks, corners, ends, inv_y)
+    )(consts, blocks, corners, ends, inv_y)
     blocks = lax.all_to_all(sent, "blk", split_axis=0, concat_axis=0, tiled=True, axis_index_groups=across)
     interior = pl.pallas_call(
-        middle_kernel,
-        out_shape=swept,
-        in_specs=[SMEM, VMEM, VMEM, VMEM, VMEM, HBM],
-        out_specs=VMEM,
-        scratch_shapes=[pltpu.VMEM(inv_x.shape, BF16), pltpu.SemaphoreType.DMA],
-        compiler_params=params(),
-        cost_estimate=cost(2 * sweep_flops, 6 * array_bytes),
+        functools.partial(middle_kernel, tile_rows, tile0),
+        out_shape=jax.ShapeDtypeStruct(moved.shape, BF16),
+        input_output_aliases={1: 0},
+        in_specs=[VMEM] * 6,
+        out_specs=VMEM,
+        compiler_params=params(),
+        cost_estimate=cost(3 * sweep_flops, 4 * array_bytes),
         name="middle",
-    )(rates, interior, ghosts, ends, inv_y, inv_x)
+    )(consts, moved, ghosts, ends, inv_y, inv_x)
     planes = pl.pallas_call(
-        functools.partial(last_kernel, tile_rows, tile0, origin),
+        functools.partial(last_kernel, tile_rows, tile0),
         out_shape=jax.ShapeDtypeStruct((lines // tile_rows, fields, tile_rows, cells), BF16),
-        in_specs=[SMEM, SMEM, VMEM, VMEM, VMEM, VMEM],
+        in_specs=[VMEM] * 5,
         out_specs=VMEM,
         compiler_params=params(),
         cost_estimate=cost(sweep_flops, 4 * array_bytes),
         name="last",
-    )(tables, rates, blocks, interior, ends, inv_y)
+    )(consts, blocks, interior, ends, inv_y)
     back = lax.all_to_all(planes, "pen", split_axis=0, concat_axis=0, tiled=True, axis_index_groups=within)
     return from_planes(back)[None]
 

time: 89.9 us -> 88.6 us (0.986)
  local copies, waits for them, and re-layouts: 4.38 us -> 1.89 us
  waiting for transfers between devices: 3.33 us -> 5.39 us
  Pallas kernels: 9.59 us -> 8.62 us
    unnamed x20 -> x16, local copies, waits for them, and re-layouts: 4.38 us -> 1.89 us
    all_to_all x2, waiting for transfers between devices: 3.33 us -> 5.39 us  [local(): lax.all_to_all(sent, 'blk', split_axis=0, concat_axis=0, tiled=True, axis...]
    pallas_call x5, Pallas kernels: 7.43 us -> 6.46 us  [the longest x1 2.37 us: local(): pl.pallas_call(functools.partial(middle_kernel, tile_rows, tile0), out_sh...]
where the time goes in v5:
time: 88.6 us; the launch traced here: 88.3 us
  blocking collectives  49.3 us (56%)
  starting transfers between devices  23 us (26%)
  Pallas kernels  8.62 us (10%)
  waiting for transfers between devices  5.39 us (6%)
  local copies, waits for them, and re-layouts  1.89 us (2%)
    all_to_all x1, blocking collectives, local(): lax.all_to_all(to_planes(magnet), 'pen', split_axis=0, concat_axis=0, til...  26.1 us
    all_to_all x1, blocking collectives, local(): lax.all_to_all(planes, 'pen', split_axis=0, concat_axis=0, tiled=True, ax...  23.2 us
    all_to_all x2, starting transfers between devices, local(): lax.all_to_all(sent, 'blk', split_axis=0, concat_axis=0, tiled=True, axis...  23 us
    all_to_all x2, waiting for transfers between devices, local(): lax.all_to_all(sent, 'blk', split_axis=0, concat_axis=0, tiled=True, axis...  5.39 us
    pallas_call x1, Pallas kernels, local(): pl.pallas_call(functools.partial(middle_kernel, tile_rows, tile0), out_sh...  2.37 us
    unnamed x16, local copies, waits for them, and re-layouts  1.89 us
  transfers between devices with their start and end apart: 2, of which 2 were waited for; matrix products, arithmetic and copies ran while one was open for 0% of the time, Pallas kernels for 4%

profile of v5, /device:TPU:1, one launch (start us, length us, event | category | flops | bytes accessed | tf_op | source)
XLA Modules:
  0.0 88.3 jit_solution(10251935687398692784)
XLA Ops:
  0.0 0.0 copy-start.2
  0.0 1.2 %copy-done.2 = bf16[1,2,32,16,512]{4,3,2,1,0:T(8,128)(2,1)S(1)} copy-done((bf16[1,2,32,16,512]{4,3,2,1,0:T(8,128)(2,1)S(1)}, bf16[1,2,32,16,512]{4,3,2,1,0:T(8,128)(2,1)}, u32[]{:S(2)}) %copy-start.2) | copy-done | bytes 1048600
  1.2 0.3 to_planes.1
  1.5 26.1 %all_to_all.20.planes = bf16[32,2,16,512]{3,2,1,0:T(8,128)(2,1)S(1)} all-to-all(bf16[32,2,16,512]{3,2,1,0:T(8,128)(2,1)S(1)} %to_planes.1), channel_id=1, replica_groups={{20,21,22,23,24,25,26,27,28,29,30,31,0,1,2,3,4,5,6,7,8,9,10,11,12,13,14..., dimensions={0} | all-to-all | bytes 2097152 | tf_op jit(solution)/shard_map/all_to_all | solution.py:303
  27.6 0.0 copy-start
  27.6 0.9 %layers.1 = bf16[16,4,512]{2,1,0:T(4,128)(2,1)} custom-call(bf16[32,2,16,512]{3,2,1,0:T(8,128)(2,1)S(1)} %all_to_all.20.planes), custom_call_target="tpu_custom_call" | custom-call | flops 33554432 | bytes 1048576 | tf_op jit(solution)/shard_map/layers/pallas_call | solution.py:313
  28.5 0.0 copy-start.4
  28.5 0.0 copy-start.5
  28.5 0.0 copy-start.6
  28.5 0.0 copy-start.7
  28.5 12.9 %all-to-all-start.1 = ((bf16[16,4,512]{2,1,0:T(4,128)(2,1)}), bf16[16,4,512]{2,1,0:T(4,128)(2,1)S(1)}, u32[]{:S(2)}, u32[]{:S(2)}) async-start(bf16[16,4,512]{2,1,0:T(4,128)(2,1)} %layers.1), calls=%async_computation.1 | async-start | bytes 131072 | tf_op jit(solution)/shard_map/all_to_all | solution.py:322
  41.4 0.0 copy-done.4
  41.4 0.0 copy-done.5
  41.4 0.0 copy-done.6
  41.4 0.0 copy-done.7
  41.5 0.0 copy-start.3
  41.5 0.0 copy-done
  41.5 0.6 copy-done.3
  42.1 0.9 %prepare.1 = (bf16[2,16,512]{2,1,0:T(8,128)(2,1)S(1)}, f32[24,128]{1,0:T(8,128)S(1)}) custom-call(s32[4,2]{1,0:T(4,128)S(1)} %pad_add_fusion.tables, f32[1,3]{1,0:T(1,128)S(1)} %copy-done.3, bf16[2,512,512]{2,1,0:T(8,128)(2,1)S(1)} %bitcast.4), custom_call_target="tpu_custom_call" | custom-call | flops 33554432 | bytes 1048576 | tf_op jit(solution)/shard_map/prepare/pallas_call | solution.py:304
  43.1 0.0 copy-start.1
  43.1 0.4 corners.1
  43.4 2.9 %all-to-all-done.1.blocks = bf16[16,4,512]{2,1,0:T(4,128)(2,1)S(1)} async-done(((bf16[16,4,512]{2,1,0:T(4,128)(2,1)}), bf16[16,4,512]{2,1,0:T(4,128)(2,1)S(1)}, u32[]{:S(2)}, u32[]{:S(2)}) %all-to-all-start.1) | async-done | bytes 65568 | tf_op jit(solution)/shard_map/all_to_all | solution.py:322
  46.3 0.0 copy-done.1
  46.3 1.3 %next_layers.1 = (bf16[16,4,512]{2,1,0:T(4,128)(2,1)}, bf16[2,16,512]{2,1,0:T(8,128)(2,1)S(1)}) custom-call(f32[24,128]{1,0:T(8,128)S(1)} %get-tuple-element.9.consts, bf16[16,4,512]{2,1,0:T(4,128)(2,1)S(1)} %all-to-all-done.1.blocks, f32[2,8,512]{2,1,0:T(8,128)S(1)} %corners.1, bf16[2,16,512]{2,1,0:T(8,128)(2,1)S(1)} %get-tuple-element.10.ends, ...), custom_call_target="tpu_custom_call" | custom-call | flops 33554432 | bytes 1048576 | tf_op jit(solution)/shard_map/next_layers/pallas_call | solution.py:332
  47.6 10.1 %all-to-all-start.2 = ((bf16[16,4,512]{2,1,0:T(4,128)(2,1)}), bf16[16,4,512]{2,1,0:T(4,128)(2,1)S(1)}, u32[]{:S(2)}, u32[]{:S(2)}) async-start(bf16[16,4,512]{2,1,0:T(4,128)(2,1)} %get-tuple-element.11), calls=%async_computation.2 | async-start | bytes 131072 | tf_op jit(solution)/shard_map/all_to_all | solution.py:341
  57.7 2.4 %middle.1.interior = bf16[32,2,16,512]{3,2,1,0:T(8,128)(2,1)S(1)} custom-call(f32[24,128]{1,0:T(8,128)S(1)} %get-tuple-element.9.consts, bf16[32,2,16,512]{3,2,1,0:T(8,128)(2,1)S(1)} %all_to_all.20.planes, bf16[2,16,512]{2,1,0:T(8,128)(2,1)S(1)} %get-tuple-element.12.ghosts, ...), custom_call_target="tpu_custom_call", output_to_operand_aliasing={{}: (1, {})} | custom-call | flops 1610612736 | bytes 4194304 | tf_op jit(solution)/shard_map/middle/pallas_call | solution.py:342
  60.1 2.5 %all-to-all-done.2.blocks = bf16[16,4,512]{2,1,0:T(4,128)(2,1)S(1)} async-done(((bf16[16,4,512]{2,1,0:T(4,128)(2,1)}), bf16[16,4,512]{2,1,0:T(4,128)(2,1)S(1)}, u32[]{:S(2)}, u32[]{:S(2)}) %all-to-all-start.2) | async-done | bytes 65568 | tf_op jit(solution)/shard_map/all_to_all | solution.py:341
  62.6 1.5 %last.1 = bf16[32,2,16,512]{3,2,1,0:T(8,128)(2,1)S(1)} custom-call(f32[24,128]{1,0:T(8,128)S(1)} %get-tuple-element.9.consts, bf16[16,4,512]{2,1,0:T(4,128)(2,1)S(1)} %all-to-all-done.2.blocks, bf16[32,2,16,512]{3,2,1,0:T(8,128)(2,1)S(1)} %middle.1.interior, bf16[2,16,512]{2,1,0:T(8,128)(2,1)S(1)} %get-tuple-element.10.ends, bf16[2,512,512]{2,1,0:T(8,128)(2,1)S(1)} %bitcast.9), custom_call_target="tpu_custom_call" | custom-call | flops 536870912 | bytes 4194304 | tf_op jit(solution)/shard_map/last/pallas_call | solution.py:352
  64.1 23.2 %all_to_all.21.source = bf16[32,2,16,512]{3,2,1,0:T(8,128)(2,1)S(1)} all-to-all(bf16[32,2,16,512]{3,2,1,0:T(8,128)(2,1)S(1)} %last.1), channel_id=1, replica_groups={{20,21,22,23,24,25,26,27,28,29,30,31,0,1,2,3,4,5,6,7,8,9,10,11,12,13,14..., dimensions={0} | all-to-all | bytes 2097152 | tf_op jit(solution)/shard_map/all_to_all | solution.py:361
  87.2 1.0 %from_planes.1 = bf16[2,32,16,512]{3,2,1,0:T(8,128)(2,1)} custom-call(bf16[32,2,16,512]{3,2,1,0:T(8,128)(2,1)S(1)} %all_to_all.21.source), custom_call_target="tpu_custom_call" | custom-call | tf_op jit(solution)/shard_map/from_planes/pallas_call | solution.py:76
  (1 shorter events, 0.0 us)
Async XLA Ops:
  0.0 1.2 %copy-start.2 = (bf16[1,2,32,16,512]{4,3,2,1,0:T(8,128)(2,1)S(1)}, bf16[1,2,32,16,512]{4,3,2,1,0:T(8,128)(2,1)}, u32[]{:S(2)}) copy-start(bf16[1,2,32,16,512]{4,3,2,1,0:T(8,128)(2,1)} %param.8) | copy-start | bytes 3145732
  27.6 13.9 %copy-start = (bf16[1,2,512,512]{3,2,1,0:T(8,128)(2,1)S(1)}, bf16[1,2,512,512]{3,2,1,0:T(8,128)(2,1)}, u32[]{:S(2)}) copy-start(bf16[1,2,512,512]{3,2,1,0:T(8,128)(2,1)} %param.9) | copy-start | bytes 3145732
  28.5 12.9 %copy-start.4 = (s32[1,2]{1,0:T(1,128)S(1)}, s32[1,2]{1,0:T(1,128)}, u32[]{:S(2)}) copy-start(s32[1,2]{1,0:T(1,128)} %param.15) | copy-start | bytes 28
  28.5 12.9 %copy-start.5 = (s32[1,2]{1,0:T(1,128)S(1)}, s32[1,2]{1,0:T(1,128)}, u32[]{:S(2)}) copy-start(s32[1,2]{1,0:T(1,128)} %param.14) | copy-start | bytes 28
  28.5 12.9 %copy-start.6 = (s32[1,2]{1,0:T(1,128)S(1)}, s32[1,2]{1,0:T(1,128)}, u32[]{:S(2)}) copy-start(s32[1,2]{1,0:T(1,128)} %param.13) | copy-start | bytes 28
  28.5 12.9 %copy-start.7 = (s32[1,2]{1,0:T(1,128)S(1)}, s32[1,2]{1,0:T(1,128)}, u32[]{:S(2)}) copy-start(s32[1,2]{1,0:T(1,128)} %param.12) | copy-start | bytes 28
  28.5 17.8 %all-to-all-start.1 = ((bf16[16,4,512]{2,1,0:T(4,128)(2,1)}), bf16[16,4,512]{2,1,0:T(4,128)(2,1)S(1)}, u32[]{:S(2)}, u32[]{:S(2)}) async-start(bf16[16,4,512]{2,1,0:T(4,128)(2,1)} %layers.1), calls=%async_computation.1 | async-start | bytes 131072 | tf_op jit(solution)/shard_map/all_to_all | solution.py:322
  41.5 0.7 copy-start.3
  43.1 3.3 %copy-start.1 = (bf16[1,2,512,512]{3,2,1,0:T(8,128)(2,1)S(1)}, bf16[1,2,512,512]{3,2,1,0:T(8,128)(2,1)}, u32[]{:S(2)}) copy-start(bf16[1,2,512,512]{3,2,1,0:T(8,128)(2,1)} %param.10) | copy-start | bytes 3145732
  47.6 15.0 %all-to-all-start.2 = ((bf16[16,4,512]{2,1,0:T(4,128)(2,1)}), bf16[16,4,512]{2,1,0:T(4,128)(2,1)S(1)}, u32[]{:S(2)}, u32[]{:S(2)}) async-start(bf16[16,4,512]{2,1,0:T(4,128)(2,1)} %get-tuple-element.11), calls=%async_computation.2 | async-start | bytes 131072 | tf_op jit(solution)/shard_map/all_to_all | solution.py:341

commit v6 on v5

--- a/solution.py
+++ b/solution.py
@@ -51,11 +51,11 @@
 
 
 def to_planes_kernel(source, target, sems):
-    transfer(pieces_of(source, target, 4), sems)
+    transfer(pieces_of(source, target, 1), sems)
 
 
 def from_planes_kernel(source, target, sems):
-    transfer([(held, sent) for sent, held in pieces_of(target, source, 4)], sems)
+    transfer([(held, sent) for sent, held in pieces_of(target, source, 1)], sems)
 
 
 def to_planes(state):
@@ -65,8 +65,8 @@
         out_shape=jax.ShapeDtypeStruct((planes, fields, lines, cells), BF16),
         in_specs=[HBM],
         out_specs=VMEM,
-        scratch_shapes=[pltpu.SemaphoreType.DMA((8,))],
-        compiler_params=params(),
+        scratch_shapes=[pltpu.SemaphoreType.DMA((2,))],
+        compiler_params=pltpu.CompilerParams(vmem_limit_bytes=52 * 1024 * 1024),
         name="to_planes",
     )(state)
 
@@ -78,7 +78,7 @@
         out_shape=jax.ShapeDtypeStruct((fields, planes, lines, cells), BF16),
         in_specs=[VMEM],
         out_specs=HBM,
-        scratch_shapes=[pltpu.SemaphoreType.DMA((8,))],
+        scratch_shapes=[pltpu.SemaphoreType.DMA((2,))],
         compiler_params=params(),
         name="from_planes",
     )(moved)
@@ -90,13 +90,12 @@
     return ordered.reshape(-1, tiles.shape[-1])
 
 
-def table_rows(lines, tile_rows):
-    bits = (lines // tile_rows).bit_length() - 1
-    names = ["proton", "carbon", "cross"]
-    for which in range(2):
-        names += [("place", which), ("far", which), ("turn", which)]
-        names += [("bit", which, bit) for bit in range(bits)]
-    return names
+def shift_bits(lines, tile_rows):
+    return (lines // tile_rows).bit_length() - 1
+
+
+def constant_names(lines, tile_rows):
+    return ["proton", "carbon", "cross", "place", "far", "turn", *range(shift_bits(lines, tile_rows))]
 
 
 def prepare_kernel(tile_rows, origin, count, tables, rates, inv_x, ends, consts):
@@ -107,34 +106,31 @@
     pick = jnp.where(pick, 1.0, 0.0).astype(BF16)
     for field in range(2):
         ends[field] = lax.dot_general(pick, inv_x[field], NT, preferred_element_type=F32).astype(BF16)
-    values = [rates[0, number] for number in range(3)]
+    values = [(rates[0, number], rates[0, number]) for number in range(3)]
+    sides = []
     for which in range(2):
         place = lax.rem(tables[0, which] + (count - origin), count)
         numbers = [place, tables[1, which], tables[2, which]]
-        bits = len(table_rows(cells, tile_rows)) // 2 - 4
-        numbers += [(tables[3, which] >> bit) & 1 for bit in range(bits)]
-        values += [number.astype(F32) for number in numbers]
-    shape = consts.shape
-    at = rows_of(shape)
-    filled = jnp.zeros(shape, F32)
-    for number, value in enumerate(values):
-        filled = jnp.where(at == number, value, filled)
-    consts[...] = filled
+        numbers += [(tables[3, which] >> bit) & 1 for bit in range(shift_bits(cells, tile_rows))]
+        sides.append([number.astype(F32) for number in numbers])
+    values += zip(*sides)
+    upper = rows_of((8, consts.shape[1])) < 2
+    for number, (low, high) in enumerate(values):
+        consts[8 * number:8 * number + 8] = jnp.where(upper, low, high)
 
 
 def layers_kernel(first, planes, sent):
     cells = planes.shape[-1]
-    total = None
-    lane = lax.broadcasted_iota(jnp.int32, (16, 128), 1)
-    row = rows_of((16, 128))
-    for field in range(2):
-        for end in range(2):
-            pick = (row == field * 2 + end) & (lane == end * 127)
-            pick = jnp.where(pick, 1.0, 0.0).astype(BF16)
-            start = end * (cells - 128)
-            edge = in_order(planes[:, field, :, start:start + 128], first)
-            part = lax.dot_general(pick, edge, NT, preferred_element_type=F32)
-            total = part if total is None else total + part
+    lane = lax.broadcasted_iota(jnp.int32, (16, 512), 1)
+    row = rows_of((16, 512))
+    pick = (row < SLOT_ROWS) & (lane == row * 128 + jnp.where(row >= 2, 127, 0))
+    pick = jnp.where(pick, 1.0, 0.0).astype(BF16)
+    edges = [
+        in_order(planes[:, field, :, start:start + 128], first)
+        for start in (0, cells - 128)
+        for field in range(2)
+    ]
+    total = lax.dot_general(pick, jnp.concatenate(edges, axis=1), NT, preferred_element_type=F32)
     total = total[0:SLOT_ROWS].astype(BF16)
     for slot in range(sent.shape[0]):
         sent[slot] = total
@@ -152,8 +148,8 @@
 
 
 def constant(consts, names, name, lines):
-    at = names.index(name)
-    return jnp.concatenate([consts[at:at + 1]] * (lines // consts.shape[1]), axis=1)
+    at = 8 * names.index(name)
+    return jnp.concatenate([consts[at:at + 8]] * (lines // consts.shape[1]), axis=1)
 
 
 def mirrored(layer):
@@ -167,39 +163,36 @@
 
 
 def ghost_rows(consts, blocks, tile_rows):
-    result = []
     count, _, lines = blocks.shape
-    names = table_rows(lines, tile_rows)
-    row = rows_of((8, lines))
+    names = constant_names(lines, tile_rows)
+    place = constant(consts, names, "place", lines)
+    layers = []
     for which in range(2):
-        get = lambda *name: constant(consts, names, name, lines)
-        place = get("place", which)
+        wanted = place[2 * which:2 * which + 1]
         layer = blocks[0].astype(F32)
         for slot in range(1, count):
-            layer = jnp.where(place == slot, blocks[slot].astype(F32), layer)
-        far = get("far", which) == 1
-        proton = jnp.where(far, layer[1:2], layer[0:1])
-        carbon = jnp.where(far, layer[3:4], layer[2:3])
-        both = jnp.where(row == 0, proton, carbon)
-        for bit in range(len(names) // 2 - 4):
-            moved = pltpu.roll(both, lines - (tile_rows << bit), 1)
-            both = jnp.where(get("bit", which, bit) == 1, moved, both)
-        result.append(jnp.where(get("turn", which) == 1, mirrored(both), both))
-    return result
-
-
-def packed_ghosts(sides, field):
-    cells = sides[0].shape[-1]
-    row = rows_of((16, cells))
-    low = sides[0][field:field + 1]
-    high = sides[1][field:field + 1]
+            layer = jnp.where(wanted == slot, blocks[slot].astype(F32), layer)
+        layers.append(layer)
+    near = jnp.concatenate([layers[0][0:2], layers[1][0:2]] * 2, axis=0)
+    far = jnp.concatenate([layers[0][2:4], layers[1][2:4]] * 2, axis=0)
+    rows = jnp.where(constant(consts, names, "far", lines) == 1, far, near)
+    for bit in range(shift_bits(lines, tile_rows)):
+        moved = pltpu.roll(rows, lines - (tile_rows << bit), 1)
+        rows = jnp.where(constant(consts, names, bit, lines) == 1, moved, rows)
+    return jnp.where(constant(consts, names, "turn", lines) == 1, mirrored(rows), rows)
+
+
+def packed_ghosts(found, field):
+    row = rows_of((16, found.shape[-1]))
+    low = found[field:field + 1]
+    high = found[2 + field:3 + field]
     return jnp.where(row == 0, low, jnp.where(row == 1, high, 0.0)).astype(BF16)
 
 
 def mix(consts, tile_rows, proton, carbon):
     lines = proton.shape[-1]
-    names = table_rows(lines, tile_rows)
-    first, second, cross = (constant(consts, names, name, lines) for name in names[:3])
+    names = constant_names(lines, tile_rows)
+    first, second, cross = (constant(consts, names, name, lines)[0:1] for name in names[:3])
     new_proton = proton - (first * proton + cross * carbon)
     new_carbon = carbon - (second * carbon + cross * proton)
     return new_proton, new_carbon
@@ -207,24 +200,26 @@
 
 def next_layers_kernel(tile_rows, consts, blocks, corners, ends, inv_y, sent, ghosts):
     cells = ends.shape[-1]
-    sides = ghost_rows(consts, blocks, tile_rows)
+    found = ghost_rows(consts, blocks, tile_rows)
     row = rows_of((16, cells))
     swept = []
     for field in range(2):
         edge = ends[field].astype(F32)
-        ghosts[field] = packed_ghosts(sides, field)
-        found = []
+        ghosts[field] = packed_ghosts(found, field)
+        layers = []
         for end in range(2):
             lane = end * (cells - 1)
             value = corners[field][end:end + 1]
             for which in range(2):
-                value = value + edge[which:which + 1, lane:lane + 1] * sides[which][field:field + 1]
-            found.append(value)
-        two = jnp.where(row == 0, found[0], jnp.where(row == 1, found[1], 0.0)).astype(BF16)
+                at = which * 2 + field
+                value = value + edge[which:which + 1, lane:lane + 1] * found[at:at + 1]
+            layers.append(value)
+        two = jnp.where(row == 0, layers[0], jnp.where(row == 1, layers[1], 0.0)).astype(BF16)
         swept.append(lax.dot_general(two, inv_y[field], NT, preferred_element_type=F32)[0:8])
     new_proton, new_carbon = mix(consts, tile_rows, swept[0], swept[1])
-    row8 = rows_of(new_proton.shape)
-    total = jnp.where(row8 < 2, new_proton, pltpu.roll(new_carbon, 2, 0))[0:SLOT_ROWS].astype(BF16)
+    total = jnp.concatenate(
+        [new_proton[0:1], new_carbon[0:1], new_proton[1:2], new_carbon[1:2]], axis=0
+    ).astype(BF16)
     for slot in range(sent.shape[0]):
         sent[slot] = total
 
@@ -261,8 +256,8 @@
 
 
 def last_kernel(tile_rows, tile0, consts, blocks, interior, ends, inv_y, planes):
-    sides = ghost_rows(consts, blocks, tile_rows)
-    ghosts = [packed_ghosts(sides, field) for field in range(2)]
+    found = ghost_rows(consts, blocks, tile_rows)
+    ghosts = [packed_ghosts(found, field) for field in range(2)]
 
     def whole(field):
         return interior[:, field].reshape(-1, interior.shape[-1]).astype(F32)
@@ -303,7 +298,7 @@
     moved = lax.all_to_all(to_planes(magnet), "pen", split_axis=0, concat_axis=0, tiled=True, axis_index_groups=within)
     ends, consts = pl.pallas_call(
         functools.partial(prepare_kernel, tile_rows, origin, count),
-        out_shape=(packed, jax.ShapeDtypeStruct((24, 128), F32)),
+        out_shape=(packed, jax.ShapeDtypeStruct((8 * len(constant_names(lines, tile_rows)), 128), F32)),
         in_specs=[SMEM, SMEM, VMEM],
         out_specs=(VMEM, VMEM),
         compiler_params=params(),

time: 88.6 us -> 88.3 us (level)
  local copies, waits for them, and re-layouts: 1.89 us -> 0.66 us
  Pallas kernels: 8.62 us -> 9.56 us
    unnamed x16 -> x14, local copies, waits for them, and re-layouts: 1.89 us -> 0.66 us
    pallas_call x1, Pallas kernels: 0.26 us -> 1.22 us  [to_planes(): pl.pallas_call(to_planes_kernel, out_shape=jax.ShapeDtypeStruct((planes,...]
where the time goes in v6:
time: 88.3 us; the launch traced here: 88 us
  blocking collectives  49.3 us (56%)
  starting transfers between devices  23 us (26%)
  Pallas kernels  9.56 us (11%)
  waiting for transfers between devices  5.39 us (6%)
    all_to_all x1, blocking collectives, local(): lax.all_to_all(to_planes(magnet), 'pen', split_axis=0, concat_axis=0, til...  26.1 us
    all_to_all x1, blocking collectives, local(): lax.all_to_all(planes, 'pen', split_axis=0, concat_axis=0, tiled=True, ax...  23.2 us
    all_to_all x2, starting transfers between devices, local(): lax.all_to_all(sent, 'blk', split_axis=0, concat_axis=0, tiled=True, axis...  23 us
    all_to_all x2, waiting for transfers between devices, local(): lax.all_to_all(sent, 'blk', split_axis=0, concat_axis=0, tiled=True, axis...  5.39 us
    pallas_call x1, Pallas kernels, local(): pl.pallas_call(functools.partial(middle_kernel, tile_rows, tile0), out_sh...  2.36 us
  transfers between devices with their start and end apart: 2, of which 2 were waited for; matrix products, arithmetic and copies ran while one was open for 0% of the time, Pallas kernels for 4%

profile of v6, /device:TPU:1, one launch (start us, length us, event | category | flops | bytes accessed | tf_op | source)
XLA Modules:
  0.0 88.0 jit_solution(11868271440114838244)
XLA Ops:
  0.0 1.2 %to_planes.1 = bf16[32,2,16,512]{3,2,1,0:T(8,128)(2,1)S(1)} custom-call(bf16[2,32,16,512]{3,2,1,0:T(8,128)(2,1)} %bitcast.10), custom_call_target="tpu_custom_call" | custom-call | tf_op jit(solution)/shard_map/to_planes/pallas_call | solution.py:63
  1.2 26.1 %all_to_all.20.planes = bf16[32,2,16,512]{3,2,1,0:T(8,128)(2,1)S(1)} all-to-all(bf16[32,2,16,512]{3,2,1,0:T(8,128)(2,1)S(1)} %to_planes.1), channel_id=1, replica_groups={{20,21,22,23,24,25,26,27,28,29,30,31,0,1,2,3,4,5,6,7,8,9,10,11,12,13,14..., dimensions={0} | all-to-all | bytes 2097152 | tf_op jit(solution)/shard_map/all_to_all | solution.py:298
  27.3 0.0 copy-start
  27.3 0.9 %layers.1 = bf16[16,4,512]{2,1,0:T(4,128)(2,1)} custom-call(bf16[32,2,16,512]{3,2,1,0:T(8,128)(2,1)S(1)} %all_to_all.20.planes), custom_call_target="tpu_custom_call" | custom-call | flops 33554432 | bytes 1048576 | tf_op jit(solution)/shard_map/layers/pallas_call | solution.py:308
  28.2 0.0 copy-start.3
  28.2 0.0 copy-start.4
  28.2 0.0 copy-start.5
  28.2 0.0 copy-start.6
  28.2 12.9 %all-to-all-start.1 = ((bf16[16,4,512]{2,1,0:T(4,128)(2,1)}), bf16[16,4,512]{2,1,0:T(4,128)(2,1)S(1)}, u32[]{:S(2)}, u32[]{:S(2)}) async-start(bf16[16,4,512]{2,1,0:T(4,128)(2,1)} %layers.1), calls=%async_computation.1 | async-start | bytes 131072 | tf_op jit(solution)/shard_map/all_to_all | solution.py:317
  41.1 0.0 copy-done.3
  41.1 0.0 copy-done.4
  41.2 0.0 copy-done.5
  41.2 0.0 copy-done.6
  41.2 0.0 copy-start.2
  41.2 0.0 copy-done
  41.2 0.6 copy-done.2
  41.9 0.9 %prepare.1 = (bf16[2,16,512]{2,1,0:T(8,128)(2,1)S(1)}, f32[88,128]{1,0:T(8,128)S(1)}) custom-call(s32[4,2]{1,0:T(4,128)S(1)} %pad_add_fusion.tables, f32[1,3]{1,0:T(1,128)S(1)} %copy-done.2, bf16[2,512,512]{2,1,0:T(8,128)(2,1)S(1)} %bitcast.4), custom_call_target="tpu_custom_call" | custom-call | flops 33554432 | bytes 1048576 | tf_op jit(solution)/shard_map/prepare/pallas_call | solution.py:299
  42.8 0.0 copy-start.1
  42.8 0.4 corners.1
  43.2 2.9 %all-to-all-done.1.blocks = bf16[16,4,512]{2,1,0:T(4,128)(2,1)S(1)} async-done(((bf16[16,4,512]{2,1,0:T(4,128)(2,1)}), bf16[16,4,512]{2,1,0:T(4,128)(2,1)S(1)}, u32[]{:S(2)}, u32[]{:S(2)}) %all-to-all-start.1) | async-done | bytes 65568 | tf_op jit(solution)/shard_map/all_to_all | solution.py:317
  46.0 0.0 copy-done.1
  46.0 1.3 %next_layers.1 = (bf16[16,4,512]{2,1,0:T(4,128)(2,1)}, bf16[2,16,512]{2,1,0:T(8,128)(2,1)S(1)}) custom-call(f32[88,128]{1,0:T(8,128)S(1)} %get-tuple-element.9.consts, bf16[16,4,512]{2,1,0:T(4,128)(2,1)S(1)} %all-to-all-done.1.blocks, f32[2,8,512]{2,1,0:T(8,128)S(1)} %corners.1, bf16[2,16,512]{2,1,0:T(8,128)(2,1)S(1)} %get-tuple-element.10.ends, ...), custom_call_target="tpu_custom_call" | custom-call | flops 33554432 | bytes 1048576 | tf_op jit(solution)/shard_map/next_layers/pallas_call | solution.py:327
  47.4 10.1 %all-to-all-start.2 = ((bf16[16,4,512]{2,1,0:T(4,128)(2,1)}), bf16[16,4,512]{2,1,0:T(4,128)(2,1)S(1)}, u32[]{:S(2)}, u32[]{:S(2)}) async-start(bf16[16,4,512]{2,1,0:T(4,128)(2,1)} %get-tuple-element.11), calls=%async_computation.2 | async-start | bytes 131072 | tf_op jit(solution)/shard_map/all_to_all | solution.py:336
  57.5 2.4 %middle.1.interior = bf16[32,2,16,512]{3,2,1,0:T(8,128)(2,1)S(1)} custom-call(f32[88,128]{1,0:T(8,128)S(1)} %get-tuple-element.9.consts, bf16[32,2,16,512]{3,2,1,0:T(8,128)(2,1)S(1)} %all_to_all.20.planes, bf16[2,16,512]{2,1,0:T(8,128)(2,1)S(1)} %get-tuple-element.12.ghosts, ...), custom_call_target="tpu_custom_call", output_to_operand_aliasing={{}: (1, {})} | custom-call | flops 1610612736 | bytes 4194304 | tf_op jit(solution)/shard_map/middle/pallas_call | solution.py:337
  59.8 2.5 %all-to-all-done.2.blocks = bf16[16,4,512]{2,1,0:T(4,128)(2,1)S(1)} async-done(((bf16[16,4,512]{2,1,0:T(4,128)(2,1)}), bf16[16,4,512]{2,1,0:T(4,128)(2,1)S(1)}, u32[]{:S(2)}, u32[]{:S(2)}) %all-to-all-start.2) | async-done | bytes 65568 | tf_op jit(solution)/shard_map/all_to_all | solution.py:336
  62.4 1.5 %last.1 = bf16[32,2,16,512]{3,2,1,0:T(8,128)(2,1)S(1)} custom-call(f32[88,128]{1,0:T(8,128)S(1)} %get-tuple-element.9.consts, bf16[16,4,512]{2,1,0:T(4,128)(2,1)S(1)} %all-to-all-done.2.blocks, bf16[32,2,16,512]{3,2,1,0:T(8,128)(2,1)S(1)} %middle.1.interior, bf16[2,16,512]{2,1,0:T(8,128)(2,1)S(1)} %get-tuple-element.10.ends, bf16[2,512,512]{2,1,0:T(8,128)(2,1)S(1)} %bitcast.9), custom_call_target="tpu_custom_call" | custom-call | flops 536870912 | bytes 4194304 | tf_op jit(solution)/shard_map/last/pallas_call | solution.py:347
  63.8 23.2 %all_to_all.21.source = bf16[32,2,16,512]{3,2,1,0:T(8,128)(2,1)S(1)} all-to-all(bf16[32,2,16,512]{3,2,1,0:T(8,128)(2,1)S(1)} %last.1), channel_id=1, replica_groups={{20,21,22,23,24,25,26,27,28,29,30,31,0,1,2,3,4,5,6,7,8,9,10,11,12,13,14..., dimensions={0} | all-to-all | bytes 2097152 | tf_op jit(solution)/shard_map/all_to_all | solution.py:356
  87.0 1.0 %from_planes.1 = bf16[2,32,16,512]{3,2,1,0:T(8,128)(2,1)} custom-call(bf16[32,2,16,512]{3,2,1,0:T(8,128)(2,1)S(1)} %all_to_all.21.source), custom_call_target="tpu_custom_call" | custom-call | tf_op jit(solution)/shard_map/from_planes/pallas_call | solution.py:76
  (1 shorter events, 0.0 us)
Async XLA Ops:
  27.3 13.9 %copy-start = (bf16[1,2,512,512]{3,2,1,0:T(8,128)(2,1)S(1)}, bf16[1,2,512,512]{3,2,1,0:T(8,128)(2,1)}, u32[]{:S(2)}) copy-start(bf16[1,2,512,512]{3,2,1,0:T(8,128)(2,1)} %param.9) | copy-start | bytes 3145732
  28.2 12.9 %copy-start.3 = (s32[1,2]{1,0:T(1,128)S(1)}, s32[1,2]{1,0:T(1,128)}, u32[]{:S(2)}) copy-start(s32[1,2]{1,0:T(1,128)} %param.15) | copy-start | bytes 28
  28.2 12.9 %copy-start.4 = (s32[1,2]{1,0:T(1,128)S(1)}, s32[1,2]{1,0:T(1,128)}, u32[]{:S(2)}) copy-start(s32[1,2]{1,0:T(1,128)} %param.14) | copy-start | bytes 28
  28.2 12.9 %copy-start.5 = (s32[1,2]{1,0:T(1,128)S(1)}, s32[1,2]{1,0:T(1,128)}, u32[]{:S(2)}) copy-start(s32[1,2]{1,0:T(1,128)} %param.13) | copy-start | bytes 28
  28.2 12.9 %copy-start.6 = (s32[1,2]{1,0:T(1,128)S(1)}, s32[1,2]{1,0:T(1,128)}, u32[]{:S(2)}) copy-start(s32[1,2]{1,0:T(1,128)} %param.12) | copy-start | bytes 28
  28.2 17.8 %all-to-all-start.1 = ((bf16[16,4,512]{2,1,0:T(4,128)(2,1)}), bf16[16,4,512]{2,1,0:T(4,128)(2,1)S(1)}, u32[]{:S(2)}, u32[]{:S(2)}) async-start(bf16[16,4,512]{2,1,0:T(4,128)(2,1)} %layers.1), calls=%async_computation.1 | async-start | bytes 131072 | tf_op jit(solution)/shard_map/all_to_all | solution.py:317
  41.2 0.7 copy-start.2
  42.8 3.3 %copy-start.1 = (bf16[1,2,512,512]{3,2,1,0:T(8,128)(2,1)S(1)}, bf16[1,2,512,512]{3,2,1,0:T(8,128)(2,1)}, u32[]{:S(2)}) copy-start(bf16[1,2,512,512]{3,2,1,0:T(8,128)(2,1)} %param.10) | copy-start | bytes 3145732
  47.4 15.0 %all-to-all-start.2 = ((bf16[16,4,512]{2,1,0:T(4,128)(2,1)}), bf16[16,4,512]{2,1,0:T(4,128)(2,1)S(1)}, u32[]{:S(2)}, u32[]{:S(2)}) async-start(bf16[16,4,512]{2,1,0:T(4,128)(2,1)} %get-tuple-element.11), calls=%async_computation.2 | async-start | bytes 131072 | tf_op jit(solution)/shard_map/all_to_all | solution.py:336

commit v7 on v6

v7 whole, which is shorter than its diff:
```python
import functools

import jax
import jax.numpy as jnp
from jax import lax
from jax.experimental import pallas as pl
from jax.experimental.pallas import tpu as pltpu
from jax.sharding import PartitionSpec as P

STEPS = 2
SLOT_ROWS = 4
F32 = jnp.float32
BF16 = jnp.bfloat16
VMEM = pl.BlockSpec(memory_space=pltpu.VMEM)
HBM = pl.BlockSpec(memory_space=pltpu.HBM)
SMEM = pl.BlockSpec(memory_space=pltpu.SMEM)
NT = (((1,), (1,)), ((), ()))
TN = (((0,), (0,)), ((), ()))


def turned_group(size, first):
    return [[(first + member) % size for member in range(size)]]


def params():
    return pltpu.CompilerParams(vmem_limit_bytes=16 * 1024 * 1024)


def rows_of(shape):
    return lax.broadcasted_iota(jnp.int32, shape, 0)


def transfer(pairs, sems):
    copies = [
        pltpu.make_async_copy(source, target, sems.at[number])
        for number, (source, target) in enumerate(pairs)
    ]
    for copy in copies:
        copy.start()
    for copy in copies:
        copy.wait()


def pieces_of(by_field, by_plane, parts):
    chunk = by_plane.shape[0] // parts
    return [
        (by_field.at[field, pl.ds(part * chunk, chunk)], by_plane.at[pl.ds(part * chunk, chunk), field])
        for part in range(parts)
        for field in range(2)
    ]


def from_planes_kernel(source, target, sems):
    transfer([(held, sent) for sent, held in pieces_of(target, source, 1)], sems)


def from_planes(moved):
    planes, fields, lines, cells = moved.shape
    return pl.pallas_call(
        from_planes_kernel,
        out_shape=jax.ShapeDtypeStruct((fields, planes, lines, cells), BF16),
        in_specs=[VMEM],
        out_specs=HBM,
        scratch_shapes=[pltpu.SemaphoreType.DMA((2,))],
        compiler_params=params(),
        name="from_planes",
    )(moved)


def in_order(tiles, first):
    count = tiles.shape[0]
    ordered = jnp.concatenate([tiles[count - first:], tiles[:count - first]], axis=0)
    return ordered.reshape(-1, tiles.shape[-1])


def shift_bits(lines, tile_rows):
    return (lines // tile_rows).bit_length() - 1


def stage_kernel(state, inv_x, planes, ends, probe, sides, tops, sems):
    cells = inv_x.shape[-1]
    pairs = pieces_of(state, planes, 1)
    for field in range(2):
        for end in range(2):
            pairs.append((inv_x.at[field, :, pl.ds(end * (cells - 128), 128)], sides.at[field, end]))
            pairs.append((inv_x.at[field, pl.ds(end * (cells - 16), 16)], tops.at[field, end]))
    copies = [
        pltpu.make_async_copy(source, target, sems.at[number])
        for number, (source, target) in enumerate(pairs)
    ]
    for copy in copies:
        copy.start()
    for copy in copies[2:]:
        copy.wait()

    lane = lax.broadcasted_iota(jnp.int32, (16, 256), 1)
    row = rows_of((16, 256))
    pick = ((row == 0) & (lane == 0)) | ((row == 1) & (lane == 255))
    pick = jnp.where(pick, 1.0, 0.0).astype(BF16)
    row = rows_of((16, cells))
    lane = lax.broadcasted_iota(jnp.int32, (16, cells), 1)
    hot = ((row == 2) & (lane == 0)) | ((row == 3) & (lane == cells - 1))
    hot = jnp.where(hot, 1.0, 0.0)
    for field in range(2):
        both = jnp.concatenate([sides[field, 0], sides[field, 1]], axis=1)
        ends[field] = lax.dot_general(pick, both, NT, preferred_element_type=F32).astype(BF16)
        first = tops[field, 0].astype(F32)[0:1]
        last = tops[field, 1].astype(F32)[15:16]
        probe[field] = jnp.where(row == 0, first, jnp.where(row == 1, last, hot)).astype(BF16)
    for copy in copies[:2]:
        copy.wait()


def layers_kernel(tile0, planes, probe, sent, corners):
    seen = []
    for field in range(2):
        plane = in_order(planes[:, field], tile0)
        seen.append(lax.dot_general(probe[field], plane, NT, preferred_element_type=F32)[0:8])
        corners[field] = seen[field]
    rows = [seen[field][2 + end:3 + end] for end in range(2) for field in range(2)]
    total = jnp.concatenate(rows, axis=0).astype(BF16)
    for slot in range(sent.shape[0]):
        sent[slot] = total


def spread(number, lines):
    return jnp.concatenate([jnp.broadcast_to(number, (1, 128))] * (lines // 128), axis=1)


def by_side(pair, lines):
    upper = rows_of((8, 128)) < 2
    low = jnp.broadcast_to(pair[0:1, 0:1], (8, 128))
    high = jnp.broadcast_to(pair[0:1, 1:2], (8, 128))
    return jnp.concatenate([jnp.where(upper, low, high)] * (lines // 128), axis=1)


def mirrored(layer):
    cells = layer.shape[-1]
    back = 127 - lax.broadcasted_iota(jnp.int32, (layer.shape[0], 128), 1)
    pieces = [
        jnp.take_along_axis(layer[:, at:at + 128], back, axis=1)
        for at in range(cells - 128, -1, -128)
    ]
    return jnp.concatenate(pieces, axis=1)


def ghost_rows(tables, blocks, origin, tile_rows):
    count, _, lines = blocks.shape
    partner, face_side, orient, offset = (by_side(table, lines) for table in tables)
    place = partner - origin
    place = jnp.where(place < 0, place + count, place)
    layers = []
    for which in range(2):
        wanted = place[2 * which:2 * which + 1]
        layer = blocks[0].astype(F32)
        for slot in range(1, count):
            layer = jnp.where(wanted == slot, blocks[slot].astype(F32), layer)
        layers.append(layer)
    near = jnp.concatenate([layers[0][0:2], layers[1][0:2]] * 2, axis=0)
    far = jnp.concatenate([layers[0][2:4], layers[1][2:4]] * 2, axis=0)
    rows = jnp.where(face_side == 1, far, near)
    for bit in range(shift_bits(lines, tile_rows)):
        moved = pltpu.roll(rows, lines - (tile_rows << bit), 1)
        rows = jnp.where((offset >> bit) & 1 == 1, moved, rows)
    return jnp.where(orient == 1, mirrored(rows), rows)


def packed_ghosts(found, field):
    row = rows_of((16, found.shape[-1]))
    low = found[field:field + 1]
    high = found[2 + field:3 + field]
    return jnp.where(row == 0, low, jnp.where(row == 1, high, 0.0)).astype(BF16)


def mix(rates, proton, carbon):
    lines = proton.shape[-1]
    first, second, cross = (spread(rates[0:1, at:at + 1], lines) for at in range(3))
    new_proton = proton - (first * proton + cross * carbon)
    new_carbon = carbon - (second * carbon + cross * proton)
    return new_proton, new_carbon


def next_layers_kernel(
    tile_rows, origin, rates, partner, face_side, orient, offset, blocks, corners, ends, inv_y, sent, ghosts):
    cells = ends.shape[-1]
    found = ghost_rows((partner, face_side, orient, offset), blocks, origin, tile_rows)
    row = rows_of((16, cells))
    swept = []
    for field in range(2):
        edge = ends[field].astype(F32)
        ghosts[field] = packed_ghosts(found, field)
        layers = []
        for end in range(2):
            lane = end * (cells - 1)
            value = corners[field][end:end + 1]
            for which in range(2):
                at = which * 2 + field
                value = value + edge[which:which + 1, lane:lane + 1] * found[at:at + 1]
            layers.append(value)
        two = jnp.where(row == 0, layers[0], jnp.where(row == 1, layers[1], 0.0)).astype(BF16)
        swept.append(lax.dot_general(two, inv_y[field], NT, preferred_element_type=F32)[0:8])
    new_proton, new_carbon = mix(rates, swept[0], swept[1])
    total = jnp.concatenate(
        [new_proton[0:1], new_carbon[0:1], new_proton[1:2], new_carbon[1:2]], axis=0
    ).astype(BF16)
    for slot in range(sent.shape[0]):
        sent[slot] = total


def second_sweep(rates, interior, ghosts, ends, inv_y, emit):
    lines = inv_y.shape[-2]
    swept = []
    for field in range(2):
        outer = lax.dot_general(ghosts[field], ends[field], TN, preferred_element_type=F32)
        swept.append((interior(field) + outer).astype(BF16))
    chunk = lines // 2
    for start in range(0, lines, chunk):
        moved = [
            jnp.dot(inv_y[field, start:start + chunk], swept[field], preferred_element_type=F32)
            for field in range(2)
        ]
        new = mix(rates, moved[0], moved[1])
        for field in range(2):
            emit(field, start, chunk, new[field].astype(BF16))


def middle_kernel(tile_rows, tile0, rates, planes, ghosts, ends, inv_y, inv_x, following):
    def interior(field):
        plane = in_order(planes[:, field], tile0)
        return lax.dot_general(plane, inv_x[field], NT, preferred_element_type=F32)

    def emit(field, start, chunk, values):
        rows = lax.dot_general(values, inv_x[field], NT, preferred_element_type=F32)
        rows = rows.astype(BF16).reshape(-1, tile_rows, rows.shape[-1])
        first = start // tile_rows
        following[first:first + rows.shape[0], field] = rows

    second_sweep(rates, interior, ghosts, ends, inv_y, emit)


def last_kernel(
    tile_rows, tile0, origin, rates, partner, face_side, orient, offset, blocks, interior, ends,
    inv_y, planes,
):
    found = ghost_rows((partner, face_side, orient, offset), blocks, origin, tile_rows)
    ghosts = [packed_ghosts(found, field) for field in range(2)]

    def whole(field):
        return interior[:, field].reshape(-1, interior.shape[-1]).astype(F32)

    def emit(field, start, chunk, values):
        count = planes.shape[0]
        for row in range(0, chunk, tile_rows):
            place = ((start + row) // tile_rows + count - tile0) % count
            planes[place, field] = values[row:row + tile_rows]

    second_sweep(rates, whole, ghosts, ends, inv_y, emit)


def cost(flops, nbytes):
    return pl.CostEstimate(flops=flops, bytes_accessed=nbytes, transcendentals=0)


def local(state, inverse_x, inverse_y, rates, partner, face_side, orient, offset):
    magnet = state[0]
    inv_x = inverse_x[0]
    inv_y = inverse_y[0]
    fields, depth, tile_rows, cells = magnet.shape
    lines = inv_y.shape[-1]
    count = lax.axis_size("blk")
    width = lax.axis_size("pen")
    tile0 = (width * 21) // 32
    origin = (count * 5) // 8
    across = turned_group(count, origin)
    within = turned_group(width, tile0)
    numbers = (rates, partner, face_side, orient, offset)
    slots = jax.ShapeDtypeStruct((count, SLOT_ROWS, lines), BF16)
    packed = jax.ShapeDtypeStruct((fields, 16, lines), BF16)
    sweep_flops = 2 * fields * lines * cells * cells
    array_bytes = 2 * fields * lines * cells

    staged, ends, probe = pl.pallas_call(
        stage_kernel,
        out_shape=(
            jax.ShapeDtypeStruct((depth, fields, tile_rows, cells), BF16),
            packed,
            packed,
        ),
        in_specs=[HBM] * 2,
        out_specs=(VMEM,) * 3,
        scratch_shapes=[
            pltpu.VMEM((fields, 2, cells, 128), BF16),
            pltpu.VMEM((fields, 2, 16, cells), BF16),
            pltpu.SemaphoreType.DMA((10,)),
        ],
        compiler_params=pltpu.CompilerParams(vmem_limit_bytes=52 * 1024 * 1024),
        name="stage",
    )(magnet, inv_x)
    moved = lax.all_to_all(staged, "pen", split_axis=0, concat_axis=0, tiled=True, axis_index_groups=within)
    sent, corners = pl.pallas_call(
        functools.partial(layers_kernel, tile0),
        out_shape=(slots, jax.ShapeDtypeStruct((fields, 8, lines), F32)),
        in_specs=[VMEM, VMEM],
        out_specs=(VMEM, VMEM),
        compiler_params=params(),
        cost_estimate=cost(sweep_flops // 16, array_bytes),
        name="layers",
    )(moved, probe)
    blocks = lax.all_to_all(sent, "blk", split_axis=0, concat_axis=0, tiled=True, axis_index_groups=across)
    sent, ghosts = pl.pallas_call(
        functools.partial(next_layers_kernel, tile_rows, origin),
        out_shape=(slots, packed),
        in_specs=[VMEM] * 9,
        out_specs=(VMEM, VMEM),
        compiler_params=params(),
        cost_estimate=cost(sweep_flops // 16, array_bytes),
        name="next_layers",
    )(*numbers, blocks, corners, ends, inv_y)
    blocks = lax.all_to_all(sent, "blk", split_axis=0, concat_axis=0, tiled=True, axis_index_groups=across)
    interior = pl.pallas_call(
        functools.partial(middle_kernel, tile_rows, tile0),
        out_shape=jax.ShapeDtypeStruct(moved.shape, BF16),
        input_output_aliases={1: 0},
        in_specs=[VMEM] * 6,
        out_specs=VMEM,
        compiler_params=params(),
        cost_estimate=cost(3 * sweep_flops, 4 * array_bytes),
        name="middle",
    )(rates, moved, ghosts, ends, inv_y, inv_x)
    planes = pl.pallas_call(
        functools.partial(last_kernel, tile_rows, tile0, origin),
        out_shape=jax.ShapeDtypeStruct((lines // tile_rows, fields, tile_rows, cells), BF16),
        in_specs=[VMEM] * 9,
        out_specs=VMEM,
        compiler_params=params(),
        cost_estimate=cost(sweep_flops, 4 * array_bytes),
        name="last",
    )(*numbers, blocks, interior, ends, inv_y)
    back = lax.all_to_all(planes, "pen", split_axis=0, concat_axis=0, tiled=True, axis_index_groups=within)
    return from_planes(back)[None]


def solution(mesh):
    return jax.shard_map(
        local,
        mesh=mesh,
        in_specs=(
            P("blk", None, None, "pen", None),
            P("blk", None, None, None),
            P("blk", None, None, None),
            P("blk", None),
            P("blk", None),
            P("blk", None),
            P("blk", None),
            P("blk", None),
        ),
        out_specs=P("blk", None, None, "pen", None),
        check_vma=False,
    )
```

time: 88.3 us -> 87.9 us (level)
  blocking collectives: 49.3 us -> 66.4 us
  starting transfers between devices: 23 us -> 10.1 us
  waiting for transfers between devices: 5.39 us -> 2.51 us
  Pallas kernels: 9.56 us -> 8.44 us
    all_to_all x1 -> x2, blocking collectives: 26.1 us -> 43.5 us  [the longest x1 26 us: local(): lax.all_to_all(staged, 'pen', split_axis=0, concat_axis=0, tiled=True, ax...]
    all_to_all x2 -> x1, starting transfers between devices: 23 us -> 10.1 us  [local(): lax.all_to_all(sent, 'blk', split_axis=0, concat_axis=0, tiled=True, axis...]
    all_to_all x2 -> x1, waiting for transfers between devices: 5.39 us -> 2.51 us  [local(): lax.all_to_all(sent, 'blk', split_axis=0, concat_axis=0, tiled=True, axis...]
    pallas_call x6 -> x4, Pallas kernels: 6.22 us -> 5.08 us  [the longest x1 1.74 us: local(): pl.pallas_call(stage_kernel, out_shape=(jax.ShapeDtypeStruct((depth, fiel...]
  transfers between devices with their start and end apart: 2 -> 1, of which waited for: 2 -> 1; matrix products, arithmetic and copies ran while one was open for 0% -> 0% of each run, Pallas kernels for 4% -> 3%
where the time goes in v7:
time: 87.9 us; the launch traced here: 87.6 us
  blocking collectives  66.4 us (76%)
  starting transfers between devices  10.1 us (11%)
  Pallas kernels  8.44 us (10%)
  waiting for transfers between devices  2.51 us (3%)
    all_to_all x1, blocking collectives, local(): lax.all_to_all(staged, 'pen', split_axis=0, concat_axis=0, tiled=True, ax...  26 us
    all_to_all x1, blocking collectives, local(): lax.all_to_all(planes, 'pen', split_axis=0, concat_axis=0, tiled=True, ax...  22.9 us
    all_to_all x1, blocking collectives, local(): lax.all_to_all(sent, 'blk', split_axis=0, concat_axis=0, tiled=True, axis...  17.6 us
    all_to_all x1, starting transfers between devices, local(): lax.all_to_all(sent, 'blk', split_axis=0, concat_axis=0, tiled=True, axis...  10.1 us
    all_to_all x1, waiting for transfers between devices, local(): lax.all_to_all(sent, 'blk', split_axis=0, concat_axis=0, tiled=True, axis...  2.51 us
    pallas_call x1, Pallas kernels, local(): pl.pallas_call(functools.partial(middle_kernel, tile_rows, tile0), out_sh...  2.38 us
  transfers between devices with their start and end apart: 1, of which 1 were waited for; matrix products, arithmetic and copies ran while one was open for 0% of the time, Pallas kernels for 3%

profile of v7, /device:TPU:1, one launch (start us, length us, event | category | flops | bytes accessed | tf_op | source)
XLA Modules:
  0.0 87.6 jit_solution(16968273752261376461)
XLA Ops:
  0.0 1.7 %stage.1 = (bf16[32,2,16,512]{3,2,1,0:T(8,128)(2,1)S(1)}, bf16[2,16,512]{2,1,0:T(8,128)(2,1)S(1)}, bf16[2,16,512]{2,1,0:T(8,128)(2,1)S(1)}) custom-call(bf16[2,32,16,512]{3,2,1,0:T(8,128)(2,1)} %bitcast.9, bf16[2,512,512]{2,1,0:T(8,128)(2,1)} %bitcast.7), custom_call_target="tpu_custom_call" | custom-call | tf_op jit(solution)/shard_map/stage/pallas_call | solution.py:282
  1.7 0.0 copy-start.2
  1.8 0.0 copy-start.3
  1.8 0.0 copy-start.4
  1.8 0.0 copy-start.5
  1.8 0.0 copy-start.6
  1.8 26.0 %all_to_all.20.planes = bf16[32,2,16,512]{3,2,1,0:T(8,128)(2,1)S(1)} all-to-all(bf16[32,2,16,512]{3,2,1,0:T(8,128)(2,1)S(1)} %get-tuple-element.12), channel_id=1, replica_groups={{21,22,23,24,25,26,27,28,29,30,31,0,1,2,3,4,5,6,7,8,9,10,11,12,13,14,15..., dimensions={0} | all-to-all | bytes 2097152 | tf_op jit(solution)/shard_map/all_to_all | solution.py:299
  27.8 0.0 copy-start
  27.8 0.0 copy-start.1
  27.8 0.4 layers.1
  28.2 17.6 %all_to_all.21.blocks = bf16[16,4,512]{2,1,0:T(4,128)(2,1)S(1)} all-to-all(bf16[16,4,512]{2,1,0:T(4,128)(2,1)S(1)} %get-tuple-element.14), channel_id=1, replica_groups={{320,352,384,416,448,480,0,32,64,96,128,160,192,224,256,288},{321,353,3..., dimensions={0} | all-to-all | bytes 131072 | tf_op jit(solution)/shard_map/all_to_all | solution.py:309
  45.8 0.0 copy-done.2
  45.8 0.0 copy-done.3
  45.8 0.0 copy-done.4
  45.8 0.0 copy-done.5
  45.8 0.0 copy-done.6
  45.8 0.0 copy-done
  45.8 1.4 %next_layers.1 = (bf16[16,4,512]{2,1,0:T(4,128)(2,1)}, bf16[2,16,512]{2,1,0:T(8,128)(2,1)S(1)}) custom-call(f32[1,3]{1,0:T(1,128)S(1)} %copy-done.2, s32[1,2]{1,0:T(1,128)S(1)} %copy-done.3, s32[1,2]{1,0:T(1,128)S(1)} %copy-done.4, s32[1,2]{1,0:T(1,128)S(1)} %copy-done.5, s32[1,2]{1,0:T(1,128)S(1)} %copy-done.6, bf16[16,4,512]{2,1,0:T(4,128)(2,1)S(1)} %all_to_all.21.blocks, ...), custom_call_target="tpu_custom_call" | custom-call | flops 33554432 | bytes 1048576 | tf_op jit(solution)/shard_map/next_layers/pallas_call | solution.py:310
  47.2 10.1 %all-to-all-start.2 = ((bf16[16,4,512]{2,1,0:T(4,128)(2,1)}), bf16[16,4,512]{2,1,0:T(4,128)(2,1)S(1)}, u32[]{:S(2)}, u32[]{:S(2)}) async-start(bf16[16,4,512]{2,1,0:T(4,128)(2,1)} %get-tuple-element.17), calls=%async_computation.2 | async-start | bytes 131072 | tf_op jit(solution)/shard_map/all_to_all | solution.py:319
  57.3 0.0 copy-done.1
  57.3 2.4 %middle.1.interior = bf16[32,2,16,512]{3,2,1,0:T(8,128)(2,1)S(1)} custom-call(f32[1,3]{1,0:T(1,128)S(1)} %copy-done.2, bf16[32,2,16,512]{3,2,1,0:T(8,128)(2,1)S(1)} %all_to_all.20.planes, bf16[2,16,512]{2,1,0:T(8,128)(2,1)S(1)} %get-tuple-element.18.ghosts, bf16[2,16,512]{2,1,0:T(8,128)(2,1)S(1)} %get-tuple-element.16.ends, ...), custom_call_target="tpu_custom_call", output_to_operand_aliasing={{}: (1, {})} | custom-call | flops 1610612736 | bytes 4194304 | tf_op jit(solution)/shard_map/middle/pallas_call | solution.py:320
  59.7 2.5 %all-to-all-done.2.blocks = bf16[16,4,512]{2,1,0:T(4,128)(2,1)S(1)} async-done(((bf16[16,4,512]{2,1,0:T(4,128)(2,1)}), bf16[16,4,512]{2,1,0:T(4,128)(2,1)S(1)}, u32[]{:S(2)}, u32[]{:S(2)}) %all-to-all-start.2) | async-done | bytes 65568 | tf_op jit(solution)/shard_map/all_to_all | solution.py:319
  62.2 1.6 %last.1 = bf16[32,2,16,512]{3,2,1,0:T(8,128)(2,1)S(1)} custom-call(f32[1,3]{1,0:T(1,128)S(1)} %copy-done.2, s32[1,2]{1,0:T(1,128)S(1)} %copy-done.3, s32[1,2]{1,0:T(1,128)S(1)} %copy-done.4, s32[1,2]{1,0:T(1,128)S(1)} %copy-done.5, s32[1,2]{1,0:T(1,128)S(1)} %copy-done.6, bf16[16,4,512]{2,1,0:T(4,128)(2,1)S(1)} %all-to-all-done.2.blocks, ...), custom_call_target="tpu_custom_call" | custom-call | flops 536870912 | bytes 4194304 | tf_op jit(solution)/shard_map/last/pallas_call | solution.py:330
  63.8 22.9 %all_to_all.22.source = bf16[32,2,16,512]{3,2,1,0:T(8,128)(2,1)S(1)} all-to-all(bf16[32,2,16,512]{3,2,1,0:T(8,128)(2,1)S(1)} %last.1), channel_id=1, replica_groups={{21,22,23,24,25,26,27,28,29,30,31,0,1,2,3,4,5,6,7,8,9,10,11,12,13,14,15..., dimensions={0} | all-to-all | bytes 2097152 | tf_op jit(solution)/shard_map/all_to_all | solution.py:339
  86.6 1.0 %from_planes.1 = bf16[2,32,16,512]{3,2,1,0:T(8,128)(2,1)} custom-call(bf16[32,2,16,512]{3,2,1,0:T(8,128)(2,1)S(1)} %all_to_all.22.source), custom_call_target="tpu_custom_call" | custom-call | tf_op jit(solution)/shard_map/from_planes/pallas_call | solution.py:59
Async XLA Ops:
  1.7 44.0 %copy-start.2 = (f32[1,3]{1,0:T(1,128)S(1)}, f32[1,3]{1,0:T(1,128)}, u32[]{:S(2)}) copy-start(f32[1,3]{1,0:T(1,128)} %rates.5) | copy-start | bytes 40
  1.8 44.0 %copy-start.3 = (s32[1,2]{1,0:T(1,128)S(1)}, s32[1,2]{1,0:T(1,128)}, u32[]{:S(2)}) copy-start(s32[1,2]{1,0:T(1,128)} %partner.3) | copy-start | bytes 28
  1.8 44.0 %copy-start.4 = (s32[1,2]{1,0:T(1,128)S(1)}, s32[1,2]{1,0:T(1,128)}, u32[]{:S(2)}) copy-start(s32[1,2]{1,0:T(1,128)} %face_side.3) | copy-start | bytes 28
  1.8 44.0 %copy-start.5 = (s32[1,2]{1,0:T(1,128)S(1)}, s32[1,2]{1,0:T(1,128)}, u32[]{:S(2)}) copy-start(s32[1,2]{1,0:T(1,128)} %orient.3) | copy-start | bytes 28
  1.8 44.0 %copy-start.6 = (s32[1,2]{1,0:T(1,128)S(1)}, s32[1,2]{1,0:T(1,128)}, u32[]{:S(2)}) copy-start(s32[1,2]{1,0:T(1,128)} %offset.3) | copy-start | bytes 28
  27.8 18.0 %copy-start = (bf16[1,2,512,512]{3,2,1,0:T(8,128)(2,1)S(1)}, bf16[1,2,512,512]{3,2,1,0:T(8,128)(2,1)}, u32[]{:S(2)}) copy-start(bf16[1,2,512,512]{3,2,1,0:T(8,128)(2,1)} %param.10) | copy-start | bytes 3145732
  27.8 29.5 %copy-start.1 = (bf16[1,2,512,512]{3,2,1,0:T(8,128)(2,1)S(1)}, bf16[1,2,512,512]{3,2,1,0:T(8,128)(2,1)}, u32[]{:S(2)}) copy-start(bf16[1,2,512,512]{3,2,1,0:T(8,128)(2,1)} %param.9) | copy-start | bytes 3145732
  47.2 15.0 %all-to-all-start.2 = ((bf16[16,4,512]{2,1,0:T(4,128)(2,1)}), bf16[16,4,512]{2,1,0:T(4,128)(2,1)S(1)}, u32[]{:S(2)}, u32[]{:S(2)}) async-start(bf16[16,4,512]{2,1,0:T(4,128)(2,1)} %get-tuple-element.17), calls=%async_computation.2 | async-start | bytes 131072 | tf_op jit(solution)/shard_map/all_to_all | solution.py:319

commit v8 on v7

--- a/solution.py
+++ b/solution.py
@@ -77,12 +77,11 @@
     return (lines // tile_rows).bit_length() - 1
 
 
-def stage_kernel(state, inv_x, planes, ends, probe, sides, tops, sems):
+def stage_kernel(state, inv_x, planes, probe, tops, sems):
     cells = inv_x.shape[-1]
     pairs = pieces_of(state, planes, 1)
     for field in range(2):
         for end in range(2):
-            pairs.append((inv_x.at[field, :, pl.ds(end * (cells - 128), 128)], sides.at[field, end]))
             pairs.append((inv_x.at[field, pl.ds(end * (cells - 16), 16)], tops.at[field, end]))
     copies = [
         pltpu.make_async_copy(source, target, sems.at[number])
@@ -93,17 +92,11 @@
     for copy in copies[2:]:
         copy.wait()
 
-    lane = lax.broadcasted_iota(jnp.int32, (16, 256), 1)
-    row = rows_of((16, 256))
-    pick = ((row == 0) & (lane == 0)) | ((row == 1) & (lane == 255))
-    pick = jnp.where(pick, 1.0, 0.0).astype(BF16)
     row = rows_of((16, cells))
     lane = lax.broadcasted_iota(jnp.int32, (16, cells), 1)
     hot = ((row == 2) & (lane == 0)) | ((row == 3) & (lane == cells - 1))
     hot = jnp.where(hot, 1.0, 0.0)
     for field in range(2):
-        both = jnp.concatenate([sides[field, 0], sides[field, 1]], axis=1)
-        ends[field] = lax.dot_general(pick, both, NT, preferred_element_type=F32).astype(BF16)
         first = tops[field, 0].astype(F32)[0:1]
         last = tops[field, 1].astype(F32)[15:16]
         probe[field] = jnp.where(row == 0, first, jnp.where(row == 1, last, hot)).astype(BF16)
@@ -181,21 +174,21 @@
 
 
 def next_layers_kernel(
-    tile_rows, origin, rates, partner, face_side, orient, offset, blocks, corners, ends, inv_y, sent, ghosts):
-    cells = ends.shape[-1]
+    tile_rows, origin, rates, partner, face_side, orient, offset, blocks, corners, probe, inv_y, sent, ghosts):
+    cells = probe.shape[-1]
     found = ghost_rows((partner, face_side, orient, offset), blocks, origin, tile_rows)
     row = rows_of((16, cells))
     swept = []
     for field in range(2):
-        edge = ends[field].astype(F32)
+        edge = probe[field].astype(F32)
         ghosts[field] = packed_ghosts(found, field)
         layers = []
         for end in range(2):
-            lane = end * (cells - 1)
             value = corners[field][end:end + 1]
             for which in range(2):
                 at = which * 2 + field
-                value = value + edge[which:which + 1, lane:lane + 1] * found[at:at + 1]
+                lane = which * (cells - 1)
+                value = value + edge[end:end + 1, lane:lane + 1] * found[at:at + 1]
             layers.append(value)
         two = jnp.where(row == 0, layers[0], jnp.where(row == 1, layers[1], 0.0)).astype(BF16)
         swept.append(lax.dot_general(two, inv_y[field], NT, preferred_element_type=F32)[0:8])
@@ -224,7 +217,19 @@
             emit(field, start, chunk, new[field].astype(BF16))
 
 
-def middle_kernel(tile_rows, tile0, rates, planes, ghosts, ends, inv_y, inv_x, following):
+def middle_kernel(tile_rows, tile0, rates, planes, ghosts, inv_y, inv_x, following, ends):
+    cells = inv_x.shape[-1]
+    row = rows_of((16, cells))
+    lane = lax.broadcasted_iota(jnp.int32, (16, cells), 1)
+    pick = ((row == 0) & (lane == 0)) | ((row == 1) & (lane == cells - 1))
+    pick = jnp.where(pick, 1.0, 0.0).astype(BF16)
+    columns = [
+        lax.dot_general(pick, inv_x[field], NT, preferred_element_type=F32).astype(BF16)
+        for field in range(2)
+    ]
+    for field in range(2):
+        ends[field] = columns[field]
+
     def interior(field):
         plane = in_order(planes[:, field], tile0)
         return lax.dot_general(plane, inv_x[field], NT, preferred_element_type=F32)
@@ -235,7 +240,7 @@
         first = start // tile_rows
         following[first:first + rows.shape[0], field] = rows
 
-    second_sweep(rates, interior, ghosts, ends, inv_y, emit)
+    second_sweep(rates, interior, ghosts, columns, inv_y, emit)
 
 
 def last_kernel(
@@ -279,19 +284,17 @@
     sweep_flops = 2 * fields * lines * cells * cells
     array_bytes = 2 * fields * lines * cells
 
-    staged, ends, probe = pl.pallas_call(
+    staged, probe = pl.pallas_call(
         stage_kernel,
         out_shape=(
             jax.ShapeDtypeStruct((depth, fields, tile_rows, cells), BF16),
             packed,
-            packed,
         ),
         in_specs=[HBM] * 2,
-        out_specs=(VMEM,) * 3,
+        out_specs=(VMEM,) * 2,
         scratch_shapes=[
-            pltpu.VMEM((fields, 2, cells, 128), BF16),
             pltpu.VMEM((fields, 2, 16, cells), BF16),
-            pltpu.SemaphoreType.DMA((10,)),
+            pltpu.SemaphoreType.DMA((6,)),
         ],
         compiler_params=pltpu.CompilerParams(vmem_limit_bytes=52 * 1024 * 1024),
         name="stage",
@@ -315,18 +318,18 @@
         compiler_params=params(),
         cost_estimate=cost(sweep_flops // 16, array_bytes),
         name="next_layers",
-    )(*numbers, blocks, corners, ends, inv_y)
+    )(*numbers, blocks, corners, probe, inv_y)
     blocks = lax.all_to_all(sent, "blk", split_axis=0, concat_axis=0, tiled=True, axis_index_groups=across)
-    interior = pl.pallas_call(
+    interior, ends = pl.pallas_call(
         functools.partial(middle_kernel, tile_rows, tile0),
-        out_shape=jax.ShapeDtypeStruct(moved.shape, BF16),
+        out_shape=(jax.ShapeDtypeStruct(moved.shape, BF16), packed),
         input_output_aliases={1: 0},
-        in_specs=[VMEM] * 6,
-        out_specs=VMEM,
+        in_specs=[VMEM] * 5,
+        out_specs=(VMEM, VMEM),
         compiler_params=params(),
         cost_estimate=cost(3 * sweep_flops, 4 * array_bytes),
         name="middle",
-    )(rates, moved, ghosts, ends, inv_y, inv_x)
+    )(rates, moved, ghosts, inv_y, inv_x)
     planes = pl.pallas_call(
         functools.partial(last_kernel, tile_rows, tile0, origin),
         out_shape=jax.ShapeDtypeStruct((lines // tile_rows, fields, tile_rows, cells), BF16),

time: 87.9 us -> 87.5 us (level)
  no operation moved by 1% of the time
where the time goes in v8:
time: 87.5 us; the launch traced here: 87.1 us
  blocking collectives  66.4 us (76%)
  starting transfers between devices  10.1 us (12%)
  Pallas kernels  8.17 us (9%)
  waiting for transfers between devices  2.29 us (3%)
    all_to_all x1, blocking collectives, local(): lax.all_to_all(staged, 'pen', split_axis=0, concat_axis=0, tiled=True, ax...  26 us
    all_to_all x1, blocking collectives, local(): lax.all_to_all(planes, 'pen', split_axis=0, concat_axis=0, tiled=True, ax...  22.9 us
    all_to_all x1, blocking collectives, local(): lax.all_to_all(sent, 'blk', split_axis=0, concat_axis=0, tiled=True, axis...  17.6 us
    all_to_all x1, starting transfers between devices, local(): lax.all_to_all(sent, 'blk', split_axis=0, concat_axis=0, tiled=True, axis...  10.1 us
    pallas_call x1, Pallas kernels, local(): pl.pallas_call(functools.partial(middle_kernel, tile_rows, tile0), out_sh...  2.6 us
    all_to_all x1, waiting for transfers between devices, local(): lax.all_to_all(sent, 'blk', split_axis=0, concat_axis=0, tiled=True, axis...  2.29 us
  transfers between devices with their start and end apart: 1, of which 1 were waited for; matrix products, arithmetic and copies ran while one was open for 0% of the time, Pallas kernels for 3%

profile of v8, /device:TPU:1, one launch (start us, length us, event | category | flops | bytes accessed | tf_op | source)
XLA Modules:
  0.0 87.1 jit_solution(6261156033762869732)
XLA Ops:
  0.0 1.3 %stage.1 = (bf16[32,2,16,512]{3,2,1,0:T(8,128)(2,1)S(1)}, bf16[2,16,512]{2,1,0:T(8,128)(2,1)S(1)}) custom-call(bf16[2,32,16,512]{3,2,1,0:T(8,128)(2,1)} %bitcast.9, bf16[2,512,512]{2,1,0:T(8,128)(2,1)} %bitcast.7), custom_call_target="tpu_custom_call" | custom-call | tf_op jit(solution)/shard_map/stage/pallas_call | solution.py:287
  1.3 0.0 copy-start.2
  1.3 0.0 copy-start.3
  1.3 0.0 copy-start.4
  1.3 0.0 copy-start.5
  1.3 0.0 copy-start.6
  1.3 26.0 %all_to_all.20.planes = bf16[32,2,16,512]{3,2,1,0:T(8,128)(2,1)S(1)} all-to-all(bf16[32,2,16,512]{3,2,1,0:T(8,128)(2,1)S(1)} %get-tuple-element.13), channel_id=1, replica_groups={{21,22,23,24,25,26,27,28,29,30,31,0,1,2,3,4,5,6,7,8,9,10,11,12,13,14,15..., dimensions={0} | all-to-all | bytes 2097152 | tf_op jit(solution)/shard_map/all_to_all | solution.py:302
  27.3 0.0 copy-start
  27.3 0.0 copy-start.1
  27.3 0.4 layers.1
  27.7 17.6 %all_to_all.21.blocks = bf16[16,4,512]{2,1,0:T(4,128)(2,1)S(1)} all-to-all(bf16[16,4,512]{2,1,0:T(4,128)(2,1)S(1)} %get-tuple-element.15), channel_id=1, replica_groups={{320,352,384,416,448,480,0,32,64,96,128,160,192,224,256,288},{321,353,3..., dimensions={0} | all-to-all | bytes 131072 | tf_op jit(solution)/shard_map/all_to_all | solution.py:312
  45.3 0.0 copy-done.2
  45.3 0.0 copy-done.3
  45.3 0.0 copy-done.4
  45.3 0.0 copy-done.5
  45.3 0.0 copy-done.6
  45.3 0.0 copy-done
  45.3 1.4 %next_layers.1 = (bf16[16,4,512]{2,1,0:T(4,128)(2,1)}, bf16[2,16,512]{2,1,0:T(8,128)(2,1)S(1)}) custom-call(f32[1,3]{1,0:T(1,128)S(1)} %copy-done.2, s32[1,2]{1,0:T(1,128)S(1)} %copy-done.3, s32[1,2]{1,0:T(1,128)S(1)} %copy-done.4, s32[1,2]{1,0:T(1,128)S(1)} %copy-done.5, s32[1,2]{1,0:T(1,128)S(1)} %copy-done.6, bf16[16,4,512]{2,1,0:T(4,128)(2,1)S(1)} %all_to_all.21.blocks, ...), custom_call_target="tpu_custom_call" | custom-call | flops 33554432 | bytes 1048576 | tf_op jit(solution)/shard_map/next_layers/pallas_call | solution.py:313
  46.7 10.1 %all-to-all-start.2 = ((bf16[16,4,512]{2,1,0:T(4,128)(2,1)}), bf16[16,4,512]{2,1,0:T(4,128)(2,1)S(1)}, u32[]{:S(2)}, u32[]{:S(2)}) async-start(bf16[16,4,512]{2,1,0:T(4,128)(2,1)} %get-tuple-element.17), calls=%async_computation.2 | async-start | bytes 131072 | tf_op jit(solution)/shard_map/all_to_all | solution.py:322
  56.8 0.0 copy-done.1
  56.8 2.6 %middle.1 = (bf16[32,2,16,512]{3,2,1,0:T(8,128)(2,1)S(1)}, bf16[2,16,512]{2,1,0:T(8,128)(2,1)S(1)}) custom-call(f32[1,3]{1,0:T(1,128)S(1)} %copy-done.2, bf16[32,2,16,512]{3,2,1,0:T(8,128)(2,1)S(1)} %all_to_all.20.planes, bf16[2,16,512]{2,1,0:T(8,128)(2,1)S(1)} %get-tuple-element.18.ghosts, ...), custom_call_target="tpu_custom_call", output_to_operand_aliasing={{0}: (1, {})} | custom-call | flops 1610612736 | bytes 4194304 | tf_op jit(solution)/shard_map/middle/pallas_call | solution.py:323
  59.4 2.3 %all-to-all-done.2.blocks = bf16[16,4,512]{2,1,0:T(4,128)(2,1)S(1)} async-done(((bf16[16,4,512]{2,1,0:T(4,128)(2,1)}), bf16[16,4,512]{2,1,0:T(4,128)(2,1)S(1)}, u32[]{:S(2)}, u32[]{:S(2)}) %all-to-all-start.2) | async-done | bytes 65568 | tf_op jit(solution)/shard_map/all_to_all | solution.py:322
  61.7 1.6 %last.1 = bf16[32,2,16,512]{3,2,1,0:T(8,128)(2,1)S(1)} custom-call(f32[1,3]{1,0:T(1,128)S(1)} %copy-done.2, s32[1,2]{1,0:T(1,128)S(1)} %copy-done.3, s32[1,2]{1,0:T(1,128)S(1)} %copy-done.4, s32[1,2]{1,0:T(1,128)S(1)} %copy-done.5, s32[1,2]{1,0:T(1,128)S(1)} %copy-done.6, bf16[16,4,512]{2,1,0:T(4,128)(2,1)S(1)} %all-to-all-done.2.blocks, ...), custom_call_target="tpu_custom_call" | custom-call | flops 536870912 | bytes 4194304 | tf_op jit(solution)/shard_map/last/pallas_call | solution.py:333
  63.3 22.9 %all_to_all.22.source = bf16[32,2,16,512]{3,2,1,0:T(8,128)(2,1)S(1)} all-to-all(bf16[32,2,16,512]{3,2,1,0:T(8,128)(2,1)S(1)} %last.1), channel_id=1, replica_groups={{21,22,23,24,25,26,27,28,29,30,31,0,1,2,3,4,5,6,7,8,9,10,11,12,13,14,15..., dimensions={0} | all-to-all | bytes 2097152 | tf_op jit(solution)/shard_map/all_to_all | solution.py:342
  86.1 1.0 %from_planes.1 = bf16[2,32,16,512]{3,2,1,0:T(8,128)(2,1)} custom-call(bf16[32,2,16,512]{3,2,1,0:T(8,128)(2,1)S(1)} %all_to_all.22.source), custom_call_target="tpu_custom_call" | custom-call | tf_op jit(solution)/shard_map/from_planes/pallas_call | solution.py:59
Async XLA Ops:
  1.3 44.0 %copy-start.2 = (f32[1,3]{1,0:T(1,128)S(1)}, f32[1,3]{1,0:T(1,128)}, u32[]{:S(2)}) copy-start(f32[1,3]{1,0:T(1,128)} %rates.5) | copy-start | bytes 40
  1.3 44.0 %copy-start.3 = (s32[1,2]{1,0:T(1,128)S(1)}, s32[1,2]{1,0:T(1,128)}, u32[]{:S(2)}) copy-start(s32[1,2]{1,0:T(1,128)} %partner.3) | copy-start | bytes 28
  1.3 44.0 %copy-start.4 = (s32[1,2]{1,0:T(1,128)S(1)}, s32[1,2]{1,0:T(1,128)}, u32[]{:S(2)}) copy-start(s32[1,2]{1,0:T(1,128)} %face_side.3) | copy-start | bytes 28
  1.3 44.0 %copy-start.5 = (s32[1,2]{1,0:T(1,128)S(1)}, s32[1,2]{1,0:T(1,128)}, u32[]{:S(2)}) copy-start(s32[1,2]{1,0:T(1,128)} %orient.3) | copy-start | bytes 28
  1.3 44.0 %copy-start.6 = (s32[1,2]{1,0:T(1,128)S(1)}, s32[1,2]{1,0:T(1,128)}, u32[]{:S(2)}) copy-start(s32[1,2]{1,0:T(1,128)} %offset.3) | copy-start | bytes 28
  27.3 18.0 %copy-start = (bf16[1,2,512,512]{3,2,1,0:T(8,128)(2,1)S(1)}, bf16[1,2,512,512]{3,2,1,0:T(8,128)(2,1)}, u32[]{:S(2)}) copy-start(bf16[1,2,512,512]{3,2,1,0:T(8,128)(2,1)} %param.10) | copy-start | bytes 3145732
  27.3 29.5 %copy-start.1 = (bf16[1,2,512,512]{3,2,1,0:T(8,128)(2,1)S(1)}, bf16[1,2,512,512]{3,2,1,0:T(8,128)(2,1)}, u32[]{:S(2)}) copy-start(bf16[1,2,512,512]{3,2,1,0:T(8,128)(2,1)} %param.9) | copy-start | bytes 3145732
  46.7 15.0 %all-to-all-start.2 = ((bf16[16,4,512]{2,1,0:T(4,128)(2,1)}), bf16[16,4,512]{2,1,0:T(4,128)(2,1)S(1)}, u32[]{:S(2)}, u32[]{:S(2)}) async-start(bf16[16,4,512]{2,1,0:T(4,128)(2,1)} %get-tuple-element.17), calls=%async_computation.2 | async-start | bytes 131072 | tf_op jit(solution)/shard_map/all_to_all | solution.py:322

commit v9 on v8

--- a/solution.py
+++ b/solution.py
@@ -137,11 +137,19 @@
     return jnp.concatenate(pieces, axis=1)
 
 
-def ghost_rows(tables, blocks, origin, tile_rows):
-    count, _, lines = blocks.shape
-    partner, face_side, orient, offset = (by_side(table, lines) for table in tables)
+def spread_tables(tables, count, lines, origin, tile_rows):
+    partner, face_side, orient, offset = (by_side(table, 128) for table in tables)
     place = partner - origin
     place = jnp.where(place < 0, place + count, place)
+    bits = (lines // tile_rows).bit_length() - 1
+    return [place, face_side, orient, *((offset >> bit) & 1 for bit in range(bits))]
+
+
+def ghost_rows(spreads, blocks, tile_rows):
+    count, _, lines = blocks.shape
+    place, face_side, orient, *bits = (
+        jnp.concatenate([piece] * (lines // 128), axis=1) for piece in spreads
+    )
     layers = []
     for which in range(2):
         wanted = place[2 * which:2 * which + 1]
@@ -152,9 +160,9 @@
     near = jnp.concatenate([layers[0][0:2], layers[1][0:2]] * 2, axis=0)
     far = jnp.concatenate([layers[0][2:4], layers[1][2:4]] * 2, axis=0)
     rows = jnp.where(face_side == 1, far, near)
-    for bit in range(shift_bits(lines, tile_rows)):
+    for bit, mark in enumerate(bits):
         moved = pltpu.roll(rows, lines - (tile_rows << bit), 1)
-        rows = jnp.where((offset >> bit) & 1 == 1, moved, rows)
+        rows = jnp.where(mark == 1, moved, rows)
     return jnp.where(orient == 1, mirrored(rows), rows)
 
 
@@ -176,7 +184,9 @@
 def next_layers_kernel(
     tile_rows, origin, rates, partner, face_side, orient, offset, blocks, corners, probe, inv_y, sent, ghosts):
     cells = probe.shape[-1]
-    found = ghost_rows((partner, face_side, orient, offset), blocks, origin, tile_rows)
+    tables = (partner, face_side, orient, offset)
+    spreads = spread_tables(tables, blocks.shape[0], cells, origin, tile_rows)
+    found = ghost_rows(spreads, blocks, tile_rows)
     row = rows_of((16, cells))
     swept = []
     for field in range(2):
@@ -217,7 +227,10 @@
             emit(field, start, chunk, new[field].astype(BF16))
 
 
-def middle_kernel(tile_rows, tile0, rates, planes, ghosts, inv_y, inv_x, following, ends):
+def middle_kernel(
+    tile_rows, tile0, origin, count, rates, partner, face_side, orient, offset, planes, ghosts,
+    inv_y, inv_x, following, ends, marks,
+):
     cells = inv_x.shape[-1]
     row = rows_of((16, cells))
     lane = lax.broadcasted_iota(jnp.int32, (16, cells), 1)
@@ -229,6 +242,9 @@
     ]
     for field in range(2):
         ends[field] = columns[field]
+    tables = (partner, face_side, orient, offset)
+    for at, piece in enumerate(spread_tables(tables, count, cells, origin, tile_rows)):
+        marks[at] = piece
 
     def interior(field):
         plane = in_order(planes[:, field], tile0)
@@ -243,11 +259,8 @@
     second_sweep(rates, interior, ghosts, columns, inv_y, emit)
 
 
-def last_kernel(
-    tile_rows, tile0, origin, rates, partner, face_side, orient, offset, blocks, interior, ends,
-    inv_y, planes,
-):
-    found = ghost_rows((partner, face_side, orient, offset), blocks, origin, tile_rows)
+def last_kernel(tile_rows, tile0, rates, marks, blocks, interior, ends, inv_y, planes):
+    found = ghost_rows([marks[at] for at in range(marks.shape[0])], blocks, tile_rows)
     ghosts = [packed_ghosts(found, field) for field in range(2)]
 
     def whole(field):
@@ -320,25 +333,30 @@
         name="next_layers",
     )(*numbers, blocks, corners, probe, inv_y)
     blocks = lax.all_to_all(sent, "blk", split_axis=0, concat_axis=0, tiled=True, axis_index_groups=across)
-    interior, ends = pl.pallas_call(
-        functools.partial(middle_kernel, tile_rows, tile0),
-        out_shape=(jax.ShapeDtypeStruct(moved.shape, BF16), packed),
-        input_output_aliases={1: 0},
-        in_specs=[VMEM] * 5,
-        out_specs=(VMEM, VMEM),
+    marks = 3 + (lines // tile_rows).bit_length() - 1
+    interior, ends, marks = pl.pallas_call(
+        functools.partial(middle_kernel, tile_rows, tile0, origin, count),
+        out_shape=(
+            jax.ShapeDtypeStruct(moved.shape, BF16),
+            packed,
+            jax.ShapeDtypeStruct((marks, 8, 128), jnp.int32),
+        ),
+        input_output_aliases={5: 0},
+        in_specs=[VMEM] * 9,
+        out_specs=(VMEM, VMEM, VMEM),
         compiler_params=params(),
         cost_estimate=cost(3 * sweep_flops, 4 * array_bytes),
         name="middle",
-    )(rates, moved, ghosts, inv_y, inv_x)
+    )(*numbers, moved, ghosts, inv_y, inv_x)
     planes = pl.pallas_call(
-        functools.partial(last_kernel, tile_rows, tile0, origin),
+        functools.partial(last_kernel, tile_rows, tile0),
         out_shape=jax.ShapeDtypeStruct((lines // tile_rows, fields, tile_rows, cells), BF16),
-        in_specs=[VMEM] * 9,
+        in_specs=[VMEM] * 6,
         out_specs=VMEM,
         compiler_params=params(),
         cost_estimate=cost(sweep_flops, 4 * array_bytes),
         name="last",
-    )(*numbers, blocks, interior, ends, inv_y)
+    )(rates, marks, blocks, interior, ends, inv_y)
     back = lax.all_to_all(planes, "pen", split_axis=0, concat_axis=0, tiled=True, axis_index_groups=within)
     return from_planes(back)[None]
 

time: 87.5 us -> 87.4 us (level)
  no operation moved by 1% of the time
where the time goes in v9:
time: 87.4 us; the launch traced here: 87.1 us
  blocking collectives  66.4 us (76%)
  starting transfers between devices  10.1 us (12%)
  Pallas kernels  8.11 us (9%)
  waiting for transfers between devices  2.28 us (3%)
    all_to_all x1, blocking collectives, local(): lax.all_to_all(staged, 'pen', split_axis=0, concat_axis=0, tiled=True, ax...  26 us
    all_to_all x1, blocking collectives, local(): lax.all_to_all(planes, 'pen', split_axis=0, concat_axis=0, tiled=True, ax...  22.9 us
    all_to_all x1, blocking collectives, local(): lax.all_to_all(sent, 'blk', split_axis=0, concat_axis=0, tiled=True, axis...  17.6 us
    all_to_all x1, starting transfers between devices, local(): lax.all_to_all(sent, 'blk', split_axis=0, concat_axis=0, tiled=True, axis...  10.1 us
    pallas_call x1, Pallas kernels, local(): pl.pallas_call(functools.partial(middle_kernel, tile_rows, tile0, origin,...  2.62 us
    all_to_all x1, waiting for transfers between devices, local(): lax.all_to_all(sent, 'blk', split_axis=0, concat_axis=0, tiled=True, axis...  2.28 us
  transfers between devices with their start and end apart: 1, of which 1 were waited for; matrix products, arithmetic and copies ran while one was open for 0% of the time, Pallas kernels for 3%

profile of v9, /device:TPU:1, one launch (start us, length us, event | category | flops | bytes accessed | tf_op | source)
XLA Modules:
  0.0 87.1 jit_solution(13841421221540567242)
XLA Ops:
  0.0 1.3 %stage.1 = (bf16[32,2,16,512]{3,2,1,0:T(8,128)(2,1)S(1)}, bf16[2,16,512]{2,1,0:T(8,128)(2,1)S(1)}) custom-call(bf16[2,32,16,512]{3,2,1,0:T(8,128)(2,1)} %bitcast.9, bf16[2,512,512]{2,1,0:T(8,128)(2,1)} %bitcast.7), custom_call_target="tpu_custom_call" | custom-call | tf_op jit(solution)/shard_map/stage/pallas_call | solution.py:300
  1.3 0.0 copy-start.2
  1.3 0.0 copy-start.3
  1.3 0.0 copy-start.4
  1.3 0.0 copy-start.5
  1.3 0.0 copy-start.6
  1.3 26.0 %all_to_all.20.planes = bf16[32,2,16,512]{3,2,1,0:T(8,128)(2,1)S(1)} all-to-all(bf16[32,2,16,512]{3,2,1,0:T(8,128)(2,1)S(1)} %get-tuple-element.14), channel_id=1, replica_groups={{21,22,23,24,25,26,27,28,29,30,31,0,1,2,3,4,5,6,7,8,9,10,11,12,13,14,15..., dimensions={0} | all-to-all | bytes 2097152 | tf_op jit(solution)/shard_map/all_to_all | solution.py:315
  27.3 0.0 copy-start
  27.3 0.0 copy-start.1
  27.3 0.4 layers.1
  27.7 17.6 %all_to_all.21.blocks = bf16[16,4,512]{2,1,0:T(4,128)(2,1)S(1)} all-to-all(bf16[16,4,512]{2,1,0:T(4,128)(2,1)S(1)} %get-tuple-element.16), channel_id=1, replica_groups={{320,352,384,416,448,480,0,32,64,96,128,160,192,224,256,288},{321,353,3..., dimensions={0} | all-to-all | bytes 131072 | tf_op jit(solution)/shard_map/all_to_all | solution.py:325
  45.3 0.0 copy-done.2
  45.3 0.0 copy-done.3
  45.3 0.0 copy-done.4
  45.3 0.0 copy-done.5
  45.3 0.0 copy-done.6
  45.3 0.0 copy-done
  45.3 1.4 %next_layers.1 = (bf16[16,4,512]{2,1,0:T(4,128)(2,1)}, bf16[2,16,512]{2,1,0:T(8,128)(2,1)S(1)}) custom-call(f32[1,3]{1,0:T(1,128)S(1)} %copy-done.2, s32[1,2]{1,0:T(1,128)S(1)} %copy-done.3, s32[1,2]{1,0:T(1,128)S(1)} %copy-done.4, s32[1,2]{1,0:T(1,128)S(1)} %copy-done.5, s32[1,2]{1,0:T(1,128)S(1)} %copy-done.6, bf16[16,4,512]{2,1,0:T(4,128)(2,1)S(1)} %all_to_all.21.blocks, ...), custom_call_target="tpu_custom_call" | custom-call | flops 33554432 | bytes 1048576 | tf_op jit(solution)/shard_map/next_layers/pallas_call | solution.py:326
  46.7 10.1 %all-to-all-start.2 = ((bf16[16,4,512]{2,1,0:T(4,128)(2,1)}), bf16[16,4,512]{2,1,0:T(4,128)(2,1)S(1)}, u32[]{:S(2)}, u32[]{:S(2)}) async-start(bf16[16,4,512]{2,1,0:T(4,128)(2,1)} %get-tuple-element.20), calls=%async_computation.2 | async-start | bytes 131072 | tf_op jit(solution)/shard_map/all_to_all | solution.py:335
  56.8 0.0 copy-done.1
  56.8 2.6 %middle.1 = (bf16[32,2,16,512]{3,2,1,0:T(8,128)(2,1)S(1)}, bf16[2,16,512]{2,1,0:T(8,128)(2,1)S(1)}, s32[8,8,128]{2,1,0:T(8,128)S(1)}) custom-call(f32[1,3]{1,0:T(1,128)S(1)} %copy-done.2, s32[1,2]{1,0:T(1,128)S(1)} %copy-done.3, s32[1,2]{1,0:T(1,128)S(1)} %copy-done.4, s32[1,2]{1,0:T(1,128)S(1)} %copy-done.5, ...), custom_call_target="tpu_custom_call", output_to_operand_aliasing={{0}: (5, {})} | custom-call | flops 1610612736 | bytes 4194304 | tf_op jit(solution)/shard_map/middle/pallas_call | solution.py:337
  59.4 2.3 %all-to-all-done.2.blocks = bf16[16,4,512]{2,1,0:T(4,128)(2,1)S(1)} async-done(((bf16[16,4,512]{2,1,0:T(4,128)(2,1)}), bf16[16,4,512]{2,1,0:T(4,128)(2,1)S(1)}, u32[]{:S(2)}, u32[]{:S(2)}) %all-to-all-start.2) | async-done | bytes 65568 | tf_op jit(solution)/shard_map/all_to_all | solution.py:335
  61.7 1.5 %last.1 = bf16[32,2,16,512]{3,2,1,0:T(8,128)(2,1)S(1)} custom-call(f32[1,3]{1,0:T(1,128)S(1)} %copy-done.2, s32[8,8,128]{2,1,0:T(8,128)S(1)} %get-tuple-element.19.marks, bf16[16,4,512]{2,1,0:T(4,128)(2,1)S(1)} %all-to-all-done.2.blocks, bf16[32,2,16,512]{3,2,1,0:T(8,128)(2,1)S(1)} %get-tuple-element.21.interior, ...), custom_call_target="tpu_custom_call" | custom-call | flops 536870912 | bytes 4194304 | tf_op jit(solution)/shard_map/last/pallas_call | solution.py:351
  63.2 22.9 %all_to_all.22.source = bf16[32,2,16,512]{3,2,1,0:T(8,128)(2,1)S(1)} all-to-all(bf16[32,2,16,512]{3,2,1,0:T(8,128)(2,1)S(1)} %last.1), channel_id=1, replica_groups={{21,22,23,24,25,26,27,28,29,30,31,0,1,2,3,4,5,6,7,8,9,10,11,12,13,14,15..., dimensions={0} | all-to-all | bytes 2097152 | tf_op jit(solution)/shard_map/all_to_all | solution.py:360
  86.1 1.0 %from_planes.1 = bf16[2,32,16,512]{3,2,1,0:T(8,128)(2,1)} custom-call(bf16[32,2,16,512]{3,2,1,0:T(8,128)(2,1)S(1)} %all_to_all.22.source), custom_call_target="tpu_custom_call" | custom-call | tf_op jit(solution)/shard_map/from_planes/pallas_call | solution.py:59
Async XLA Ops:
  1.3 44.0 %copy-start.2 = (f32[1,3]{1,0:T(1,128)S(1)}, f32[1,3]{1,0:T(1,128)}, u32[]{:S(2)}) copy-start(f32[1,3]{1,0:T(1,128)} %rates.5) | copy-start | bytes 40
  1.3 44.0 %copy-start.3 = (s32[1,2]{1,0:T(1,128)S(1)}, s32[1,2]{1,0:T(1,128)}, u32[]{:S(2)}) copy-start(s32[1,2]{1,0:T(1,128)} %partner.3) | copy-start | bytes 28
  1.3 44.0 %copy-start.4 = (s32[1,2]{1,0:T(1,128)S(1)}, s32[1,2]{1,0:T(1,128)}, u32[]{:S(2)}) copy-start(s32[1,2]{1,0:T(1,128)} %face_side.3) | copy-start | bytes 28
  1.3 44.0 %copy-start.5 = (s32[1,2]{1,0:T(1,128)S(1)}, s32[1,2]{1,0:T(1,128)}, u32[]{:S(2)}) copy-start(s32[1,2]{1,0:T(1,128)} %orient.3) | copy-start | bytes 28
  1.3 44.0 %copy-start.6 = (s32[1,2]{1,0:T(1,128)S(1)}, s32[1,2]{1,0:T(1,128)}, u32[]{:S(2)}) copy-start(s32[1,2]{1,0:T(1,128)} %offset.3) | copy-start | bytes 28
  27.3 18.0 %copy-start = (bf16[1,2,512,512]{3,2,1,0:T(8,128)(2,1)S(1)}, bf16[1,2,512,512]{3,2,1,0:T(8,128)(2,1)}, u32[]{:S(2)}) copy-start(bf16[1,2,512,512]{3,2,1,0:T(8,128)(2,1)} %param.10) | copy-start | bytes 3145732
  27.3 29.5 %copy-start.1 = (bf16[1,2,512,512]{3,2,1,0:T(8,128)(2,1)S(1)}, bf16[1,2,512,512]{3,2,1,0:T(8,128)(2,1)}, u32[]{:S(2)}) copy-start(bf16[1,2,512,512]{3,2,1,0:T(8,128)(2,1)} %param.9) | copy-start | bytes 3145732
  46.7 15.0 %all-to-all-start.2 = ((bf16[16,4,512]{2,1,0:T(4,128)(2,1)}), bf16[16,4,512]{2,1,0:T(4,128)(2,1)S(1)}, u32[]{:S(2)}, u32[]{:S(2)}) async-start(bf16[16,4,512]{2,1,0:T(4,128)(2,1)} %get-tuple-element.20), calls=%async_computation.2 | async-start | bytes 131072 | tf_op jit(solution)/shard_map/all_to_all | solution.py:335

commit v10 on v9

--- a/solution.py
+++ b/solution.py
@@ -288,7 +288,7 @@
     count = lax.axis_size("blk")
     width = lax.axis_size("pen")
     tile0 = (width * 21) // 32
-    origin = (count * 5) // 8
+    origin = (count * 9) // 16
     across = turned_group(count, origin)
     within = turned_group(width, tile0)
     numbers = (rates, partner, face_side, orient, offset)

time: 87.4 us -> 87.3 us (level)
  no operation moved by 1% of the time
where the time goes in v10:
time: 87.3 us; the launch traced here: 86.9 us
  blocking collectives  66.6 us (76%)
  starting transfers between devices  10.7 us (12%)
  Pallas kernels  8.11 us (9%)
  waiting for transfers between devices  1.41 us (2%)
    all_to_all x1, blocking collectives, local(): lax.all_to_all(staged, 'pen', split_axis=0, concat_axis=0, tiled=True, ax...  26 us
    all_to_all x1, blocking collectives, local(): lax.all_to_all(planes, 'pen', split_axis=0, concat_axis=0, tiled=True, ax...  23 us
    all_to_all x1, blocking collectives, local(): lax.all_to_all(sent, 'blk', split_axis=0, concat_axis=0, tiled=True, axis...  17.6 us
    all_to_all x1, starting transfers between devices, local(): lax.all_to_all(sent, 'blk', split_axis=0, concat_axis=0, tiled=True, axis...  10.7 us
    pallas_call x1, Pallas kernels, local(): pl.pallas_call(functools.partial(middle_kernel, tile_rows, tile0, origin,...  2.61 us
  transfers between devices with their start and end apart: 1, of which 1 were waited for; matrix products, arithmetic and copies ran while one was open for 0% of the time, Pallas kernels for 3%

profile of v10, /device:TPU:1, one launch (start us, length us, event | category | flops | bytes accessed | tf_op | source)
XLA Modules:
  0.0 86.9 jit_solution(9678668822652882613)
XLA Ops:
  0.0 1.3 %stage.1 = (bf16[32,2,16,512]{3,2,1,0:T(8,128)(2,1)S(1)}, bf16[2,16,512]{2,1,0:T(8,128)(2,1)S(1)}) custom-call(bf16[2,32,16,512]{3,2,1,0:T(8,128)(2,1)} %bitcast.9, bf16[2,512,512]{2,1,0:T(8,128)(2,1)} %bitcast.7), custom_call_target="tpu_custom_call" | custom-call | tf_op jit(solution)/shard_map/stage/pallas_call | solution.py:300
  1.3 0.0 copy-start.2
  1.3 0.0 copy-start.3
  1.3 0.0 copy-start.4
  1.3 0.0 copy-start.5
  1.3 0.0 copy-start.6
  1.3 26.0 %all_to_all.20.planes = bf16[32,2,16,512]{3,2,1,0:T(8,128)(2,1)S(1)} all-to-all(bf16[32,2,16,512]{3,2,1,0:T(8,128)(2,1)S(1)} %get-tuple-element.14), channel_id=1, replica_groups={{21,22,23,24,25,26,27,28,29,30,31,0,1,2,3,4,5,6,7,8,9,10,11,12,13,14,15..., dimensions={0} | all-to-all | bytes 2097152 | tf_op jit(solution)/shard_map/all_to_all | solution.py:315
  27.3 0.0 copy-start
  27.3 0.0 copy-start.1
  27.3 0.4 layers.1
  27.7 17.6 %all_to_all.21.blocks = bf16[16,4,512]{2,1,0:T(4,128)(2,1)S(1)} all-to-all(bf16[16,4,512]{2,1,0:T(4,128)(2,1)S(1)} %get-tuple-element.16), channel_id=1, replica_groups={{288,320,352,384,416,448,480,0,32,64,96,128,160,192,224,256},{289,321,3..., dimensions={0} | all-to-all | bytes 131072 | tf_op jit(solution)/shard_map/all_to_all | solution.py:325
  45.3 0.0 copy-done.2
  45.3 0.0 copy-done.3
  45.3 0.0 copy-done.4
  45.3 0.0 copy-done.5
  45.3 0.0 copy-done.6
  45.3 0.0 copy-done
  45.4 1.4 %next_layers.1 = (bf16[16,4,512]{2,1,0:T(4,128)(2,1)}, bf16[2,16,512]{2,1,0:T(8,128)(2,1)S(1)}) custom-call(f32[1,3]{1,0:T(1,128)S(1)} %copy-done.2, s32[1,2]{1,0:T(1,128)S(1)} %copy-done.3, s32[1,2]{1,0:T(1,128)S(1)} %copy-done.4, s32[1,2]{1,0:T(1,128)S(1)} %copy-done.5, s32[1,2]{1,0:T(1,128)S(1)} %copy-done.6, bf16[16,4,512]{2,1,0:T(4,128)(2,1)S(1)} %all_to_all.21.blocks, ...), custom_call_target="tpu_custom_call" | custom-call | flops 33554432 | bytes 1048576 | tf_op jit(solution)/shard_map/next_layers/pallas_call | solution.py:326
  46.7 10.7 %all-to-all-start.2 = ((bf16[16,4,512]{2,1,0:T(4,128)(2,1)}), bf16[16,4,512]{2,1,0:T(4,128)(2,1)S(1)}, u32[]{:S(2)}, u32[]{:S(2)}) async-start(bf16[16,4,512]{2,1,0:T(4,128)(2,1)} %get-tuple-element.20), calls=%async_computation.2 | async-start | bytes 131072 | tf_op jit(solution)/shard_map/all_to_all | solution.py:335
  57.4 0.0 copy-done.1
  57.4 2.6 %middle.1 = (bf16[32,2,16,512]{3,2,1,0:T(8,128)(2,1)S(1)}, bf16[2,16,512]{2,1,0:T(8,128)(2,1)S(1)}, s32[8,8,128]{2,1,0:T(8,128)S(1)}) custom-call(f32[1,3]{1,0:T(1,128)S(1)} %copy-done.2, s32[1,2]{1,0:T(1,128)S(1)} %copy-done.3, s32[1,2]{1,0:T(1,128)S(1)} %copy-done.4, s32[1,2]{1,0:T(1,128)S(1)} %copy-done.5, ...), custom_call_target="tpu_custom_call", output_to_operand_aliasing={{0}: (5, {})} | custom-call | flops 1610612736 | bytes 4194304 | tf_op jit(solution)/shard_map/middle/pallas_call | solution.py:337
  60.0 1.4 %all-to-all-done.2.blocks = bf16[16,4,512]{2,1,0:T(4,128)(2,1)S(1)} async-done(((bf16[16,4,512]{2,1,0:T(4,128)(2,1)}), bf16[16,4,512]{2,1,0:T(4,128)(2,1)S(1)}, u32[]{:S(2)}, u32[]{:S(2)}) %all-to-all-start.2) | async-done | bytes 65568 | tf_op jit(solution)/shard_map/all_to_all | solution.py:335
  61.5 1.5 %last.1 = bf16[32,2,16,512]{3,2,1,0:T(8,128)(2,1)S(1)} custom-call(f32[1,3]{1,0:T(1,128)S(1)} %copy-done.2, s32[8,8,128]{2,1,0:T(8,128)S(1)} %get-tuple-element.19.marks, bf16[16,4,512]{2,1,0:T(4,128)(2,1)S(1)} %all-to-all-done.2.blocks, bf16[32,2,16,512]{3,2,1,0:T(8,128)(2,1)S(1)} %get-tuple-element.21.interior, ...), custom_call_target="tpu_custom_call" | custom-call | flops 536870912 | bytes 4194304 | tf_op jit(solution)/shard_map/last/pallas_call | solution.py:351
  63.0 23.0 %all_to_all.22.source = bf16[32,2,16,512]{3,2,1,0:T(8,128)(2,1)S(1)} all-to-all(bf16[32,2,16,512]{3,2,1,0:T(8,128)(2,1)S(1)} %last.1), channel_id=1, replica_groups={{21,22,23,24,25,26,27,28,29,30,31,0,1,2,3,4,5,6,7,8,9,10,11,12,13,14,15..., dimensions={0} | all-to-all | bytes 2097152 | tf_op jit(solution)/shard_map/all_to_all | solution.py:360
  86.0 1.0 %from_planes.1 = bf16[2,32,16,512]{3,2,1,0:T(8,128)(2,1)} custom-call(bf16[32,2,16,512]{3,2,1,0:T(8,128)(2,1)S(1)} %all_to_all.22.source), custom_call_target="tpu_custom_call" | custom-call | tf_op jit(solution)/shard_map/from_planes/pallas_call | solution.py:59
Async XLA Ops:
  1.3 44.1 %copy-start.2 = (f32[1,3]{1,0:T(1,128)S(1)}, f32[1,3]{1,0:T(1,128)}, u32[]{:S(2)}) copy-start(f32[1,3]{1,0:T(1,128)} %rates.5) | copy-start | bytes 40
  1.3 44.0 %copy-start.3 = (s32[1,2]{1,0:T(1,128)S(1)}, s32[1,2]{1,0:T(1,128)}, u32[]{:S(2)}) copy-start(s32[1,2]{1,0:T(1,128)} %partner.3) | copy-start | bytes 28
  1.3 44.0 %copy-start.4 = (s32[1,2]{1,0:T(1,128)S(1)}, s32[1,2]{1,0:T(1,128)}, u32[]{:S(2)}) copy-start(s32[1,2]{1,0:T(1,128)} %face_side.3) | copy-start | bytes 28
  1.3 44.0 %copy-start.5 = (s32[1,2]{1,0:T(1,128)S(1)}, s32[1,2]{1,0:T(1,128)}, u32[]{:S(2)}) copy-start(s32[1,2]{1,0:T(1,128)} %orient.3) | copy-start | bytes 28
  1.3 44.0 %copy-start.6 = (s32[1,2]{1,0:T(1,128)S(1)}, s32[1,2]{1,0:T(1,128)}, u32[]{:S(2)}) copy-start(s32[1,2]{1,0:T(1,128)} %offset.3) | copy-start | bytes 28
  27.3 18.1 %copy-start = (bf16[1,2,512,512]{3,2,1,0:T(8,128)(2,1)S(1)}, bf16[1,2,512,512]{3,2,1,0:T(8,128)(2,1)}, u32[]{:S(2)}) copy-start(bf16[1,2,512,512]{3,2,1,0:T(8,128)(2,1)} %param.10) | copy-start | bytes 3145732
  27.3 30.1 %copy-start.1 = (bf16[1,2,512,512]{3,2,1,0:T(8,128)(2,1)S(1)}, bf16[1,2,512,512]{3,2,1,0:T(8,128)(2,1)}, u32[]{:S(2)}) copy-start(bf16[1,2,512,512]{3,2,1,0:T(8,128)(2,1)} %param.9) | copy-start | bytes 3145732
  46.7 14.7 %all-to-all-start.2 = ((bf16[16,4,512]{2,1,0:T(4,128)(2,1)}), bf16[16,4,512]{2,1,0:T(4,128)(2,1)S(1)}, u32[]{:S(2)}, u32[]{:S(2)}) async-start(bf16[16,4,512]{2,1,0:T(4,128)(2,1)} %get-tuple-element.20), calls=%async_computation.2 | async-start | bytes 131072 | tf_op jit(solution)/shard_map/all_to_all | solution.py:335
